TPU v7x, 256 devices: a whole 4x4x8 slice. The times are simulated.
256 devices in a mesh: pts: 32 (over x_hi, z, core), dir: 8 (over x_lo, y).
Axes of the slice: x: 4 (x_hi: 2, x_lo: 2; x = x_hi * 2 + x_lo), y: 4, z: 8, core: 2. Of those that a mesh axis runs over, the one named last changes fastest.
Arguments:
- action: float32 [50, 32, 512, 256], P(None, 'dir', 'pts'), may hold values from 0 to 60, as said below
- currents: float32 [2, 512, 256], P(None, 'pts'), may hold values from -0.1 to 0.1, as said below
- land_mask: int32 [512, 256], P('pts'), may hold values 0 or 1
- group_speed: float32 [50], replicated, may hold values from 0.02 to 0.55
- group_ratio: float32 [50], replicated, may hold values from 0.5 to 1
- bin_weight: float32 [50], replicated, may hold values from 0.002 to 0.02
Outputs:
- new_action: float32 [50, 32, 512, 256], P(None, 'dir', 'pts')
- wave_force: float32 [2, 512, 256], P(None, 'pts')
Inputs may be any that keep to these rules, and one draw needn't show every extreme that they name: Positive action densities. currents vary slowly from point to point.
All inputs are finite; a program needn't handle non-finite values. No bound on the sum of `land_mask` on one device may be relied on, other than what follows from the above.
Results may differ from a plain program's by a relative error of at most 0.00022.
Values sent between devices are 32-bit elements; how exact they have to be, the bound alone decides.
No kernel may reach another device: no remote copies, remote signals or barrier semaphores. Data moves between devices by JAX's collectives and lax.ppermute only.
A program may use at most 64 MiB of HBM per device.

v0:
```python
import math

import jax
import jax.numpy as jnp
from jax import lax
from jax.sharding import PartitionSpec as P


def with_halo(value, sides, width, wrap):
    for axis, dim in sides:
        count, length = (lax.axis_size(axis), value.shape[dim])
        up = [(i, (i + 1) % count) for i in range(count if wrap else count - 1)]
        down = [(j, i) for i, j in up]
        last = lax.slice_in_dim(value, length - width, length, axis=dim)
        first = lax.slice_in_dim(value, 0, width, axis=dim)
        before = lax.ppermute(last, axis, up)
        after = lax.ppermute(first, axis, down)
        value = jnp.concatenate([before, value, after], axis=dim)
    return value


def upwind(velocity, behind, in_front):
    return jnp.maximum(velocity, 0.0) * behind + jnp.minimum(velocity, 0.0) * in_front


def advance(extended, cur_u, cur_v, land_cells, cosine_terms, sine_terms, group_speed):
    speed_x = group_speed[:, None, None, None] * cosine_terms[None, :, None, None]
    speed_y = group_speed[:, None, None, None] * sine_terms[None, :, None, None]
    drift_x = speed_x + (0.5 * (cur_u[:-1] + cur_u[1:]))[None, None]
    flux_x = upwind(drift_x, extended[:, :, :-1], extended[:, :, 1:])
    middle = extended[:, :, 1:-1]
    side_v = jnp.pad(cur_v[1:-1], ((0, 0), (1, 1)))
    drift_y = speed_y + (0.5 * (side_v[:, :-1] + side_v[:, 1:]))[None, None]
    padded = jnp.pad(middle, ((0, 0), (0, 0), (0, 0), (1, 1)))
    flux_y = upwind(drift_y, padded[..., :-1], padded[..., 1:])
    change = flux_x[:, :, 1:] - flux_x[:, :, :-1] + (flux_y[..., 1:] - flux_y[..., :-1])
    return land_cells * (middle - change)


def row_slope(values):
    return 0.5 * (values[2:] - values[:-2])


def col_slope(values):
    padded = jnp.pad(values[1:-1], ((0, 0), (1, 1)))
    return 0.5 * (padded[:, 2:] - padded[:, :-2])


def shear_terms(ext_u, ext_v):
    return (row_slope(ext_u), col_slope(ext_u), row_slope(ext_v), col_slope(ext_v))


def turn_rate(face_angles, shears, total_dirs):
    u_dx, u_dy, v_dx, v_dy = shears
    sines = jnp.sin(face_angles)[:, None, None]
    cosines = jnp.cos(face_angles)[:, None, None]
    scale = total_dirs / (2.0 * math.pi)
    return scale * (
        sines * cosines * (u_dx - v_dy) + sines * sines * u_dy - cosines * cosines * v_dx
    )


def refract(cycle_ext, turning):
    flux = upwind(turning[None], cycle_ext[:, :-1], cycle_ext[:, 1:])
    return cycle_ext[:, 1:-1] - (flux[:, 1:] - flux[:, :-1])


def stress_table(angles, bin_weight, group_ratio):
    cos_sq = (jnp.cos(angles) * jnp.cos(angles))[None]
    sin_sq = (jnp.sin(angles) * jnp.sin(angles))[None]
    cross = (jnp.sin(angles) * jnp.cos(angles))[None]
    ratio = group_ratio[:, None]
    weight = bin_weight[:, None]
    return jnp.stack(
        [
            weight * (ratio * (1.0 + cos_sq) - 0.5),
            weight * ratio * cross,
            weight * (ratio * (1.0 + sin_sq) - 0.5),
        ]
    )


def wave_force_of(extended):
    first = -(row_slope(extended[0]) + col_slope(extended[1]))
    second = -(row_slope(extended[1]) + col_slope(extended[2]))
    return jnp.stack([first, second])


def per_device(action, currents, land_mask, group_speed, group_ratio, bin_weight):
    sector_count = action.shape[1]
    total_dirs = sector_count * lax.axis_size("dir")
    step_angle = 2.0 * math.pi / total_dirs
    offset = lax.axis_index("dir") * sector_count
    angles = (offset + jnp.arange(sector_count)).astype(jnp.float32) * step_angle
    cosine_terms = jnp.cos(angles)
    sine_terms = jnp.sin(angles)
    land_cells = land_mask.astype(jnp.float32)
    fields = jnp.stack([currents[0], currents[1], land_cells])
    beside_all = with_halo(fields, (("pts", 1),), 2, False)
    ext_u = beside_all[0, 1:-1]
    ext_v = beside_all[1, 1:-1]
    spectra = land_cells * action
    for substep in range(2):
        extended = with_halo(spectra, (("pts", 2),), 1, False)
        spectra = advance(extended, ext_u, ext_v, land_cells, cosine_terms, sine_terms, group_speed)
    shears = shear_terms(ext_u, ext_v)
    face_angles = ((offset + jnp.arange(sector_count + 1)).astype(jnp.float32) - 0.5) * step_angle
    turning = turn_rate(face_angles, shears, total_dirs)
    cycle_ext = with_halo(spectra, (("dir", 1),), 1, True)
    new_action = refract(cycle_ext, turning)
    partial_value = jnp.einsum(
        "kfd,fdry->kry",
        stress_table(angles, bin_weight, group_ratio),
        new_action,
        precision=lax.Precision.HIGHEST,
    )
    summed = lax.psum(partial_value, "dir")
    extended = with_halo(summed, (("pts", 1),), 1, False)
    return (new_action, wave_force_of(extended))


def solution(mesh):
    in_specs = (P(None, "dir", "pts", None), P(None, "pts", None), P("pts", None), P(), P(), P())
    out_specs = (P(None, "dir", "pts", None), P(None, "pts", None))
    return jax.shard_map(
        per_device, mesh=mesh, in_specs=in_specs, out_specs=out_specs, check_vma=False
    )
```

profile of v0, /device:TPU:6, one launch (start us, length us, event | category | flops | bytes accessed | tf_op | source)
XLA Modules:
  0.0 132.3 jit_solution(10773098734468614222)
XLA Ops:
  2.1 1.9 %collective-permute-start = (f32[3,2,256]{2,1,0:T(2,128)S(1)}, f32[3,2,256]{2,1,0:T(2,128)S(1)}, u32[]{:S(2)}, u32[]{:S(2)}) collective-permute-start(f32[3,2,256]{2,1,0:T(2,128)S(1)} %get-tuple-element.24), channel_id=1, source_target_pairs={{0,8},{8,16},{16,24},{24,32},{32,40},{40,48},{48,56},{56,64},{64,7... | collective-permute-start | bytes 18440 | tf_op jit(solution)/shard_map/ppermute | solution.py:16
  4.0 8.0 %collective-permute-start.1 = (f32[3,2,256]{2,1,0:T(2,128)S(1)}, f32[3,2,256]{2,1,0:T(2,128)S(1)}, u32[]{:S(2)}, u32[]{:S(2)}) collective-permute-start(f32[3,2,256]{2,1,0:T(2,128)S(1)} %get-tuple-element.25), channel_id=1, source_target_pairs={{8,0},{16,8},{24,16},{32,24},{40,32},{48,40},{56,48},{64,56},{72,6... | collective-permute-start | bytes 18440 | tf_op jit(solution)/shard_map/ppermute | solution.py:17
  12.1 3.9 %copy_multiply_fusion = f32[50,4,16,256]{3,0,2,1:T(8,128)S(1)} fusion(f32[50,4,16,256]{3,2,1,0:T(8,128)} %param.6, f32[16,256]{1,0:T(8,128)S(1)} %get-tuple-element.30), kind=kLoop, calls=%fused_computation.35 | loop fusion | flops 819200 | bytes 6569984 | tf_op jit(solution)/shard_map/mul | solution.py:102
  16.0 1.8 %copy-done = f32[50,4,16,256]{3,0,2,1:T(8,128)} copy-done((f32[50,4,16,256]{3,0,2,1:T(8,128)}, f32[50,4,16,256]{3,0,2,1:T(8,128)S(1)}, u32[]{:S(2)}) %copy-start) | copy-done | bytes 3276824
  17.8 1.9 %collective-permute-start.2 = (f32[50,4,1,256]{3,0,2,1:T(8,128)S(1)}, f32[50,4,1,256]{3,0,2,1:T(8,128)S(1)}, u32[]{:S(2)}, u32[]{:S(2)}) collective-permute-start(f32[50,4,1,256]{3,0,2,1:T(8,128)S(1)} %get-tuple-element.15), channel_id=1, source_target_pairs={{0,8},{8,16},{16,24},{24,32},{32,40},{40,48},{48,56},{56,64},{64,7... | collective-permute-start | bytes 614408 | tf_op jit(solution)/shard_map/ppermute | solution.py:16
  19.7 7.3 %collective-permute-start.3 = (f32[50,4,1,256]{3,0,2,1:T(8,128)S(1)}, f32[50,4,1,256]{3,0,2,1:T(8,128)S(1)}, u32[]{:S(2)}, u32[]{:S(2)}) collective-permute-start(f32[50,4,1,256]{3,0,2,1:T(8,128)S(1)} %get-tuple-element.14), channel_id=1, source_target_pairs={{8,0},{16,8},{24,16},{32,24},{40,32},{48,40},{56,48},{64,56},{72,6... | collective-permute-start | bytes 614408 | tf_op jit(solution)/shard_map/ppermute | solution.py:17
  27.4 4.8 %fusion.4 = f32[50,4,16,257]{3,0,2,1:T(8,128)S(1)} fusion(f32[50,4,16,256]{3,0,2,1:T(8,128)} %copy-done, f32[16,257]{1,0:T(8,128)S(1)} %fusion.23, f32[50,4]{0,1:T(4,128)S(1)} %get-tuple-element.34), kind=kLoop, calls=%fused_computation.12 | loop fusion | flops 4934400 | bytes 6583648 | tf_op jit(solution)/shard_map/add | solution.py:23
  32.3 1.2 fusion.11
  34.2 5.1 %fusion.19 = f32[50,4,16,256]{3,0,2,1:T(8,128)S(1)} fusion(f32[50,4,16,257]{3,0,2,1:T(8,128)S(1)} %fusion.4, f32[50,4,17,256]{3,0,2,1:T(8,128)S(1)} %fusion.11, f32[16,256]{1,0:T(8,128)S(1)} %get-tuple-element.30, f32[50,4,16,256]{3,2,1,0:T(8,128)S(1)} %copy-done.3), kind=kLoop, calls=%fused_computation.33 | loop fusion | flops 4915200 | bytes 19677184 | tf_op jit(solution)/shard_map/mul | solution.py:37
  39.4 1.9 %collective-permute-start.4 = (f32[50,4,1,256]{3,0,2,1:T(8,128)S(1)}, f32[50,4,1,256]{3,0,2,1:T(8,128)S(1)}, u32[]{:S(2)}, u32[]{:S(2)}) collective-permute-start(f32[50,4,1,256]{3,0,2,1:T(8,128)S(1)} %get-tuple-element.13), channel_id=1, source_target_pairs={{0,8},{8,16},{16,24},{24,32},{32,40},{40,48},{48,56},{56,64},{64,7... | collective-permute-start | bytes 614408 | tf_op jit(solution)/shard_map/ppermute | solution.py:16
  41.3 7.3 %collective-permute-start.5 = (f32[50,4,1,256]{3,0,2,1:T(8,128)S(1)}, f32[50,4,1,256]{3,0,2,1:T(8,128)S(1)}, u32[]{:S(2)}, u32[]{:S(2)}) collective-permute-start(f32[50,4,1,256]{3,0,2,1:T(8,128)S(1)} %get-tuple-element.12), channel_id=1, source_target_pairs={{8,0},{16,8},{24,16},{32,24},{40,32},{48,40},{56,48},{64,56},{72,6... | collective-permute-start | bytes 614408 | tf_op jit(solution)/shard_map/ppermute | solution.py:17
  48.6 3.3 %fusion.5 = f32[50,4,16,257]{3,0,2,1:T(8,128)} fusion(f32[50,4,16,256]{3,0,2,1:T(8,128)S(1)} %fusion.19, f32[16,257]{1,0:T(8,128)S(1)} %fusion.23, f32[50,4]{0,1:T(4,128)S(1)} %get-tuple-element.34), kind=kLoop, calls=%fused_computation.13 | loop fusion | flops 4934400 | bytes 6583648 | tf_op jit(solution)/shard_map/add | solution.py:23
  52.1 2.5 %fusion.12 = f32[50,4,17,256]{3,0,2,1:T(8,128)} fusion(f32[50,4,16,256]{3,0,2,1:T(8,128)S(1)} %fusion.19, f32[50,4,1,256]{3,0,2,1:T(8,128)S(1)} %collective-permute-done.4, f32[50,4,1,256]{3,0,2,1:T(8,128)S(1)} %collective-permute-done.5, f32[17,256]{1,0:T(8,128)S(1)} %fusion.25, f32[50,4]{0,1:T(4,128)S(1)} %get-tuple-element.33), kind=kLoop, calls=%fused_computation.22 | loop fusion | flops 6963200 | bytes 7186208 | tf_op jit(solution)/shard_map/add | solution.py:23
  54.6 7.5 %fusion.16 = f32[50,4,16,256]{3,0,2,1:T(8,128)S(1)} fusion(f32[50,4,16,256]{3,0,2,1:T(8,128)S(1)} %fusion.19, f32[50,4,16,257]{3,0,2,1:T(8,128)} %fusion.5, f32[50,4,17,256]{3,0,2,1:T(8,128)} %fusion.12, f32[16,256]{1,0:T(8,128)S(1)} %get-tuple-element.30), kind=kLoop, calls=%fused_computation.28 | loop fusion | flops 4096000 | bytes 19677184 | tf_op jit(solution)/shard_map/mul | solution.py:37
  62.5 1.7 %collective-permute-start.6 = (f32[50,1,16,256]{3,2,1,0:T(8,128)S(1)}, f32[50,1,16,256]{3,2,1,0:T(8,128)S(1)}, u32[]{:S(2)}, u32[]{:S(2)}) collective-permute-start(f32[50,1,16,256]{3,2,1,0:T(8,128)S(1)} %copy.35), channel_id=1, source_target_pairs={{0,1},{1,2},{2,3},{3,4},{4,5},{5,6},{6,7},{7,0},{8,9},{9,10},{10,1... | collective-permute-start | bytes 2457608 | tf_op jit(solution)/shard_map/ppermute | solution.py:16
  64.4 2.8 %collective-permute-start.7 = (f32[50,1,16,256]{3,2,1,0:T(8,128)S(1)}, f32[50,1,16,256]{3,2,1,0:T(8,128)S(1)}, u32[]{:S(2)}, u32[]{:S(2)}) collective-permute-start(f32[50,1,16,256]{3,2,1,0:T(8,128)S(1)} %copy.37), channel_id=1, source_target_pairs={{1,0},{2,1},{3,2},{4,3},{5,4},{6,5},{7,6},{0,7},{9,8},{10,9},{11,1... | collective-permute-start | bytes 2457608 | tf_op jit(solution)/shard_map/ppermute | solution.py:17
  67.6 12.2 %collective-permute-done.6 = f32[50,1,16,256]{3,2,1,0:T(8,128)S(1)} collective-permute-done((f32[50,1,16,256]{3,2,1,0:T(8,128)S(1)}, f32[50,1,16,256]{3,2,1,0:T(8,128)S(1)}, u32[]{:S(2)}, u32[]{:S(2)}) %collective-permute-start.6) | collective-permute-done | bytes 819232 | tf_op jit(solution)/shard_map/ppermute | solution.py:16
  82.6 1.8 %copy-done.2 = f32[50,4,16,256]{3,0,2,1:T(8,128)} copy-done((f32[50,4,16,256]{3,0,2,1:T(8,128)}, f32[50,4,16,256]{3,0,2,1:T(8,128)S(1)}, u32[]{:S(2)}) %copy-start.2) | copy-done | bytes 3276824
  84.4 1.9 %convolution_bitcast_fusion = f32[3,16,256]{2,0,1:T(4,128)S(1)} fusion(f32[50,4,16,256]{3,0,2,1:T(8,128)S(1)} %fusion.13, f32[3,50,4]{1,2,0:T(4,128)S(1)} %pad_maximum_fusion.5), kind=kOutput, calls=%fused_computation.36 | convolution fusion | flops 29491200 | bytes 3328352 | tf_op jit(solution)/shard_map/kfd,fdry->kry/dot_general | solution.py:111
  86.3 34.8 %psum.7 = f32[3,16,256]{2,0,1:T(4,128)S(1)} all-reduce(f32[3,16,256]{2,0,1:T(4,128)S(1)} %convolution_bitcast_fusion), channel_id=1, replica_groups=mesh['pts'=32,'dir'=8] {'dir'}, use_global_device_ids=true, to_apply=%region_0.1 | all-reduce | flops 12288 | bytes 98304 | tf_op jit(solution)/shard_map/psum | solution.py:117
  121.1 1.9 %collective-permute-start.8 = (f32[3,1,256]{2,1,0:T(1,128)S(1)}, f32[3,1,256]{2,1,0:T(1,128)S(1)}, u32[]{:S(2)}, u32[]{:S(2)}) collective-permute-start(f32[3,1,256]{2,1,0:T(1,128)S(1)} %get-tuple-element.20), channel_id=1, source_target_pairs={{8,0},{16,8},{24,16},{32,24},{40,32},{48,40},{56,48},{64,56},{72,6... | collective-permute-start | bytes 9224 | tf_op jit(solution)/shard_map/ppermute | solution.py:17
  123.1 2.4 %collective-permute-start.9 = (f32[3,1,256]{2,1,0:T(1,128)S(1)}, f32[3,1,256]{2,1,0:T(1,128)S(1)}, u32[]{:S(2)}, u32[]{:S(2)}) collective-permute-start(f32[3,1,256]{2,1,0:T(1,128)S(1)} %get-tuple-element.21), channel_id=1, source_target_pairs={{0,8},{8,16},{16,24},{24,32},{32,40},{40,48},{48,56},{56,64},{64,7... | collective-permute-start | bytes 9224 | tf_op jit(solution)/shard_map/ppermute | solution.py:16
  125.5 4.8 %copy.46 = f32[50,4,16,256]{3,2,1,0:T(8,128)} copy(f32[50,4,16,256]{3,0,2,1:T(8,128)} %copy-done.2) | data formatting | bytes 6553600
  130.4 1.2 collective-permute-done.9
  (57 shorter events, 7.4 us)
Async XLA Ops:
  2.1 25.2 %collective-permute-start = (f32[3,2,256]{2,1,0:T(2,128)S(1)}, f32[3,2,256]{2,1,0:T(2,128)S(1)}, u32[]{:S(2)}, u32[]{:S(2)}) collective-permute-start(f32[3,2,256]{2,1,0:T(2,128)S(1)} %get-tuple-element.24), channel_id=1, source_target_pairs={{0,8},{8,16},{16,24},{24,32},{32,40},{40,48},{48,56},{56,64},{64,7... | collective-permute-start | bytes 18440 | tf_op jit(solution)/shard_map/ppermute | solution.py:16
  4.0 23.3 %collective-permute-start.1 = (f32[3,2,256]{2,1,0:T(2,128)S(1)}, f32[3,2,256]{2,1,0:T(2,128)S(1)}, u32[]{:S(2)}, u32[]{:S(2)}) collective-permute-start(f32[3,2,256]{2,1,0:T(2,128)S(1)} %get-tuple-element.25), channel_id=1, source_target_pairs={{8,0},{16,8},{24,16},{32,24},{40,32},{48,40},{56,48},{64,56},{72,6... | collective-permute-start | bytes 18440 | tf_op jit(solution)/shard_map/ppermute | solution.py:17
  12.1 15.0 %copy-start.5 = (f32[50]{0:T(128)S(1)}, f32[50]{0:T(128)}, u32[]{:S(2)}) copy-start(f32[50]{0:T(128)} %param.10) | copy-start | bytes 604
  12.1 15.0 %copy-start.6 = (f32[50]{0:T(128)S(1)}, f32[50]{0:T(128)}, u32[]{:S(2)}) copy-start(f32[50]{0:T(128)} %param.11) | copy-start | bytes 604
  12.1 15.1 %copy-start.7 = (f32[50]{0:T(128)S(1)}, f32[50]{0:T(128)}, u32[]{:S(2)}) copy-start(f32[50]{0:T(128)} %param.9) | copy-start | bytes 604
  12.1 15.2 %copy-start.4 = (f32[2,16,256]{2,1,0:T(8,128)S(1)}, f32[2,16,256]{2,1,0:T(8,128)}, u32[]{:S(2)}) copy-start(f32[2,16,256]{2,1,0:T(8,128)} %param.7) | copy-start | bytes 98308
  16.0 1.8 %copy-start = (f32[50,4,16,256]{3,0,2,1:T(8,128)}, f32[50,4,16,256]{3,0,2,1:T(8,128)S(1)}, u32[]{:S(2)}) copy-start(f32[50,4,16,256]{3,0,2,1:T(8,128)S(1)} %copy_multiply_fusion) | copy-start | bytes 9830404
  17.8 14.5 %collective-permute-start.2 = (f32[50,4,1,256]{3,0,2,1:T(8,128)S(1)}, f32[50,4,1,256]{3,0,2,1:T(8,128)S(1)}, u32[]{:S(2)}, u32[]{:S(2)}) collective-permute-start(f32[50,4,1,256]{3,0,2,1:T(8,128)S(1)} %get-tuple-element.15), channel_id=1, source_target_pairs={{0,8},{8,16},{16,24},{24,32},{32,40},{40,48},{48,56},{56,64},{64,7... | collective-permute-start | bytes 614408 | tf_op jit(solution)/shard_map/ppermute | solution.py:16
  19.7 12.6 %collective-permute-start.3 = (f32[50,4,1,256]{3,0,2,1:T(8,128)S(1)}, f32[50,4,1,256]{3,0,2,1:T(8,128)S(1)}, u32[]{:S(2)}, u32[]{:S(2)}) collective-permute-start(f32[50,4,1,256]{3,0,2,1:T(8,128)S(1)} %get-tuple-element.14), channel_id=1, source_target_pairs={{8,0},{16,8},{24,16},{32,24},{40,32},{48,40},{56,48},{64,56},{72,6... | collective-permute-start | bytes 614408 | tf_op jit(solution)/shard_map/ppermute | solution.py:17
  27.4 4.9 %copy-start.1 = (f32[50,4,16,256]{3,0,2,1:T(8,128)S(1)}, f32[50,4,16,256]{3,0,2,1:T(8,128)}, u32[]{:S(2)}) copy-start(f32[50,4,16,256]{3,0,2,1:T(8,128)} %copy-done) | copy-start | bytes 9830404
  32.3 1.9 %copy-start.3 = (f32[50,4,16,256]{3,2,1,0:T(8,128)S(1)}, f32[50,4,16,256]{3,2,1,0:T(8,128)}, u32[]{:S(2)}) copy-start(f32[50,4,16,256]{3,2,1,0:T(8,128)} %param.6) | copy-start | bytes 9830404
  39.4 12.5 %collective-permute-start.4 = (f32[50,4,1,256]{3,0,2,1:T(8,128)S(1)}, f32[50,4,1,256]{3,0,2,1:T(8,128)S(1)}, u32[]{:S(2)}, u32[]{:S(2)}) collective-permute-start(f32[50,4,1,256]{3,0,2,1:T(8,128)S(1)} %get-tuple-element.13), channel_id=1, source_target_pairs={{0,8},{8,16},{16,24},{24,32},{32,40},{40,48},{48,56},{56,64},{64,7... | collective-permute-start | bytes 614408 | tf_op jit(solution)/shard_map/ppermute | solution.py:16
  41.3 10.8 %collective-permute-start.5 = (f32[50,4,1,256]{3,0,2,1:T(8,128)S(1)}, f32[50,4,1,256]{3,0,2,1:T(8,128)S(1)}, u32[]{:S(2)}, u32[]{:S(2)}) collective-permute-start(f32[50,4,1,256]{3,0,2,1:T(8,128)S(1)} %get-tuple-element.12), channel_id=1, source_target_pairs={{8,0},{16,8},{24,16},{32,24},{40,32},{48,40},{56,48},{64,56},{72,6... | collective-permute-start | bytes 614408 | tf_op jit(solution)/shard_map/ppermute | solution.py:17
  62.5 17.3 %collective-permute-start.6 = (f32[50,1,16,256]{3,2,1,0:T(8,128)S(1)}, f32[50,1,16,256]{3,2,1,0:T(8,128)S(1)}, u32[]{:S(2)}, u32[]{:S(2)}) collective-permute-start(f32[50,1,16,256]{3,2,1,0:T(8,128)S(1)} %copy.35), channel_id=1, source_target_pairs={{0,1},{1,2},{2,3},{3,4},{4,5},{5,6},{6,7},{7,0},{8,9},{9,10},{10,1... | collective-permute-start | bytes 2457608 | tf_op jit(solution)/shard_map/ppermute | solution.py:16
  64.4 15.9 %collective-permute-start.7 = (f32[50,1,16,256]{3,2,1,0:T(8,128)S(1)}, f32[50,1,16,256]{3,2,1,0:T(8,128)S(1)}, u32[]{:S(2)}, u32[]{:S(2)}) collective-permute-start(f32[50,1,16,256]{3,2,1,0:T(8,128)S(1)} %copy.37), channel_id=1, source_target_pairs={{1,0},{2,1},{3,2},{4,3},{5,4},{6,5},{7,6},{0,7},{9,8},{10,9},{11,1... | collective-permute-start | bytes 2457608 | tf_op jit(solution)/shard_map/ppermute | solution.py:17
  82.6 1.8 %copy-start.2 = (f32[50,4,16,256]{3,0,2,1:T(8,128)}, f32[50,4,16,256]{3,0,2,1:T(8,128)S(1)}, u32[]{:S(2)}) copy-start(f32[50,4,16,256]{3,0,2,1:T(8,128)S(1)} %fusion.13) | copy-start | bytes 9830404
  121.1 9.2 %collective-permute-start.8 = (f32[3,1,256]{2,1,0:T(1,128)S(1)}, f32[3,1,256]{2,1,0:T(1,128)S(1)}, u32[]{:S(2)}, u32[]{:S(2)}) collective-permute-start(f32[3,1,256]{2,1,0:T(1,128)S(1)} %get-tuple-element.20), channel_id=1, source_target_pairs={{8,0},{16,8},{24,16},{32,24},{40,32},{48,40},{56,48},{64,56},{72,6... | collective-permute-start | bytes 9224 | tf_op jit(solution)/shard_map/ppermute | solution.py:17
  123.1 8.5 %collective-permute-start.9 = (f32[3,1,256]{2,1,0:T(1,128)S(1)}, f32[3,1,256]{2,1,0:T(1,128)S(1)}, u32[]{:S(2)}, u32[]{:S(2)}) collective-permute-start(f32[3,1,256]{2,1,0:T(1,128)S(1)} %get-tuple-element.21), channel_id=1, source_target_pairs={{0,8},{8,16},{16,24},{24,32},{32,40},{40,48},{48,56},{56,64},{64,7... | collective-permute-start | bytes 9224 | tf_op jit(solution)/shard_map/ppermute | solution.py:16
where the time goes:
time: 133 us; the launch traced here: 132 us
  starting transfers between devices  37.1 us (28%)
  blocking collectives  34.8 us (26%)
  other arithmetic  32.9 us (25%)
  waiting for transfers between devices  13.6 us (10%)
  local copies, waits for them, and re-layouts  10.9 us (8%)
  matrix products  1.93 us (1%)
    psum x1, blocking collectives, per_device(): summed = lax.psum(partial_value, 'dir')  34.8 us
    ppermute x5, starting transfers between devices, with_halo(): after = lax.ppermute(first, axis, down)  27.3 us
    ppermute x5, waiting for transfers between devices, with_halo(): before = lax.ppermute(last, axis, up)  13.4 us
    add x5, other arithmetic, upwind(): jnp.maximum(velocity, 0.0) * behind + jnp.minimum(velocity, 0.0) * in_front  13 us
    mul x2, other arithmetic, advance(): return land_cells * (middle - change)  12.6 us
    ppermute x5, starting transfers between devices, with_halo(): before = lax.ppermute(last, axis, up)  9.81 us
    unnamed x19, local copies, waits for them, and re-layouts  9.12 us
    mul x1, other arithmetic, per_device(): spectra = land_cells * action  3.85 us
  transfers between devices with their start and end apart: 10, of which 3 were waited for; matrix products, arithmetic and copies ran while one was open for 14% of the time, Pallas kernels for 0%

commit v1 on v0

v1 whole, which is shorter than its diff:
```python
import math
import functools

import numpy as np
import jax
import jax.numpy as jnp
from jax import lax
from jax.sharding import PartitionSpec as P
from jax.experimental import pallas as pl
from jax.experimental.pallas import tpu as pltpu

F32 = jnp.float32
LANES = 128
SUB = 8


def iota_masks():
    s = lax.broadcasted_iota(jnp.int32, (SUB, LANES), 0)
    l = lax.broadcasted_iota(jnp.int32, (SUB, LANES), 1)
    return s, l


def roll(x, shift, axis):
    return pltpu.roll(x, shift, axis)


class Grid:
    def __init__(self):
        s, l = iota_masks()
        self.s = s
        self.first_row = s == 0
        self.last_row = s == SUB - 1
        self.first_col = l == 0
        self.last_col = l == LANES - 1

    def below(self, t, hi):
        n, m = len(t), len(t[0])
        moved = [[roll(t[r][c], SUB - 1, 0) for c in range(m)] for r in range(n)]
        return [
            [
                jnp.where(self.last_row, moved[r + 1][c] if r + 1 < n else hi[c], moved[r][c])
                for c in range(m)
            ]
            for r in range(n)
        ]

    def above(self, t, lo):
        n, m = len(t), len(t[0])
        moved = [[roll(t[r][c], 1, 0) for c in range(m)] for r in range(n)]
        return [
            [
                jnp.where(self.first_row, moved[r - 1][c] if r > 0 else lo[c], moved[r][c])
                for c in range(m)
            ]
            for r in range(n)
        ]

    def right(self, row):
        m = len(row)
        moved = [roll(v, LANES - 1, 1) for v in row]
        return [
            jnp.where(self.last_col, moved[c + 1] if c + 1 < m else 0.0, moved[c]) for c in range(m)
        ]

    def left(self, row, start):
        m = len(row)
        moved = [roll(v, 1, 1) for v in row]
        return [
            jnp.where(self.first_col, moved[c - 1] if c > 0 else start, moved[c]) for c in range(m)
        ]


def face_flux(c, behind, in_front):
    return c * jnp.where(c > 0.0, behind, in_front)


def col_change(g, row, gs, vb, vl):
    right = g.right(row)
    flux = [face_flux(gs + vb[c], row[c], right[c]) for c in range(len(row))]
    edge = jnp.minimum(gs + vl, 0.0) * row[0]
    left = g.left(flux, edge)
    return [flux[c] - left[c] for c in range(len(row))]


def advance(g, t, gc, gs, ub, ub0, vb, vl, land, lo, hi):
    n, m = len(t), len(t[0])
    ahead = g.below(t, hi)
    flux = [[face_flux(gc + ub[r][c], t[r][c], ahead[r][c]) for c in range(m)] for r in range(n)]
    start = [face_flux(gc + ub0[c], lo[c], t[0][c]) for c in range(m)]
    before = g.above(flux, start)
    out = []
    for r in range(n):
        dy = col_change(g, t[r], gs, vb[r], vl[r])
        out.append(
            [land[r][c] * (t[r][c] - ((flux[r][c] - before[r][c]) + dy[c])) for c in range(m)]
        )
    return out


def tiles(ref, *lead):
    rows, cols = ref.shape[-2] // SUB, ref.shape[-1] // LANES
    return [
        [ref[(*lead, pl.ds(r * SUB, SUB), pl.ds(c * LANES, LANES))] for c in range(cols)]
        for r in range(rows)
    ]


def put_tiles(ref, t, *lead):
    for r, row in enumerate(t):
        for c, v in enumerate(row):
            ref[(*lead, pl.ds(r * SUB, SUB), pl.ds(c * LANES, LANES))] = v


def spread_row(ref, cols, *index):
    *lead, row = index
    return [
        jnp.broadcast_to(ref[(*lead, pl.ds(row, 1), pl.ds(c * LANES, LANES))], (SUB, LANES))
        for c in range(cols)
    ]


def turning(shears, sine, cosine, total_dirs):
    ux, uy, vx, vy = shears
    scale = total_dirs / (2.0 * math.pi)
    return [
        [
            scale
            * (
                sine * cosine * (ux[r][c] - vy[r][c])
                + sine * sine * uy[r][c]
                - cosine * cosine * vx[r][c]
            )
            for c in range(len(ux[0]))
        ]
        for r in range(len(ux))
    ]


def half_sum(a, b):
    return [[0.5 * (x + y) for x, y in zip(p, q)] for p, q in zip(a, b)]


def half_diff(a, b):
    return [[0.5 * (x - y) for x, y in zip(p, q)] for p, q in zip(a, b)]


def shears_of(g, u, v, u_lo, u_hi, v_lo, v_hi):
    ux = half_diff(g.below(u, u_hi), g.above(u, u_lo))
    vx = half_diff(g.below(v, v_hi), g.above(v, v_lo))
    uy = half_diff([g.right(r) for r in u], [g.left(r, 0.0) for r in u])
    vy = half_diff([g.right(r) for r in v], [g.left(r, 0.0) for r in v])
    return ux, uy, vx, vy


COS, SIN, FCOS, FSIN = 0, 6, 12, 17
TABLE = 22


def angle_table(sectors, per):
    total = sectors * per
    step = 2.0 * math.pi / total
    out = np.zeros((sectors, TABLE), np.float64)
    for k in range(sectors):
        d = np.arange(-1, per + 1) + k * per
        out[k, COS : COS + per + 2] = np.cos(d * step)
        out[k, SIN : SIN + per + 2] = np.sin(d * step)
        face = (np.arange(per + 1) + k * per - 0.5) * step
        out[k, FCOS : FCOS + per + 1] = np.cos(face)
        out[k, FSIN : FSIN + per + 1] = np.sin(face)
    return out.astype(np.float32)


def rows_kernel(x_ref, cur_ref, land_ref, up_ref, dn_ref):
    i = pl.program_id(0)
    count = x_ref.shape[0] // 32
    last = up_ref.shape[1] - SUB
    for ref, rows in ((up_ref, (14, 15)), (dn_ref, (0, 1))):
        for k, row in enumerate(rows):
            land = [
                jnp.broadcast_to(
                    land_ref[pl.ds(row, 1), pl.ds(c * LANES, LANES)].astype(F32), (SUB, LANES)
                )
                for c in range(2)
            ]
            for q in range(count // SUB):
                for c in range(2):
                    start = q * SUB * 32 + (row // SUB * 2 + c) * SUB + row % SUB
                    v = x_ref[pl.ds(start, SUB, stride=32), :]
                    at = pl.multiple_of(i * count + q * SUB, SUB)
                    ref[k, pl.ds(at, SUB), pl.ds(c * LANES, LANES)] = v * land[c]

    @pl.when(i == 0)
    def _():
        for ref, rows in ((up_ref, (14, 15)), (dn_ref, (0, 1))):
            for k, row in enumerate(rows):
                ref[k, pl.ds(last, SUB), :] = jnp.zeros((SUB, 2 * LANES), F32)
                ref[k, pl.ds(last, 1), :] = cur_ref[0, pl.ds(row, 1), :]
                ref[k, pl.ds(last + 1, 1), :] = cur_ref[1, pl.ds(row, 1), :]
                ref[k, pl.ds(last + 2, 1), :] = land_ref[pl.ds(row, 1), :].astype(F32)


def pack_inner(g, a, b):
    low2 = g.s < 6
    first = jnp.where(low2, roll(a[0], 6, 0), roll(a[1], 6, 0))
    mid = jnp.where(g.s < 4, roll(a[1], 6, 0), roll(b[0], 2, 0))
    last = jnp.where(g.s < 2, roll(b[0], 2, 0), roll(b[1], 2, 0))
    return first, mid, last


def pack_outer(g, a, b):
    one = jnp.where(g.s < 2, a[0], roll(a[1], 4, 0))
    two = jnp.where(g.s < 6, roll(b[0], 4, 0), b[1])
    return jnp.where(g.s < 4, one, two)


def unpack(g, inner, outer):
    a, b, c = inner
    a2, b2, b6, c6, o4 = roll(a, 2, 0), roll(b, 2, 0), roll(b, 6, 0), roll(c, 6, 0), roll(outer, 4, 0)
    low2, low6 = g.s < 2, g.s < 6
    one = [jnp.where(low2, outer, a2), jnp.where(low2, a2, jnp.where(low6, b2, o4))]
    two = [jnp.where(low2, o4, jnp.where(low6, b6, c6)), jnp.where(low6, c6, outer)]
    return one, two


def ends_kernel(total, sec_ref, tab_ref, cg_ref, x0_ref, x3_ref, cur_ref, land_ref,
                prev_ref, next_ref, ub_s, vb_s, k_s):
    g = Grid()
    i = pl.program_id(0)
    sec = sec_ref[0]
    freqs = x0_ref.shape[0]
    zero = [jnp.zeros((SUB, LANES), F32)] * 2

    @pl.when(i == 0)
    def _():
        u, v = tiles(cur_ref, 0), tiles(cur_ref, 1)
        put_tiles(ub_s, half_sum(u, g.below(u, zero)))
        put_tiles(vb_s, half_sum(v, [g.right(r) for r in v]))
        sh = shears_of(g, u, v, zero, zero, zero, zero)
        for n, f in ((0, 0), (1, 4)):
            put_tiles(k_s, turning(sh, tab_ref[sec, FSIN + f], tab_ref[sec, FCOS + f], total), n)

    def one(pair, _):
        for n, (x_ref, out_ref, d) in enumerate(((x0_ref, prev_ref, 0), (x3_ref, next_ref, 3))):
            ends = []
            for h in range(2):
                f = pair * 2 + h
                cg = cg_ref[i * freqs + f]
                gc, gs = cg * tab_ref[sec, COS + 1 + d], cg * tab_ref[sec, SIN + 1 + d]
                ub, vb = tiles(ub_s), tiles(vb_s)
                vl = [0.5 * cur_ref[1, pl.ds(r * SUB, SUB), pl.ds(0, LANES)] for r in range(2)]
                land = [[m.astype(F32) for m in row] for row in tiles(land_ref)]
                t = tiles(x_ref, f, 0)
                t = [[land[r][c] * t[r][c] for c in range(2)] for r in range(2)]
                for _s in range(2):
                    t = advance(g, t, gc, gs, ub, zero, vb, vl, land, zero, zero)
                k = tiles(k_s, n)
                limit = jnp.minimum if d == 0 else jnp.maximum
                ends.append([[limit(k[r][c], 0.0) * t[r][c] for c in range(2)] for r in range(2)])
            for c in range(2):
                got = pack_inner(g, [ends[0][r][c] for r in range(2)], [ends[1][r][c] for r in range(2)])
                for q in range(3):
                    out_ref[pair, pl.ds(q * SUB, SUB), pl.ds(c * LANES, LANES)] = got[q]
        return 0

    lax.fori_loop(0, freqs // 2, one, 0)


def main_kernel(total, sec_ref, tab_ref, cg_ref, ratio_ref, weight_ref,
                x_ref, cgc_ref, cgs_ref, cur_ref, land_ref,
                top_ref, bot_ref, ownup_ref, owndn_ref, topf_ref, botf_ref,
                new_ref, prev_ref, next_ref, force_ref, brow_ref,
                ub_s, ub0_s, vb_s, k_s, fld_s, at_s, ab_s, r_s, b_s):
    g = Grid()
    i = pl.program_id(0)
    blocks = pl.num_programs(0)
    sec = sec_ref[0]
    freqs = x_ref.shape[0]
    dirs = x_ref.shape[1]

    @pl.when(i == 0)
    def _():
        u, v = tiles(cur_ref, 0), tiles(cur_ref, 1)
        um2, vm2, lm2 = (spread_row(topf_ref, 2, 0, n) for n in range(3))
        um1, vm1, lm1 = (spread_row(topf_ref, 2, 1, n) for n in range(3))
        up0, vp0, lp0 = (spread_row(botf_ref, 2, 0, n) for n in range(3))
        up1, vp1, lp1 = (spread_row(botf_ref, 2, 1, n) for n in range(3))
        u0 = spread_row(cur_ref, 2, 0, 0)
        u15 = spread_row(cur_ref, 2, 0, 15)
        put_tiles(ub_s, half_sum(u, g.below(u, up0)))
        put_tiles(vb_s, half_sum(v, [g.right(r) for r in v]))
        put_tiles(ub0_s, half_sum([um1], [u0]))
        put_tiles(fld_s, half_sum([um2], [um1]), 0)
        put_tiles(fld_s, half_sum([u15], [up0]), 1)
        put_tiles(fld_s, half_sum([up0], [up1]), 2)
        put_tiles(fld_s, half_sum([vm1], [g.right(vm1)]), 3)
        put_tiles(fld_s, half_sum([vp0], [g.right(vp0)]), 4)
        put_tiles(fld_s, [[0.5 * w for w in vm1]], 5)
        put_tiles(fld_s, [[0.5 * w for w in vp0]], 6)
        put_tiles(fld_s, [lm1], 7)
        put_tiles(fld_s, [lp0], 8)
        sh = shears_of(g, u, v, um1, up0, vm1, vp0)
        for f in range(dirs + 1):
            put_tiles(k_s, turning(sh, tab_ref[sec, FSIN + f], tab_ref[sec, FCOS + f], total), f)
        r_s[...] = jnp.zeros_like(r_s)
        b_s[...] = jnp.zeros_like(b_s)

    def field(n):
        return [fld_s[n, :, pl.ds(c * LANES, LANES)] for c in range(2)]

    for q in range(freqs * dirs // SUB):
        at = pl.ds(q * SUB, SUB)
        gc, gs = cgc_ref[at, :], cgs_ref[at, :]
        row = lambda ref, n: [ref[n, at, pl.ds(c * LANES, LANES)] for c in range(2)]
        for outer, mid, inner, ca, cb, nv, nl, nm, sign, out in (
            (row(top_ref, 0), row(top_ref, 1), row(owndn_ref, 0), field(0),
             [ub0_s[:, pl.ds(c * LANES, LANES)] for c in range(2)], 3, 5, 7, 1, at_s),
            (row(ownup_ref, 1), row(bot_ref, 0), row(bot_ref, 1), field(1), field(2), 4, 6, 8, 1, ab_s),
        ):
            fa = [face_flux(gc + ca[c], outer[c], mid[c]) for c in range(2)]
            fb = [face_flux(gc + cb[c], mid[c], inner[c]) for c in range(2)]
            dy = col_change(g, mid, gs, field(nv), field(nl)[0])
            lm = field(nm)
            for c in range(2):
                out[at, pl.ds(c * LANES, LANES)] = lm[c] * (mid[c] - ((fb[c] - fa[c]) + dy[c]))

    ub0 = [ub0_s[:, pl.ds(c * LANES, LANES)] for c in range(2)]

    def one(pair, _):
        outs = [[], []]
        group = pl.ds(pl.multiple_of(pair * SUB, SUB), SUB)

        def beside(ref, n, *lead):
            return [
                jnp.broadcast_to(ref[(*lead, group, pl.ds(c * LANES, LANES))][n : n + 1], (SUB, LANES))
                for c in range(2)
            ]

        for h in range(2):
            f = pair * 2 + h
            cg = cg_ref[i * freqs + f]
            w = weight_ref[i * freqs + f]
            wr = w * ratio_ref[i * freqs + f]
            a2 = []
            for d in range(dirs):
                gc, gs = cg * tab_ref[sec, COS + 1 + d], cg * tab_ref[sec, SIN + 1 + d]
                ub, vb = tiles(ub_s), tiles(vb_s)
                vl = [0.5 * cur_ref[1, pl.ds(r * SUB, SUB), pl.ds(0, LANES)] for r in range(2)]
                land = [[m.astype(F32) for m in rw] for rw in tiles(land_ref)]
                t = tiles(x_ref, f, d)
                t = [[land[r][c] * t[r][c] for c in range(2)] for r in range(2)]
                lo, hi = beside(top_ref, h * dirs + d, 1), beside(bot_ref, h * dirs + d, 0)
                t = advance(g, t, gc, gs, ub, ub0, vb, vl, land, lo, hi)
                lo, hi = beside(at_s, h * dirs + d), beside(ab_s, h * dirs + d)
                t = advance(g, t, gc, gs, ub, ub0, vb, vl, land, lo, hi)
                a2.append(t)
            for r in range(2):
                for c in range(2):
                    here = (pl.ds(r * SUB, SUB), pl.ds(c * LANES, LANES))
                    v = [a2[d][r][c] for d in range(dirs)]
                    for d in range(dirs):
                        r_s[(d, *here)] += wr * v[d]
                    b_s[here] += w * ((v[0] + v[1]) + (v[2] + v[3]))
                    k = [k_s[(n, *here)] for n in range(dirs + 1)]
                    inside = [face_flux(k[d + 1], v[d], v[d + 1]) for d in range(dirs - 1)]
                    new_ref[(f, 1, *here)] = v[1] - (inside[1] - inside[0])
                    new_ref[(f, 2, *here)] = v[2] - (inside[2] - inside[1])
                    new_ref[(f, 0, *here)] = v[0] - (inside[0] - jnp.minimum(k[0], 0.0) * v[0])
                    new_ref[(f, 3, *here)] = v[3] - (jnp.maximum(k[4], 0.0) * v[3] - inside[2])
            k0, k4 = tiles(k_s, 0), tiles(k_s, dirs)
            outs[0].append([[jnp.minimum(k0[r][c], 0.0) * a2[0][r][c] for c in range(2)] for r in range(2)])
            outs[1].append([[jnp.maximum(k4[r][c], 0.0) * a2[3][r][c] for c in range(2)] for r in range(2)])
        for ref, ends in ((prev_ref, outs[0]), (next_ref, outs[1])):
            for c in range(2):
                ref[pair, :, pl.ds(c * LANES, LANES)] = pack_outer(
                    g, [ends[0][r][c] for r in range(2)], [ends[1][r][c] for r in range(2)]
                )
        return 0

    lax.fori_loop(0, freqs // 2, one, 0)

    @pl.when(i == blocks - 1)
    def _():
        cs = [tab_ref[sec, COS + n] for n in range(dirs + 2)]
        sn = [tab_ref[sec, SIN + n] for n in range(dirs + 2)]
        coef = (
            [1.0 + a * a for a in cs],
            [a * b for a, b in zip(sn, cs)],
            [1.0 + b * b for b in sn],
        )
        k = [tiles(k_s, n) for n in range(dirs + 1)]
        b = tiles(b_s)
        stress = []
        for n, co in enumerate(coef):
            total_s = [[None] * 2 for _ in range(2)]
            for r in range(2):
                for c in range(2):
                    here = (pl.ds(r * SUB, SUB), pl.ds(c * LANES, LANES))
                    acc = -0.5 * b[r][c] if n != 1 else jnp.zeros((SUB, LANES), F32)
                    for d in range(dirs):
                        q = (
                            co[d + 1]
                            + jnp.maximum(k[d + 1][r][c], 0.0) * (co[d + 2] - co[d + 1])
                            + jnp.minimum(k[d][r][c], 0.0) * (co[d + 1] - co[d])
                        )
                        acc = acc + q * r_s[(d, *here)]
                    total_s[r][c] = acc
            stress.append(total_s)
        zero = [jnp.zeros((SUB, LANES), F32)] * 2
        xx, xy, yy = stress
        dx = lambda t: half_diff(g.below(t, zero), g.above(t, zero))
        dy = lambda t: half_diff([g.right(r) for r in t], [g.left(r, 0.0) for r in t])
        for n, (p, q) in enumerate(((dx(xx), dy(xy)), (dx(xy), dy(yy)))):
            put_tiles(force_ref, [[-(p[r][c] + q[r][c]) for c in range(2)] for r in range(2)], n)
        for n, t in enumerate((xx, xy)):
            for c in range(2):
                brow_ref[0, pl.ds(n, 1), pl.ds(c * LANES, LANES)] = 0.5 * t[1][c][7:8, :]
                brow_ref[1, pl.ds(n, 1), pl.ds(c * LANES, LANES)] = -0.5 * t[0][c][0:1, :]


def join_kernel(e_ref, inp_ref, inn_ref, outp_ref, outn_ref, o_ref):
    g = Grid()
    j = pl.program_id(1)
    pairs = inp_ref.shape[0]

    def run(inner_ref, outer_ref, sign):
        def one(pair, _):
            for c in range(2):
                cc = pl.ds(c * LANES, LANES)
                inner = [inner_ref[pair, pl.ds(q * SUB, SUB), cc] for q in range(3)]
                both = unpack(g, inner, outer_ref[pair, :, cc])
                for h in range(2):
                    for r in range(2):
                        at = (pair * 2 + h, 0, pl.ds(r * SUB, SUB), cc)
                        o_ref[at] = e_ref[at] + sign * both[h][r]
            return 0

        lax.fori_loop(0, pairs, one, 0)

    @pl.when(j == 0)
    def _():
        run(inp_ref, outp_ref, 1.0)

    @pl.when(j == 1)
    def _():
        run(inn_ref, outn_ref, -1.0)


def per_device(sectors, points, action, currents, land_mask, group_speed, group_ratio, bin_weight):
    freqs, dirs, rows, cols = action.shape
    total = dirs * sectors
    table = jnp.asarray(angle_table(sectors, dirs))
    sec = lax.axis_index("dir").reshape(1).astype(jnp.int32)
    smem = pl.BlockSpec(memory_space=pltpu.SMEM)
    whole = lambda a: pl.BlockSpec(a.shape, lambda i: (0,) * a.ndim)
    fb = 10
    nb = freqs // fb
    combos = freqs * dirs
    f32 = lambda *s: jax.ShapeDtypeStruct(s, F32)
    vmem = lambda *s: pltpu.VMEM(s, F32)
    params = lambda: pltpu.CompilerParams(vmem_limit_bytes=24 * 2**20)

    flat = action.reshape(combos, rows // SUB, SUB, cols // LANES, LANES)
    flat = flat.transpose(0, 1, 3, 2, 4).reshape(combos * rows * cols // LANES, LANES)
    up_rows, dn_rows = pl.pallas_call(
        rows_kernel,
        grid=(nb,),
        in_specs=[
            pl.BlockSpec((fb * dirs * rows * cols // LANES, LANES), lambda i: (i, 0)),
            whole(currents),
            whole(land_mask),
        ],
        out_specs=[pl.BlockSpec((2, combos + SUB, cols), lambda i: (0, 0, 0))] * 2,
        out_shape=[f32(2, combos + SUB, cols)] * 2,
        compiler_params=params(),
        name="boundary_rows",
    )(flat, currents, land_mask)
    up = [(i, i + 1) for i in range(points - 1)]
    down = [(j, i) for i, j in up]
    top = lax.ppermute(up_rows, "pts", up)
    bot = lax.ppermute(dn_rows, "pts", down)

    in_prev, in_next = pl.pallas_call(
        functools.partial(ends_kernel, total),
        grid=(nb,),
        in_specs=[
            smem, smem, smem,
            pl.BlockSpec((fb, 1, rows, cols), lambda i: (i, 0, 0, 0)),
            pl.BlockSpec((fb, 1, rows, cols), lambda i: (i, dirs - 1, 0, 0)),
            whole(currents),
            whole(land_mask),
        ],
        out_specs=[pl.BlockSpec((fb // 2, 24, cols), lambda i: (i, 0, 0))] * 2,
        out_shape=[f32(freqs // 2, 24, cols)] * 2,
        scratch_shapes=[vmem(rows, cols), vmem(rows, cols), vmem(2, rows, cols)],
        compiler_params=params(),
        name="sector_ends",
    )(sec, table, group_speed, action, action, currents, land_mask)
    fwd = [(i, (i + 1) % sectors) for i in range(sectors)]
    back = [(j, i) for i, j in fwd]
    inner_from_prev = lax.ppermute(in_next, "dir", fwd)
    inner_from_next = lax.ppermute(in_prev, "dir", back)

    angles = table[lax.axis_index("dir")]
    cgc = (group_speed[:, None] * angles[None, COS + 1 : COS + 1 + dirs]).reshape(combos, 1)
    cgs = (group_speed[:, None] * angles[None, SIN + 1 : SIN + 1 + dirs]).reshape(combos, 1)
    cgc = jnp.broadcast_to(cgc, (combos, LANES))
    cgs = jnp.broadcast_to(cgs, (combos, LANES))
    cb = fb * dirs
    halo = pl.BlockSpec((2, cb, cols), lambda i: (0, i, 0))
    halo_fields = pl.BlockSpec((2, SUB, cols), lambda i: (0, combos // SUB, 0))
    part, out_prev, out_next, force, brow = pl.pallas_call(
        functools.partial(main_kernel, total),
        grid=(nb,),
        in_specs=[
            smem, smem, smem, smem, smem,
            pl.BlockSpec((fb, dirs, rows, cols), lambda i: (i, 0, 0, 0)),
            pl.BlockSpec((cb, LANES), lambda i: (i, 0)),
            pl.BlockSpec((cb, LANES), lambda i: (i, 0)),
            whole(currents),
            whole(land_mask),
            halo, halo, halo, halo, halo_fields, halo_fields,
        ],
        out_specs=[
            pl.BlockSpec((fb, dirs, rows, cols), lambda i: (i, 0, 0, 0)),
            pl.BlockSpec((fb // 2, SUB, cols), lambda i: (i, 0, 0)),
            pl.BlockSpec((fb // 2, SUB, cols), lambda i: (i, 0, 0)),
            pl.BlockSpec((2, rows, cols), lambda i: (0, 0, 0)),
            pl.BlockSpec((2, 2, cols), lambda i: (0, 0, 0)),
        ],
        out_shape=[
            f32(freqs, dirs, rows, cols),
            f32(freqs // 2, SUB, cols),
            f32(freqs // 2, SUB, cols),
            f32(2, rows, cols),
            f32(2, 2, cols),
        ],
        scratch_shapes=[
            vmem(rows, cols), vmem(SUB, cols), vmem(rows, cols), vmem(dirs + 1, rows, cols),
            vmem(9, SUB, cols), vmem(cb, cols), vmem(cb, cols),
            vmem(dirs, rows, cols), vmem(rows, cols),
        ],
        compiler_params=params(),
        name="transport",
    )(sec, table, group_speed, group_ratio, bin_weight, action, cgc, cgs, currents, land_mask,
      top, bot, up_rows, dn_rows, top, bot)

    from_above = lax.ppermute(brow[0], "pts", up)
    from_below = lax.ppermute(brow[1], "pts", down)
    outer_from_prev = lax.ppermute(out_next, "dir", fwd)
    outer_from_next = lax.ppermute(out_prev, "dir", back)
    force = jnp.concatenate(
        [force[:, :1] + from_above[:, None], force[:, 1:-1], force[:, -1:] + from_below[:, None]], axis=1
    )
    half = sectors // 2
    force = force + lax.ppermute(force, "dir", [(i, (i + half) % sectors) for i in range(sectors)])
    near = [
        lax.ppermute(
            force, "dir", [(i, i // half * half + (i % half + s) % half) for i in range(sectors)]
        )
        for s in range(1, half)
    ]
    force = (force + near[1]) + (near[0] + near[2])

    new_action = pl.pallas_call(
        join_kernel,
        grid=(nb, 2),
        in_specs=[
            pl.BlockSpec((fb, 1, rows, cols), lambda i, j: (i, j * (dirs - 1), 0, 0)),
            pl.BlockSpec((fb // 2, 24, cols), lambda i, j: (i, 0, 0)),
            pl.BlockSpec((fb // 2, 24, cols), lambda i, j: (i, 0, 0)),
            pl.BlockSpec((fb // 2, SUB, cols), lambda i, j: (i, 0, 0)),
            pl.BlockSpec((fb // 2, SUB, cols), lambda i, j: (i, 0, 0)),
        ],
        out_specs=pl.BlockSpec((fb, 1, rows, cols), lambda i, j: (i, j * (dirs - 1), 0, 0)),
        out_shape=f32(freqs, dirs, rows, cols),
        input_output_aliases={0: 0},
        compiler_params=params(),
        name="join_sectors",
    )(part, inner_from_prev, inner_from_next, outer_from_prev, outer_from_next)
    return new_action, force


def solution(mesh):
    in_specs = (P(None, "dir", "pts", None), P(None, "pts", None), P("pts", None), P(), P(), P())
    out_specs = (P(None, "dir", "pts", None), P(None, "pts", None))
    return jax.shard_map(
        functools.partial(per_device, mesh.shape["dir"], mesh.shape["pts"]),
        mesh=mesh, in_specs=in_specs, out_specs=out_specs, check_vma=False,
    )
```

time: 133 us -> 86.9 us (0.65)
  blocking collectives: 34.8 us -> 0 us
  other arithmetic: 32.9 us -> 0.73 us
  Pallas kernels: 0 us -> 29.3 us
  waiting for transfers between devices: 13.6 us -> 23.2 us
  starting transfers between devices: 37.1 us -> 27.7 us
  local copies, waits for them, and re-layouts: 10.9 us -> 3.94 us
  matrix products: 1.93 us -> 0 us
    psum x1 -> x0, blocking collectives: 34.8 us -> none  [per_device(): summed = lax.psum(partial_value, 'dir')]
    pallas_call x0 -> x4, Pallas kernels: none -> 29.3 us  [the longest x1 12.6 us: per_device(): pl.pallas_call(functools.partial(main_kernel, total), grid=(nb,), in_spec...]
    mul x13 -> x1, other arithmetic: 16.9 us -> 0.07 us  [per_device(): group_speed[:, None] * angles[None, SIN + 1:SIN + 1 + dirs]]
    add x6 -> x3, other arithmetic: 13 us -> 0.65 us  [the longest x1 0.63 us: per_device(): force = force + near[1] + (near[0] + near[2])]
    ppermute x10 -> x12, waiting for transfers between devices: 13.6 us -> 23.2 us  [the longest x1 9.31 us: per_device(): lax.ppermute(force, 'dir', [(i, (i + half) % sectors) for i in range(sect...]
    ppermute x10 -> x12, starting transfers between devices: 37.1 us -> 27.7 us  [the longest x1 8.05 us: per_device(): bot = lax.ppermute(dn_rows, 'pts', down)]
    unnamed x19 -> x20, local copies, waits for them, and re-layouts: 9.12 us -> 3.44 us
    dot_general x1 -> x0, matrix products: 1.93 us -> none  [per_device(): jnp.einsum('kfd,fdry->kry', stress_table(angles, bin_weight, group_ratio)...]
  transfers between devices with their start and end apart: 10 -> 12, of which waited for: 3 -> 7; matrix products, arithmetic and copies ran while one was open for 14% -> 1% of each run, Pallas kernels for 0% -> 10%
where the time goes in v1:
time: 86.9 us; the launch traced here: 85.8 us
  Pallas kernels  29.3 us (34%)
  starting transfers between devices  27.7 us (32%)
  waiting for transfers between devices  23.2 us (27%)
  local copies, waits for them, and re-layouts  3.94 us (5%)
    pallas_call x1, Pallas kernels, per_device(): pl.pallas_call(functools.partial(main_kernel, total), grid=(nb,), in_spec...  12.6 us
    ppermute x1, waiting for transfers between devices, per_device(): lax.ppermute(force, 'dir', [(i, (i + half) % sectors) for i in range(sect...  9.31 us
    pallas_call x1, Pallas kernels, per_device(): pl.pallas_call(functools.partial(ends_kernel, total), grid=(nb,), in_spec...  8.66 us
    ppermute x1, starting transfers between devices, per_device(): bot = lax.ppermute(dn_rows, 'pts', down)  8.05 us
    ppermute x1, starting transfers between devices, per_device(): from_below = lax.ppermute(brow[1], 'pts', down)  7.43 us
    pallas_call x1, Pallas kernels, per_device(): pl.pallas_call(join_kernel, grid=(nb, 2), in_specs=[pl.BlockSpec((fb, 1,...  6.58 us
    ppermute x3, waiting for transfers between devices, per_device(): lax.ppermute(force, 'dir', [(i, i // half * half + (i % half + s) % half)...  4.79 us
    ppermute x1, waiting for transfers between devices, per_device(): top = lax.ppermute(up_rows, 'pts', up)  3.79 us
  transfers between devices with their start and end apart: 12, of which 7 were waited for; matrix products, arithmetic and copies ran while one was open for 1% of the time, Pallas kernels for 10%

profile of v1, /device:TPU:6, one launch (start us, length us, event | category | flops | bytes accessed | tf_op | source)
XLA Modules:
  0.0 85.8 jit_solution(9565661074513992229)
XLA Ops:
  0.7 1.9 %copy-done = f32[50,4,16,256]{3,2,1,0:T(8,128)S(1)} copy-done((f32[50,4,16,256]{3,2,1,0:T(8,128)S(1)}, f32[50,4,16,256]{3,2,1,0:T(8,128)}, u32[]{:S(2)}) %copy-start) | copy-done | bytes 3276824
  2.6 0.8 copy-done.2
  3.4 0.7 copy-done.4
  4.1 1.5 %boundary_rows.1 = (f32[2,208,256]{2,1,0:T(8,128)}, f32[2,208,256]{2,1,0:T(8,128)}) custom-call(f32[6400,128]{1,0:T(8,128)S(1)} %bitcast.18, f32[2,16,256]{2,1,0:T(8,128)S(1)} %copy-done.2, s32[16,256]{1,0:T(8,128)S(1)} %copy-done.4), custom_call_target="tpu_custom_call" | custom-call | tf_op jit(solution)/shard_map/boundary_rows/pallas_call | solution.py:464
  5.6 1.9 %collective-permute-start = (f32[2,208,256]{2,1,0:T(8,128)}, f32[2,208,256]{2,1,0:T(8,128)}, u32[]{:S(2)}, u32[]{:S(2)}) collective-permute-start(f32[2,208,256]{2,1,0:T(8,128)} %get-tuple-element.11.ownup_ref), channel_id=1, source_target_pairs={{0,8},{8,16},{16,24},{24,32},{32,40},{40,48},{48,56},{56,64},{64,7... | collective-permute-start | bytes 1277960 | tf_op jit(solution)/shard_map/ppermute | solution.py:479
  7.5 8.0 %collective-permute-start.1 = (f32[2,208,256]{2,1,0:T(8,128)}, f32[2,208,256]{2,1,0:T(8,128)}, u32[]{:S(2)}, u32[]{:S(2)}) collective-permute-start(f32[2,208,256]{2,1,0:T(8,128)} %get-tuple-element.12.owndn_ref), channel_id=1, source_target_pairs={{8,0},{16,8},{24,16},{32,24},{40,32},{48,40},{56,48},{64,56},{72,6... | collective-permute-start | bytes 1277960 | tf_op jit(solution)/shard_map/ppermute | solution.py:480
  16.0 3.8 %collective-permute-done.top_ref.topf_ref = f32[2,208,256]{2,1,0:T(8,128)} collective-permute-done((f32[2,208,256]{2,1,0:T(8,128)}, f32[2,208,256]{2,1,0:T(8,128)}, u32[]{:S(2)}, u32[]{:S(2)}) %collective-permute-start) | collective-permute-done | bytes 426016 | tf_op jit(solution)/shard_map/ppermute | solution.py:479
  19.7 1.8 %collective-permute-done.1.bot_ref.botf_ref = f32[2,208,256]{2,1,0:T(8,128)} collective-permute-done((f32[2,208,256]{2,1,0:T(8,128)}, f32[2,208,256]{2,1,0:T(8,128)}, u32[]{:S(2)}, u32[]{:S(2)}) %collective-permute-start.1) | collective-permute-done | bytes 426016 | tf_op jit(solution)/shard_map/ppermute | solution.py:480
  21.7 12.6 %transport.1 = (f32[50,4,16,256]{3,2,1,0:T(8,128)}, f32[25,8,256]{2,1,0:T(8,128)S(1)}, f32[25,8,256]{2,1,0:T(8,128)S(1)}, f32[2,16,256]{2,1,0:T(8,128)S(1)}, f32[2,2,256]{2,1,0:T(2,128)S(1)}) custom-call(s32[1]{0:T(128)} %bitcast.sec_ref, f32[8,22]{1,0:T(8,128)S(1)} %copy-done.6, f32[50]{0:T(128)S(1)} %copy-done.7, f32[50]{0:T(128)S(1)} %copy-done.8, ...), custom_call_target="tpu_custom_call" | custom-call | tf_op jit(solution)/shard_map/transport/pallas_call | solution.py:511
  34.3 1.9 %collective-permute-start.6 = (f32[2,256]{1,0:T(2,128)S(1)}, f32[2,256]{1,0:T(2,128)S(1)}, u32[]{:S(2)}, u32[]{:S(2)}) collective-permute-start(f32[2,256]{1,0:T(2,128)S(1)} %get-tuple-element.22), channel_id=1, source_target_pairs={{0,8},{8,16},{16,24},{24,32},{32,40},{40,48},{48,56},{56,64},{64,7... | collective-permute-start | bytes 6152 | tf_op jit(solution)/shard_map/ppermute | solution.py:547
  36.3 7.4 %collective-permute-start.7 = (f32[2,256]{1,0:T(2,128)S(1)}, f32[2,256]{1,0:T(2,128)S(1)}, u32[]{:S(2)}, u32[]{:S(2)}) collective-permute-start(f32[2,256]{1,0:T(2,128)S(1)} %get-tuple-element.23), channel_id=1, source_target_pairs={{8,0},{16,8},{24,16},{32,24},{40,32},{48,40},{56,48},{64,56},{72,6... | collective-permute-start | bytes 6152 | tf_op jit(solution)/shard_map/ppermute | solution.py:548
  43.7 8.7 %sector_ends.1 = (f32[25,24,256]{2,1,0:T(8,128)S(1)}, f32[25,24,256]{2,1,0:T(8,128)S(1)}) custom-call(s32[1]{0:T(128)} %bitcast.sec_ref, f32[8,22]{1,0:T(8,128)S(1)} %copy-done.6, f32[50]{0:T(128)S(1)} %copy-done.7, f32[50,4,16,256]{3,2,1,0:T(8,128)S(1)} %copy-done.1, f32[50,4,16,256]{3,2,1,0:T(8,128)S(1)} %copy-done.1, f32[2,16,256]{2,1,0:T(8,128)S(1)} %copy-done.3, ...), custom_call_target="tpu_custom_call" | custom-call | tf_op jit(solution)/shard_map/sector_ends/pallas_call | solution.py:482
  52.4 1.7 %collective-permute-start.2 = (f32[25,24,256]{2,1,0:T(8,128)S(1)}, f32[25,24,256]{2,1,0:T(8,128)S(1)}, u32[]{:S(2)}, u32[]{:S(2)}) collective-permute-start(f32[25,24,256]{2,1,0:T(8,128)S(1)} %get-tuple-element.14), channel_id=1, source_target_pairs={{0,1},{1,2},{2,3},{3,4},{4,5},{5,6},{6,7},{7,0},{8,9},{9,10},{10,1... | collective-permute-start | bytes 1843208 | tf_op jit(solution)/shard_map/ppermute | solution.py:500
  54.0 2.6 %collective-permute-start.3 = (f32[25,24,256]{2,1,0:T(8,128)S(1)}, f32[25,24,256]{2,1,0:T(8,128)S(1)}, u32[]{:S(2)}, u32[]{:S(2)}) collective-permute-start(f32[25,24,256]{2,1,0:T(8,128)S(1)} %get-tuple-element.15), channel_id=1, source_target_pairs={{1,0},{2,1},{3,2},{4,3},{5,4},{6,5},{7,6},{0,7},{9,8},{10,9},{11,1... | collective-permute-start | bytes 1843208 | tf_op jit(solution)/shard_map/ppermute | solution.py:501
  56.7 0.5 collective-permute-start.8
  57.2 9.3 %collective-permute-done.8 = f32[2,16,256]{2,1,0:T(8,128)S(1)} collective-permute-done((f32[2,16,256]{2,1,0:T(8,128)S(1)}, f32[2,16,256]{2,1,0:T(8,128)S(1)}, u32[]{:S(2)}, u32[]{:S(2)}) %collective-permute-start.8) | collective-permute-done | bytes 32800 | tf_op jit(solution)/shard_map/ppermute | solution.py:555
  66.7 2.0 %collective-permute-start.10 = (f32[2,16,256]{2,1,0:T(8,128)S(1)}, f32[2,16,256]{2,1,0:T(8,128)S(1)}, u32[]{:S(2)}, u32[]{:S(2)}) collective-permute-start(f32[2,16,256]{2,1,0:T(8,128)S(1)} %fusion), channel_id=1, source_target_pairs={{0,1},{1,2},{2,3},{3,0},{4,5},{5,6},{6,7},{7,4},{8,9},{9,10},{10,1... | collective-permute-start | bytes 98312 | tf_op jit(solution)/shard_map/ppermute | solution.py:557
  68.6 2.2 %collective-permute-done.11 = f32[2,16,256]{2,1,0:T(8,128)S(1)} collective-permute-done((f32[2,16,256]{2,1,0:T(8,128)S(1)}, f32[2,16,256]{2,1,0:T(8,128)S(1)}, u32[]{:S(2)}, u32[]{:S(2)}) %collective-permute-start.11) | collective-permute-done | bytes 32800 | tf_op jit(solution)/shard_map/ppermute | solution.py:557
  70.9 2.6 %collective-permute-done.10 = f32[2,16,256]{2,1,0:T(8,128)S(1)} collective-permute-done((f32[2,16,256]{2,1,0:T(8,128)S(1)}, f32[2,16,256]{2,1,0:T(8,128)S(1)}, u32[]{:S(2)}, u32[]{:S(2)}) %collective-permute-start.10) | collective-permute-done | bytes 32800 | tf_op jit(solution)/shard_map/ppermute | solution.py:557
  73.4 1.6 %collective-permute-start.5 = (f32[25,8,256]{2,1,0:T(8,128)S(1)}, f32[25,8,256]{2,1,0:T(8,128)S(1)}, u32[]{:S(2)}, u32[]{:S(2)}) collective-permute-start(f32[25,8,256]{2,1,0:T(8,128)S(1)} %get-tuple-element.17), channel_id=1, source_target_pairs={{1,0},{2,1},{3,2},{4,3},{5,4},{6,5},{7,6},{0,7},{9,8},{10,9},{11,1... | collective-permute-start | bytes 614408 | tf_op jit(solution)/shard_map/ppermute | solution.py:550
  75.0 0.6 add_add_fusion
  75.6 3.1 %collective-permute-done.4.outp_ref = f32[25,8,256]{2,1,0:T(8,128)S(1)} collective-permute-done((f32[25,8,256]{2,1,0:T(8,128)S(1)}, f32[25,8,256]{2,1,0:T(8,128)S(1)}, u32[]{:S(2)}, u32[]{:S(2)}) %collective-permute-start.4) | collective-permute-done | bytes 204832 | tf_op jit(solution)/shard_map/ppermute | solution.py:549
  78.7 0.4 collective-permute-done.5.outn_ref
  79.2 6.6 %join_sectors.1 = f32[50,4,16,256]{3,2,1,0:T(8,128)} custom-call(f32[50,4,16,256]{3,2,1,0:T(8,128)} %get-tuple-element.13.e_ref, f32[25,24,256]{2,1,0:T(8,128)S(1)} %collective-permute-done.2.inp_ref, f32[25,24,256]{2,1,0:T(8,128)S(1)} %collective-permute-done.3.inn_ref, ...), custom_call_target="tpu_custom_call", output_to_operand_aliasing={{}: (0, {})} | custom-call | tf_op jit(solution)/shard_map/join_sectors/pallas_call | solution.py:564
  (40 shorter events, 0.8 us)
Async XLA Ops:
  0.6 15.0 %copy-start.7 = (f32[50]{0:T(128)S(1)}, f32[50]{0:T(128)}, u32[]{:S(2)}) copy-start(f32[50]{0:T(128)} %cg_ref.3) | copy-start | bytes 604
  0.6 21.0 %copy-start.9 = (f32[50]{0:T(128)S(1)}, f32[50]{0:T(128)}, u32[]{:S(2)}) copy-start(f32[50]{0:T(128)} %weight_ref.1) | copy-start | bytes 604
  0.7 21.0 %copy-start.8 = (f32[50]{0:T(128)S(1)}, f32[50]{0:T(128)}, u32[]{:S(2)}) copy-start(f32[50]{0:T(128)} %ratio_ref.1) | copy-start | bytes 604
  0.7 1.9 %copy-start = (f32[50,4,16,256]{3,2,1,0:T(8,128)S(1)}, f32[50,4,16,256]{3,2,1,0:T(8,128)}, u32[]{:S(2)}) copy-start(f32[50,4,16,256]{3,2,1,0:T(8,128)} %x3_ref.1) | copy-start | bytes 9830404
  2.6 0.8 copy-start.2
  3.4 0.7 copy-start.4
  4.1 11.5 %copy-start.6 = (f32[8,22]{1,0:T(8,128)S(1)}, f32[8,22]{1,0:T(8,128)}, u32[]{:S(2)}) copy-start(f32[8,22]{1,0:T(8,128)} %constant.10.clone.tab_ref) | copy-start | bytes 2116
  4.1 17.6 %copy-start.1 = (f32[50,4,16,256]{3,2,1,0:T(8,128)S(1)}, f32[50,4,16,256]{3,2,1,0:T(8,128)}, u32[]{:S(2)}) copy-start(f32[50,4,16,256]{3,2,1,0:T(8,128)} %x3_ref.1) | copy-start | bytes 9830404
  4.1 17.6 %copy-start.3 = (f32[2,16,256]{2,1,0:T(8,128)S(1)}, f32[2,16,256]{2,1,0:T(8,128)}, u32[]{:S(2)}) copy-start(f32[2,16,256]{2,1,0:T(8,128)} %cur_ref.5) | copy-start | bytes 98308
  4.1 17.6 %copy-start.5 = (s32[16,256]{1,0:T(8,128)S(1)}, s32[16,256]{1,0:T(8,128)}, u32[]{:S(2)}) copy-start(s32[16,256]{1,0:T(8,128)} %land_ref.5) | copy-start | bytes 49156
  5.6 14.2 %collective-permute-start = (f32[2,208,256]{2,1,0:T(8,128)}, f32[2,208,256]{2,1,0:T(8,128)}, u32[]{:S(2)}, u32[]{:S(2)}) collective-permute-start(f32[2,208,256]{2,1,0:T(8,128)} %get-tuple-element.11.ownup_ref), channel_id=1, source_target_pairs={{0,8},{8,16},{16,24},{24,32},{32,40},{40,48},{48,56},{56,64},{64,7... | collective-permute-start | bytes 1277960 | tf_op jit(solution)/shard_map/ppermute | solution.py:479
  7.5 14.0 %collective-permute-start.1 = (f32[2,208,256]{2,1,0:T(8,128)}, f32[2,208,256]{2,1,0:T(8,128)}, u32[]{:S(2)}, u32[]{:S(2)}) collective-permute-start(f32[2,208,256]{2,1,0:T(8,128)} %get-tuple-element.12.owndn_ref), channel_id=1, source_target_pairs={{8,0},{16,8},{24,16},{32,24},{40,32},{48,40},{56,48},{64,56},{72,6... | collective-permute-start | bytes 1277960 | tf_op jit(solution)/shard_map/ppermute | solution.py:480
  34.3 22.3 %collective-permute-start.6 = (f32[2,256]{1,0:T(2,128)S(1)}, f32[2,256]{1,0:T(2,128)S(1)}, u32[]{:S(2)}, u32[]{:S(2)}) collective-permute-start(f32[2,256]{1,0:T(2,128)S(1)} %get-tuple-element.22), channel_id=1, source_target_pairs={{0,8},{8,16},{16,24},{24,32},{32,40},{40,48},{48,56},{56,64},{64,7... | collective-permute-start | bytes 6152 | tf_op jit(solution)/shard_map/ppermute | solution.py:547
  36.3 20.4 %collective-permute-start.7 = (f32[2,256]{1,0:T(2,128)S(1)}, f32[2,256]{1,0:T(2,128)S(1)}, u32[]{:S(2)}, u32[]{:S(2)}) collective-permute-start(f32[2,256]{1,0:T(2,128)S(1)} %get-tuple-element.23), channel_id=1, source_target_pairs={{8,0},{16,8},{24,16},{32,24},{40,32},{48,40},{56,48},{64,56},{72,6... | collective-permute-start | bytes 6152 | tf_op jit(solution)/shard_map/ppermute | solution.py:548
  52.4 23.3 %collective-permute-start.2 = (f32[25,24,256]{2,1,0:T(8,128)S(1)}, f32[25,24,256]{2,1,0:T(8,128)S(1)}, u32[]{:S(2)}, u32[]{:S(2)}) collective-permute-start(f32[25,24,256]{2,1,0:T(8,128)S(1)} %get-tuple-element.14), channel_id=1, source_target_pairs={{0,1},{1,2},{2,3},{3,4},{4,5},{5,6},{6,7},{7,0},{8,9},{9,10},{10,1... | collective-permute-start | bytes 1843208 | tf_op jit(solution)/shard_map/ppermute | solution.py:500
  54.0 21.6 %collective-permute-start.3 = (f32[25,24,256]{2,1,0:T(8,128)S(1)}, f32[25,24,256]{2,1,0:T(8,128)S(1)}, u32[]{:S(2)}, u32[]{:S(2)}) collective-permute-start(f32[25,24,256]{2,1,0:T(8,128)S(1)} %get-tuple-element.15), channel_id=1, source_target_pairs={{1,0},{2,1},{3,2},{4,3},{5,4},{6,5},{7,6},{0,7},{9,8},{10,9},{11,1... | collective-permute-start | bytes 1843208 | tf_op jit(solution)/shard_map/ppermute | solution.py:501
  56.7 9.8 %collective-permute-start.8 = (f32[2,16,256]{2,1,0:T(8,128)S(1)}, f32[2,16,256]{2,1,0:T(8,128)S(1)}, u32[]{:S(2)}, u32[]{:S(2)}) collective-permute-start(f32[2,16,256]{2,1,0:T(8,128)S(1)} %pad_maximum_fusion), channel_id=1, source_target_pairs={{0,4},{1,5},{2,6},{3,7},{4,0},{5,1},{6,2},{7,3},{8,12},{9,13},{10,... | collective-permute-start | bytes 98312 | tf_op jit(solution)/shard_map/ppermute | solution.py:555
  66.5 4.3 %collective-permute-start.11 = (f32[2,16,256]{2,1,0:T(8,128)S(1)}, f32[2,16,256]{2,1,0:T(8,128)S(1)}, u32[]{:S(2)}, u32[]{:S(2)}) collective-permute-start(f32[2,16,256]{2,1,0:T(8,128)S(1)} %fusion), channel_id=1, source_target_pairs={{0,3},{1,0},{2,1},{3,2},{4,7},{5,4},{6,5},{7,6},{8,11},{9,8},{10,9... | collective-permute-start | bytes 98312 | tf_op jit(solution)/shard_map/ppermute | solution.py:557
  66.7 6.8 %collective-permute-start.10 = (f32[2,16,256]{2,1,0:T(8,128)S(1)}, f32[2,16,256]{2,1,0:T(8,128)S(1)}, u32[]{:S(2)}, u32[]{:S(2)}) collective-permute-start(f32[2,16,256]{2,1,0:T(8,128)S(1)} %fusion), channel_id=1, source_target_pairs={{0,1},{1,2},{2,3},{3,0},{4,5},{5,6},{6,7},{7,4},{8,9},{9,10},{10,1... | collective-permute-start | bytes 98312 | tf_op jit(solution)/shard_map/ppermute | solution.py:557
  68.6 6.4 %collective-permute-start.9 = (f32[2,16,256]{2,1,0:T(8,128)S(1)}, f32[2,16,256]{2,1,0:T(8,128)S(1)}, u32[]{:S(2)}, u32[]{:S(2)}) collective-permute-start(f32[2,16,256]{2,1,0:T(8,128)S(1)} %fusion), channel_id=1, source_target_pairs={{0,2},{1,3},{2,0},{3,1},{4,6},{5,7},{6,4},{7,5},{8,10},{9,11},{10,... | collective-permute-start | bytes 98312 | tf_op jit(solution)/shard_map/ppermute | solution.py:557
  70.9 7.9 %collective-permute-start.4 = (f32[25,8,256]{2,1,0:T(8,128)S(1)}, f32[25,8,256]{2,1,0:T(8,128)S(1)}, u32[]{:S(2)}, u32[]{:S(2)}) collective-permute-start(f32[25,8,256]{2,1,0:T(8,128)S(1)} %get-tuple-element.16), channel_id=1, source_target_pairs={{0,1},{1,2},{2,3},{3,4},{4,5},{5,6},{6,7},{7,0},{8,9},{9,10},{10,1... | collective-permute-start | bytes 614408 | tf_op jit(solution)/shard_map/ppermute | solution.py:549
  73.4 5.8 %collective-permute-start.5 = (f32[25,8,256]{2,1,0:T(8,128)S(1)}, f32[25,8,256]{2,1,0:T(8,128)S(1)}, u32[]{:S(2)}, u32[]{:S(2)}) collective-permute-start(f32[25,8,256]{2,1,0:T(8,128)S(1)} %get-tuple-element.17), channel_id=1, source_target_pairs={{1,0},{2,1},{3,2},{4,3},{5,4},{6,5},{7,6},{0,7},{9,8},{10,9},{11,1... | collective-permute-start | bytes 614408 | tf_op jit(solution)/shard_map/ppermute | solution.py:550

commit v2 on v1

v2 whole, which is shorter than its diff:
```python
import math
import functools

import numpy as np
import jax
import jax.numpy as jnp
from jax import lax
from jax.sharding import PartitionSpec as P
from jax.experimental import pallas as pl
from jax.experimental.pallas import tpu as pltpu


F32 = jnp.float32
LANES = 128
SUB = 8


def iota_masks():
    s = lax.broadcasted_iota(jnp.int32, (SUB, LANES), 0)
    l = lax.broadcasted_iota(jnp.int32, (SUB, LANES), 1)
    return s, l


def roll(x, shift, axis):
    return pltpu.roll(x, shift, axis)


class Grid:
    def __init__(self):
        s, l = iota_masks()
        self.s = s
        self.first_row = s == 0
        self.last_row = s == SUB - 1
        self.first_col = l == 0
        self.last_col = l == LANES - 1

    def below(self, t, hi):
        n, m = len(t), len(t[0])
        moved = [[roll(t[r][c], SUB - 1, 0) for c in range(m)] for r in range(n)]
        return [
            [
                jnp.where(self.last_row, moved[r + 1][c] if r + 1 < n else hi[c], moved[r][c])
                for c in range(m)
            ]
            for r in range(n)
        ]

    def above(self, t, lo):
        n, m = len(t), len(t[0])
        moved = [[roll(t[r][c], 1, 0) for c in range(m)] for r in range(n)]
        return [
            [
                jnp.where(self.first_row, moved[r - 1][c] if r > 0 else lo[c], moved[r][c])
                for c in range(m)
            ]
            for r in range(n)
        ]

    def right(self, row):
        m = len(row)
        moved = [roll(v, LANES - 1, 1) for v in row]
        return [
            jnp.where(self.last_col, moved[c + 1] if c + 1 < m else 0.0, moved[c]) for c in range(m)
        ]

    def left(self, row, start):
        m = len(row)
        moved = [roll(v, 1, 1) for v in row]
        return [
            jnp.where(self.first_col, moved[c - 1] if c > 0 else start, moved[c]) for c in range(m)
        ]


def face_flux(c, behind, in_front):
    return c * jnp.where(c > 0.0, behind, in_front)


def col_change(g, row, gs, vb, vl):
    right = g.right(row)
    flux = [face_flux(gs + vb[c], row[c], right[c]) for c in range(len(row))]
    edge = jnp.minimum(gs + vl, 0.0) * row[0]
    left = g.left(flux, edge)
    return [flux[c] - left[c] for c in range(len(row))]


def advance(g, t, gc, gs, ub, vb, vl, land, start, hi):
    n, m = len(t), len(t[0])
    ahead = g.below(t, hi)
    flux = [[face_flux(gc + ub[r][c], t[r][c], ahead[r][c]) for c in range(m)] for r in range(n)]
    before = g.above(flux, start)
    out = []
    for r in range(n):
        dy = col_change(g, t[r], gs, vb[r], vl[r])
        out.append(
            [land[r][c] * (t[r][c] - ((flux[r][c] - before[r][c]) + dy[c])) for c in range(m)]
        )
    return out


def tiles(ref, *lead):
    rows, cols = ref.shape[-2] // SUB, ref.shape[-1] // LANES
    return [
        [ref[(*lead, pl.ds(r * SUB, SUB), pl.ds(c * LANES, LANES))] for c in range(cols)]
        for r in range(rows)
    ]


def put_tiles(ref, t, *lead):
    for r, row in enumerate(t):
        for c, v in enumerate(row):
            ref[(*lead, pl.ds(r * SUB, SUB), pl.ds(c * LANES, LANES))] = v


def spread_row(ref, cols, *index):
    *lead, row = index
    return [
        jnp.broadcast_to(ref[(*lead, pl.ds(row, 1), pl.ds(c * LANES, LANES))], (SUB, LANES))
        for c in range(cols)
    ]


def turning(shears, sine, cosine, total_dirs):
    ux, uy, vx, vy = shears
    scale = total_dirs / (2.0 * math.pi)
    return [
        [
            scale
            * (
                sine * cosine * (ux[r][c] - vy[r][c])
                + sine * sine * uy[r][c]
                - cosine * cosine * vx[r][c]
            )
            for c in range(len(ux[0]))
        ]
        for r in range(len(ux))
    ]


def half_sum(a, b):
    return [[0.5 * (x + y) for x, y in zip(p, q)] for p, q in zip(a, b)]


def half_diff(a, b):
    return [[0.5 * (x - y) for x, y in zip(p, q)] for p, q in zip(a, b)]


def shears_of(g, u, v, u_lo, u_hi, v_lo, v_hi):
    ux = half_diff(g.below(u, u_hi), g.above(u, u_lo))
    vx = half_diff(g.below(v, v_hi), g.above(v, v_lo))
    uy = half_diff([g.right(r) for r in u], [g.left(r, 0.0) for r in u])
    vy = half_diff([g.right(r) for r in v], [g.left(r, 0.0) for r in v])
    return ux, uy, vx, vy


COS, SIN, FCOS, FSIN = 0, 6, 12, 17
TABLE = 22


def angle_table(sectors, per):
    total = sectors * per
    step = 2.0 * math.pi / total
    out = np.zeros((sectors, TABLE), np.float64)
    for k in range(sectors):
        d = np.arange(-1, per + 1) + k * per
        out[k, COS : COS + per + 2] = np.cos(d * step)
        out[k, SIN : SIN + per + 2] = np.sin(d * step)
        face = (np.arange(per + 1) + k * per - 0.5) * step
        out[k, FCOS : FCOS + per + 1] = np.cos(face)
        out[k, FSIN : FSIN + per + 1] = np.sin(face)
    return out.astype(np.float32)


HALO = 3


def rows_kernel(x_ref, fld_ref, up_ref, dn_ref):
    last = up_ref.shape[1] - SUB
    sides = ((up_ref, range(16 - HALO, 16)), (dn_ref, range(HALO)))
    for ref, rows in sides:
        for k, row in enumerate(rows):
            ref[k, pl.ds(last, SUB), :] = jnp.zeros((SUB, 2 * LANES), F32)
            for n in range(3):
                ref[k, pl.ds(last + n, 1), :] = fld_ref[n, pl.ds(row, 1), :]

    def one(q, _):
        at = pl.multiple_of(q * SUB, SUB)
        for ref, rows in sides:
            for k, row in enumerate(rows):
                for c in range(2):
                    start = at * 32 + (row // SUB * 2 + c) * SUB + row % SUB
                    v = x_ref[pl.ds(start, SUB, stride=32), :]
                    land = spread_row(fld_ref, 2, 2, row)[c]
                    ref[k, pl.ds(at, SUB), pl.ds(c * LANES, LANES)] = v * land
        return 0

    lax.fori_loop(0, last // SUB, one, 0)


def pack_inner(g, a, b):
    low2 = g.s < 6
    first = jnp.where(low2, roll(a[0], 6, 0), roll(a[1], 6, 0))
    mid = jnp.where(g.s < 4, roll(a[1], 6, 0), roll(b[0], 2, 0))
    last = jnp.where(g.s < 2, roll(b[0], 2, 0), roll(b[1], 2, 0))
    return first, mid, last


def pack_outer(g, a, b):
    one = jnp.where(g.s < 2, a[0], roll(a[1], 4, 0))
    two = jnp.where(g.s < 6, roll(b[0], 4, 0), b[1])
    return jnp.where(g.s < 4, one, two)


def unpack(g, inner, outer):
    a, b, c = inner
    a2, b2, b6, c6, o4 = roll(a, 2, 0), roll(b, 2, 0), roll(b, 6, 0), roll(c, 6, 0), roll(outer, 4, 0)
    low2, low6 = g.s < 2, g.s < 6
    one = [jnp.where(low2, outer, a2), jnp.where(low2, a2, jnp.where(low6, b2, o4))]
    two = [jnp.where(low2, o4, jnp.where(low6, b6, c6)), jnp.where(low6, c6, outer)]
    return one, two


def ends_kernel(total, sec_ref, tab_ref, cg_ref, x_ref, cur_ref,
                prev_ref, next_ref, ub_s, vb_s, k_s):
    g = Grid()
    sec = sec_ref[0]
    freqs = x_ref.shape[0]
    zero = [jnp.zeros((SUB, LANES), F32)] * 2

    u, v = tiles(cur_ref, 0), tiles(cur_ref, 1)
    put_tiles(ub_s, half_sum(u, g.below(u, zero)))
    put_tiles(vb_s, half_sum(v, [g.right(r) for r in v]))
    sh = shears_of(g, u, v, zero, zero, zero, zero)
    for n, f in ((0, 0), (1, 4)):
        put_tiles(k_s, turning(sh, tab_ref[sec, FSIN + f], tab_ref[sec, FCOS + f], total), n)

    def one(pair, _):
        for n, (out_ref, d) in enumerate(((prev_ref, 0), (next_ref, 3))):
            ends = []
            for h in range(2):
                f = pair * 2 + h
                cg = cg_ref[f]
                gc, gs = cg * tab_ref[sec, COS + 1 + d], cg * tab_ref[sec, SIN + 1 + d]
                ub, vb = tiles(ub_s), tiles(vb_s)
                vl = [0.5 * cur_ref[1, pl.ds(r * SUB, SUB), pl.ds(0, LANES)] for r in range(2)]
                land = tiles(cur_ref, 2)
                t = tiles(x_ref, f, d)
                t = [[land[r][c] * t[r][c] for c in range(2)] for r in range(2)]
                for _ in range(2):
                    t = advance(g, t, gc, gs, ub, vb, vl, land, zero, zero)
                k = tiles(k_s, n)
                limit = jnp.minimum if d == 0 else jnp.maximum
                ends.append([[limit(k[r][c], 0.0) * t[r][c] for c in range(2)] for r in range(2)])
            for c in range(2):
                got = pack_inner(g, [ends[0][r][c] for r in range(2)], [ends[1][r][c] for r in range(2)])
                for q in range(3):
                    out_ref[pair, pl.ds(q * SUB, SUB), pl.ds(c * LANES, LANES)] = got[q]
        return 0

    lax.fori_loop(0, freqs // 2, one, 0)


FACE, VROW, VLEFT, LAND, SIDE = 0, 4, 7, 10, 13


def column_rows(g, rows, field, gc, gs):
    m = range(2)
    flux = [
        [face_flux(gc + field(FACE + i)[c], rows[i][c], rows[i + 1][c]) for c in m] for i in range(4)
    ]
    once = []
    for i in range(3):
        dy = col_change(g, rows[i + 1], gs, field(VROW + i), field(VLEFT + i)[0])
        land = field(LAND + i)
        once.append([land[c] * (rows[i + 1][c] - ((flux[i + 1][c] - flux[i][c]) + dy[c])) for c in m])
    again = [
        [face_flux(gc + field(FACE + 1 + i)[c], once[i][c], once[i + 1][c]) for c in m] for i in range(2)
    ]
    dy = col_change(g, once[1], gs, field(VROW + 1), field(VLEFT + 1)[0])
    land = field(LAND + 1)
    twice = [land[c] * (once[1][c] - ((again[1][c] - again[0][c]) + dy[c])) for c in m]
    return flux, again, once, twice


def stress_of(co, k, r, b, n, dirs):
    acc = -0.5 * b if n != 1 else jnp.zeros((SUB, LANES), F32)
    for d in range(dirs):
        q = (
            co[d + 1]
            + jnp.maximum(k[d + 1], 0.0) * (co[d + 2] - co[d + 1])
            + jnp.minimum(k[d], 0.0) * (co[d + 1] - co[d])
        )
        acc = acc + q * r[d]
    return acc


def main_kernel(total, sec_ref, tab_ref, cg_ref, ratio_ref, weight_ref,
                x_ref, cur_ref, top_ref, bot_ref, ownup_ref, owndn_ref,
                part_ref, e0_ref, e3_ref, prev_ref, next_ref, force_ref,
                new_ref, sem, ub_s, vb_s, k_s, fld_s, ke_s, st_s, r_s, b_s, re_s, be_s):
    g = Grid()
    chunks = sem.shape[0]
    sec = sec_ref[0]
    freqs = x_ref.shape[0]
    dirs = x_ref.shape[1]

    last = freqs * dirs
    u, v = tiles(cur_ref, 0), tiles(cur_ref, 1)

    def beside_fields(n):
        above = [spread_row(top_ref, 2, q, last + n) for q in range(HALO)]
        below = [spread_row(bot_ref, 2, q, last + n) for q in range(HALO)]
        own = [spread_row(cur_ref, 2, n, q) for q in (0, 1, 14, 15)]
        return above + own[:2], own[2:] + below

    us, vs, ls = (beside_fields(n) for n in range(3))
    put_tiles(ub_s, half_sum(u, g.below(u, us[1][2])))
    put_tiles(vb_s, half_sum(v, [g.right(r) for r in v]))
    for side in range(2):
        for q in range(4):
            put_tiles(fld_s, half_sum([us[side][q]], [us[side][q + 1]]), side, FACE + q)
        for q in range(3):
            vv = vs[side][q + 1]
            put_tiles(fld_s, half_sum([vv], [g.right(vv)]), side, VROW + q)
            put_tiles(fld_s, [[0.5 * w for w in vv]], side, VLEFT + q)
            put_tiles(fld_s, [ls[side][q + 1]], side, LAND + q)
        edge = (
            half_diff([us[side][3]], [us[side][1]]),
            half_diff([g.right(us[side][2])], [g.left(us[side][2], 0.0)]),
            half_diff([vs[side][3]], [vs[side][1]]),
            half_diff([g.right(vs[side][2])], [g.left(vs[side][2], 0.0)]),
        )
        for f in range(dirs + 1):
            k = turning(edge, tab_ref[sec, FSIN + f], tab_ref[sec, FCOS + f], total)
            put_tiles(ke_s, k, side, f)
    sh = shears_of(g, u, v, us[0][2], us[1][2], vs[0][2], vs[1][2])
    for f in range(dirs + 1):
        put_tiles(k_s, turning(sh, tab_ref[sec, FSIN + f], tab_ref[sec, FCOS + f], total), f)
    for ref in (r_s, b_s, re_s, be_s):
        ref[...] = jnp.zeros_like(ref)

    def by_direction(n):
        out = jnp.zeros((SUB, LANES), F32)
        for d in range(dirs):
            out = jnp.where(g.s % dirs == d, tab_ref[sec, n + 1 + d], out)
        return out

    cos_rows, sin_rows = by_direction(COS), by_direction(SIN)

    def beside_rows(q, _):
        at = pl.ds(pl.multiple_of(q * SUB, SUB), SUB)
        pair = lambda a, b: jnp.where(g.s < dirs, a, b)
        f = q * 2
        cg = pair(cg_ref[f], cg_ref[f + 1])
        gc, gs = cg * cos_rows, cg * sin_rows
        w = pair(weight_ref[f], weight_ref[f + 1])
        wr = w * pair(ratio_ref[f], ratio_ref[f + 1])
        row = lambda ref, n: [ref[n, at, pl.ds(c * LANES, LANES)] for c in range(2)]
        above = [row(top_ref, n) for n in range(HALO)]
        below = [row(bot_ref, n) for n in range(HALO)]
        for side, rows in (
            (0, above + [row(owndn_ref, 0), row(owndn_ref, 1)]),
            (1, [row(ownup_ref, 1), row(ownup_ref, 2)] + below),
        ):
            field = lambda n: [fld_s[side, n, :, pl.ds(c * LANES, LANES)] for c in range(2)]
            flux, again, once, twice = column_rows(g, rows, field, gc, gs)
            for c in range(2):
                cc = pl.ds(c * LANES, LANES)
                if side == 0:
                    st_s[0, at, cc] = flux[2][c]
                    st_s[1, at, cc] = again[1][c]
                else:
                    st_s[2, at, cc] = once[1][c]
                re_s[side, :, cc] += wr * twice[c]
                be_s[side, :, cc] += w * twice[c]
        return 0

    lax.fori_loop(0, freqs * dirs // SUB, beside_rows, 0)

    def one(pair, _):
        outs = [[], []]
        group = pl.ds(pl.multiple_of(pair * SUB, SUB), SUB)

        def beside(ref, n, *lead):
            return [
                jnp.broadcast_to(ref[(*lead, group, pl.ds(c * LANES, LANES))][n : n + 1], (SUB, LANES))
                for c in range(2)
            ]

        for h in range(2):
            f = pair * 2 + h
            cg = cg_ref[f]
            w = weight_ref[f]
            wr = w * ratio_ref[f]
            a2 = []
            for d in range(dirs):
                gc, gs = cg * tab_ref[sec, COS + 1 + d], cg * tab_ref[sec, SIN + 1 + d]
                ub, vb = tiles(ub_s), tiles(vb_s)
                vl = [0.5 * cur_ref[1, pl.ds(r * SUB, SUB), pl.ds(0, LANES)] for r in range(2)]
                land = tiles(cur_ref, 2)
                t = tiles(x_ref, f, d)
                t = [[land[r][c] * t[r][c] for c in range(2)] for r in range(2)]
                n = h * dirs + d
                t = advance(g, t, gc, gs, ub, vb, vl, land, beside(st_s, n, 0), beside(bot_ref, n, 0))
                t = advance(g, t, gc, gs, ub, vb, vl, land, beside(st_s, n, 1), beside(st_s, n, 2))
                a2.append(t)
            for r in range(2):
                for c in range(2):
                    here = (pl.ds(r * SUB, SUB), pl.ds(c * LANES, LANES))
                    v = [a2[d][r][c] for d in range(dirs)]
                    for d in range(dirs):
                        r_s[(d, *here)] += wr * v[d]
                    b_s[here] += w * ((v[0] + v[1]) + (v[2] + v[3]))
                    k = [k_s[(n, *here)] for n in range(dirs + 1)]
                    inside = [face_flux(k[d + 1], v[d], v[d + 1]) for d in range(dirs - 1)]
                    new_ref[(f, 0, *here)] = v[1] - (inside[1] - inside[0])
                    new_ref[(f, 1, *here)] = v[2] - (inside[2] - inside[1])
                    e0_ref[(f, *here)] = v[0] - (inside[0] - jnp.minimum(k[0], 0.0) * v[0])
                    e3_ref[(f, *here)] = v[3] - (jnp.maximum(k[4], 0.0) * v[3] - inside[2])
            k0, k4 = tiles(k_s, 0), tiles(k_s, dirs)
            outs[0].append([[jnp.minimum(k0[r][c], 0.0) * a2[0][r][c] for c in range(2)] for r in range(2)])
            outs[1].append([[jnp.maximum(k4[r][c], 0.0) * a2[3][r][c] for c in range(2)] for r in range(2)])
        for ref, ends in ((prev_ref, outs[0]), (next_ref, outs[1])):
            for c in range(2):
                ref[pair, :, pl.ds(c * LANES, LANES)] = pack_outer(
                    g, [ends[0][r][c] for r in range(2)], [ends[1][r][c] for r in range(2)]
                )
        return 0

    per = freqs // chunks

    def put(q):
        span = pl.ds(q * per, per)
        return pltpu.make_async_copy(
            new_ref.at[span], part_ref.at[span, pl.ds(1, dirs - 2)], sem.at[q]
        )

    def chunk(q, _):
        lax.fori_loop(q * (per // 2), (q + 1) * (per // 2), one, 0)
        put(q).start()
        return 0

    lax.fori_loop(0, chunks, chunk, 0)
    cs = [tab_ref[sec, COS + n] for n in range(dirs + 2)]
    sn = [tab_ref[sec, SIN + n] for n in range(dirs + 2)]
    coef = (
        [1.0 + a * a for a in cs],
        [a * b for a, b in zip(sn, cs)],
        [1.0 + b * b for b in sn],
    )
    stress, edges = [], []
    for n, co in enumerate(coef):
        now = []
        for r in range(2):
            now.append([])
            for c in range(2):
                here = (pl.ds(r * SUB, SUB), pl.ds(c * LANES, LANES))
                k = [k_s[(m, *here)] for m in range(dirs + 1)]
                now[r].append(
                    stress_of(co, k, [r_s[(d, *here)] for d in range(dirs)], b_s[here], n, dirs)
                )
        stress.append(now)
        both = []
        for side in range(2):
            both.append([])
            for c in range(2):
                cc = pl.ds(c * LANES, LANES)
                rr, bb = re_s[side, :, cc], be_s[side, :, cc]
                spread = lambda v: jnp.broadcast_to(v, (SUB, LANES))
                k = [ke_s[side, m, :, cc] for m in range(dirs + 1)]
                rd = [spread(rr[d : d + 1] + rr[d + dirs : d + dirs + 1]) for d in range(dirs)]
                both[side].append(
                    stress_of(co, k, rd, spread(jnp.sum(bb, axis=0, keepdims=True)), n, dirs)
                )
        edges.append(both)
    xx, xy, yy = stress
    dx = lambda t, e: half_diff(g.below(t, e[1]), g.above(t, e[0]))
    dy = lambda t: half_diff([g.right(r) for r in t], [g.left(r, 0.0) for r in t])
    for n, (p, q) in enumerate(((dx(xx, edges[0]), dy(xy)), (dx(xy, edges[1]), dy(yy)))):
        put_tiles(force_ref, [[-(p[r][c] + q[r][c]) for c in range(2)] for r in range(2)], n)

    def done(q, _):
        put(q).wait()
        return 0

    lax.fori_loop(0, chunks, done, 0)


def join_kernel(e0_ref, e3_ref, inp_ref, inn_ref, outp_ref, outn_ref, part_ref, o_ref, buf, sem):
    g = Grid()
    pairs = inp_ref.shape[0]
    dirs = o_ref.shape[1]
    parts = 5
    step = pairs // parts

    def put(q, n, d):
        span = pl.ds(q * step * 2, step * 2)
        return pltpu.make_async_copy(buf.at[n, span], o_ref.at[span, d], sem.at[q, n])

    for q in range(parts):
        for n, (e_ref, inner_ref, outer_ref, sign, d) in enumerate(
            ((e0_ref, inp_ref, outp_ref, 1.0, 0), (e3_ref, inn_ref, outn_ref, -1.0, dirs - 1))
        ):
            def one(pair, _):
                for c in range(2):
                    cc = pl.ds(c * LANES, LANES)
                    inner = [inner_ref[pair, pl.ds(k * SUB, SUB), cc] for k in range(3)]
                    both = unpack(g, inner, outer_ref[pair, :, cc])
                    for h in range(2):
                        for r in range(2):
                            at = (pair * 2 + h, pl.ds(r * SUB, SUB), cc)
                            buf[(n, *at)] = e_ref[at] + sign * both[h][r]
                return 0

            lax.fori_loop(q * step, (q + 1) * step, one, 0)
            put(q, n, d).start()
    for q in range(parts):
        put(q, 0, 0).wait()
        put(q, 1, dirs - 1).wait()


def per_device(sectors, points, action, currents, land_mask, group_speed, group_ratio, bin_weight):
    freqs, dirs, rows, cols = action.shape
    total = dirs * sectors
    table = jnp.asarray(angle_table(sectors, dirs))
    sec = lax.axis_index("dir").reshape(1).astype(jnp.int32)
    smem = pl.BlockSpec(memory_space=pltpu.SMEM)
    combos = freqs * dirs
    f32 = lambda *s: jax.ShapeDtypeStruct(s, F32)

    def send(value, axis, pairs):
        return lax.ppermute(value, axis, pairs)

    vmem = lambda *s: pltpu.VMEM(s, F32)
    params = lambda: pltpu.CompilerParams(vmem_limit_bytes=24 * 2**20)

    fields = jnp.concatenate([currents, land_mask.astype(F32)[None]])
    flat = action.reshape(combos, rows // SUB, SUB, cols // LANES, LANES)
    flat = flat.transpose(0, 1, 3, 2, 4).reshape(combos * rows * cols // LANES, LANES)
    vm = pl.BlockSpec(memory_space=pltpu.VMEM)
    hbm = pl.BlockSpec(memory_space=pl.ANY)
    up_rows, dn_rows = pl.pallas_call(
        rows_kernel,
        in_specs=[vm, vm],
        out_specs=[vm, vm],
        out_shape=[f32(HALO, combos + SUB, cols)] * 2,
        compiler_params=params(),
        name="boundary_rows",
    )(flat, fields)
    up = [(i, i + 1) for i in range(points - 1)]
    down = [(j, i) for i, j in up]
    top = send(up_rows, "pts", up)
    bot = send(dn_rows, "pts", down)

    in_prev, in_next = pl.pallas_call(
        functools.partial(ends_kernel, total),
        in_specs=[smem, smem, smem, vm, vm],
        out_specs=[vm, vm],
        out_shape=[f32(freqs // 2, 24, cols)] * 2,
        scratch_shapes=[vmem(rows, cols), vmem(rows, cols), vmem(2, rows, cols)],
        compiler_params=params(),
        name="sector_ends",
    )(sec, table, group_speed, action, fields)
    fwd = [(i, (i + 1) % sectors) for i in range(sectors)]
    back = [(j, i) for i, j in fwd]
    inner_from_prev = send(in_next, "dir", fwd)
    inner_from_next = send(in_prev, "dir", back)

    part, e0, e3, out_prev, out_next, force = pl.pallas_call(
        functools.partial(main_kernel, total),
        in_specs=[smem] * 5 + [vm] * 6,
        out_specs=[hbm, vm, vm, vm, vm, vm],
        out_shape=[
            f32(freqs, dirs, rows, cols),
            f32(freqs, rows, cols),
            f32(freqs, rows, cols),
            f32(freqs // 2, SUB, cols),
            f32(freqs // 2, SUB, cols),
            f32(2, rows, cols),
        ],
        scratch_shapes=[
            vmem(freqs, dirs - 2, rows, cols), pltpu.SemaphoreType.DMA((5,)),
            vmem(rows, cols), vmem(rows, cols), vmem(dirs + 1, rows, cols),
            vmem(2, SIDE, SUB, cols), vmem(2, dirs + 1, SUB, cols), vmem(3, combos, cols),
            vmem(dirs, rows, cols), vmem(rows, cols), vmem(2, SUB, cols), vmem(2, SUB, cols),
        ],
        compiler_params=params(),
        name="transport",
    )(sec, table, group_speed, group_ratio, bin_weight, action, fields,
      top, bot, up_rows, dn_rows)

    outer_from_prev = send(out_next, "dir", fwd)
    outer_from_next = send(out_prev, "dir", back)
    half = sectors // 2
    force = force + send(force, "dir", [(i, (i + half) % sectors) for i in range(sectors)])
    near = [
        send(force, "dir",
             [(i, i // half * half + (i % half + s) % half) for i in range(sectors)])
        for s in range(1, half)
    ]
    force = (force + near[1]) + (near[0] + near[2])

    new_action = pl.pallas_call(
        join_kernel,
        in_specs=[vm] * 6 + [hbm],
        out_specs=hbm,
        out_shape=f32(freqs, dirs, rows, cols),
        input_output_aliases={6: 0},
        scratch_shapes=[vmem(2, freqs, rows, cols), pltpu.SemaphoreType.DMA((5, 2))],
        compiler_params=params(),
        name="join_sectors",
    )(e0, e3, inner_from_prev, inner_from_next, outer_from_prev, outer_from_next, part)
    return new_action, force


def solution(mesh):
    in_specs = (P(None, "dir", "pts", None), P(None, "pts", None), P("pts", None), P(), P(), P())
    out_specs = (P(None, "dir", "pts", None), P(None, "pts", None))

    def body(*args):
        return per_device(mesh.shape["dir"], mesh.shape["pts"], *args)

    return jax.shard_map(body, mesh=mesh, in_specs=in_specs, out_specs=out_specs, check_vma=False)
```

time: 86.9 us -> 66.3 us (0.76)
  waiting for transfers between devices: 23.2 us -> 8.76 us
  starting transfers between devices: 27.7 us -> 20.9 us
  local copies, waits for them, and re-layouts: 3.94 us -> 1.95 us
  other arithmetic: 0.73 us -> 2.13 us
  Pallas kernels: 29.3 us -> 30.7 us
    ppermute x12 -> x10, waiting for transfers between devices: 23.2 us -> 8.76 us  [send(): return lax.ppermute(value, axis, pairs)]
    ppermute x12 -> x10, starting transfers between devices: 27.7 us -> 20.9 us  [send(): return lax.ppermute(value, axis, pairs)]
    unnamed x20 -> x12, local copies, waits for them, and re-layouts: 3.44 us -> 1.95 us
    pallas_call x4, Pallas kernels: 29.3 us -> 30.7 us  [the longest x1 19.1 us: per_device(): pl.pallas_call(functools.partial(main_kernel, total), in_specs=[smem] * 5...]
  transfers between devices with their start and end apart: 12 -> 10, of which waited for: 7 -> 4; matrix products, arithmetic and copies ran while one was open for 1% -> 1% of each run, Pallas kernels for 10% -> 42%
where the time goes in v2:
time: 66.3 us; the launch traced here: 65.2 us
  Pallas kernels  30.7 us (46%)
  starting transfers between devices  20.9 us (32%)
  waiting for transfers between devices  8.76 us (13%)
  other arithmetic  2.13 us (3%)
  local copies, waits for them, and re-layouts  1.95 us (3%)
  between operations  0.73 us (1%)
    ppermute x10, starting transfers between devices, send(): return lax.ppermute(value, axis, pairs)  20.9 us
    pallas_call x1, Pallas kernels, per_device(): pl.pallas_call(functools.partial(main_kernel, total), in_specs=[smem] * 5...  19.1 us
    ppermute x10, waiting for transfers between devices, send(): return lax.ppermute(value, axis, pairs)  8.76 us
    pallas_call x1, Pallas kernels, per_device(): pl.pallas_call(functools.partial(ends_kernel, total), in_specs=[smem, sme...  8.4 us
    unnamed x12, local copies, waits for them, and re-layouts  1.95 us
    pallas_call x1, Pallas kernels, per_device(): pl.pallas_call(rows_kernel, in_specs=[vm, vm], out_specs=[vm, vm], out_sh...  1.94 us
  transfers between devices with their start and end apart: 10, of which 4 were waited for; matrix products, arithmetic and copies ran while one was open for 1% of the time, Pallas kernels for 42%

profile of v2, /device:TPU:6, one launch (start us, length us, event | category | flops | bytes accessed | tf_op | source)
XLA Modules:
  0.0 65.2 jit_solution(7683859239957524757)
XLA Ops:
  0.6 0.0 copy-start.2
  0.7 0.7 %convert_bitcast_fusion = f32[1,16,256]{2,1,0:T(8,128)S(1)} fusion(s32[16,256]{1,0:T(8,128)} %param.9), kind=kLoop, calls=%fused_computation.2 | loop fusion | flops 4096 | bytes 32768 | tf_op jit(solution)/shard_map/broadcast_in_dim | solution.py:536
  1.4 0.8 %pad_maximum_fusion.fld_ref.cur_ref = f32[3,16,256]{2,1,0:T(8,128)S(1)} fusion(f32[1,16,256]{2,1,0:T(8,128)S(1)} %convert_bitcast_fusion, f32[2,16,256]{2,1,0:T(8,128)} %param.8), kind=kLoop, calls=%fused_computation | loop fusion | flops 12288 | bytes 98304 | tf_op jit(solution)/shard_map/concatenate | solution.py:536
  2.1 1.9 %copy-done = f32[50,4,16,256]{3,2,1,0:T(8,128)S(1)} copy-done((f32[50,4,16,256]{3,2,1,0:T(8,128)S(1)}, f32[50,4,16,256]{3,2,1,0:T(8,128)}, u32[]{:S(2)}) %copy-start) | copy-done | bytes 3276824
  4.1 1.9 %boundary_rows.1 = (f32[3,208,256]{2,1,0:T(8,128)}, f32[3,208,256]{2,1,0:T(8,128)}) custom-call(f32[6400,128]{1,0:T(8,128)S(1)} %bitcast.8, f32[3,16,256]{2,1,0:T(8,128)S(1)} %pad_maximum_fusion.fld_ref.cur_ref), custom_call_target="tpu_custom_call" | custom-call | tf_op jit(solution)/shard_map/boundary_rows/pallas_call | solution.py:541
  6.0 1.9 %collective-permute-start = (f32[3,208,256]{2,1,0:T(8,128)}, f32[3,208,256]{2,1,0:T(8,128)}, u32[]{:S(2)}, u32[]{:S(2)}) collective-permute-start(f32[3,208,256]{2,1,0:T(8,128)} %get-tuple-element.12.ownup_ref), channel_id=1, source_target_pairs={{0,8},{8,16},{16,24},{24,32},{32,40},{40,48},{48,56},{56,64},{64,7... | collective-permute-start | bytes 1916936 | tf_op jit(solution)/shard_map/ppermute | solution.py:531
  7.9 8.0 %collective-permute-start.1 = (f32[3,208,256]{2,1,0:T(8,128)}, f32[3,208,256]{2,1,0:T(8,128)}, u32[]{:S(2)}, u32[]{:S(2)}) collective-permute-start(f32[3,208,256]{2,1,0:T(8,128)} %get-tuple-element.13.owndn_ref), channel_id=1, source_target_pairs={{8,0},{16,8},{24,16},{32,24},{40,32},{48,40},{56,48},{64,56},{72,6... | collective-permute-start | bytes 1916936 | tf_op jit(solution)/shard_map/ppermute | solution.py:531
  16.0 8.4 %sector_ends.1 = (f32[25,24,256]{2,1,0:T(8,128)S(1)}, f32[25,24,256]{2,1,0:T(8,128)S(1)}) custom-call(s32[1]{0:T(128)} %bitcast.sec_ref, f32[8,22]{1,0:T(8,128)S(1)} %copy-done.2, f32[50]{0:T(128)S(1)} %copy-done.3, f32[50,4,16,256]{3,2,1,0:T(8,128)S(1)} %copy-done.1, f32[3,16,256]{2,1,0:T(8,128)S(1)} %pad_maximum_fusion.fld_ref.cur_ref), custom_call_target="tpu_custom_call" | custom-call | tf_op jit(solution)/shard_map/sector_ends/pallas_call | solution.py:554
  24.4 1.7 %collective-permute-start.2 = (f32[25,24,256]{2,1,0:T(8,128)S(1)}, f32[25,24,256]{2,1,0:T(8,128)S(1)}, u32[]{:S(2)}, u32[]{:S(2)}) collective-permute-start(f32[25,24,256]{2,1,0:T(8,128)S(1)} %get-tuple-element.16), channel_id=1, source_target_pairs={{0,1},{1,2},{2,3},{3,4},{4,5},{5,6},{6,7},{7,0},{8,9},{9,10},{10,1... | collective-permute-start | bytes 1843208 | tf_op jit(solution)/shard_map/ppermute | solution.py:531
  26.1 2.6 %collective-permute-start.3 = (f32[25,24,256]{2,1,0:T(8,128)S(1)}, f32[25,24,256]{2,1,0:T(8,128)S(1)}, u32[]{:S(2)}, u32[]{:S(2)}) collective-permute-start(f32[25,24,256]{2,1,0:T(8,128)S(1)} %get-tuple-element.17), channel_id=1, source_target_pairs={{1,0},{2,1},{3,2},{4,3},{5,4},{6,5},{7,6},{0,7},{9,8},{10,9},{11,1... | collective-permute-start | bytes 1843208 | tf_op jit(solution)/shard_map/ppermute | solution.py:531
  28.6 0.0 collective-permute-done.1.bot_ref
  28.7 19.1 %transport.1 = (f32[50,4,16,256]{3,2,1,0:T(8,128)}, f32[50,16,256]{2,1,0:T(8,128)S(1)}, f32[50,16,256]{2,1,0:T(8,128)S(1)}, f32[25,8,256]{2,1,0:T(8,128)S(1)}, f...) custom-call(s32[1]{0:T(128)} %bitcast.sec_ref, f32[8,22]{1,0:T(8,128)S(1)} %copy-done.2, f32[50]{0:T(128)S(1)} %copy-done.3, ...), custom_call_target="tpu_custom_call" | custom-call | tf_op jit(solution)/shard_map/transport/pallas_call | solution.py:568
  47.7 0.5 collective-permute-start.6
  48.3 3.5 %collective-permute-done.6 = f32[2,16,256]{2,1,0:T(8,128)S(1)} collective-permute-done((f32[2,16,256]{2,1,0:T(8,128)S(1)}, f32[2,16,256]{2,1,0:T(8,128)S(1)}, u32[]{:S(2)}, u32[]{:S(2)}) %collective-permute-start.6) | collective-permute-done | bytes 32800 | tf_op jit(solution)/shard_map/ppermute | solution.py:531
  51.7 0.9 %collective-permute-start.9 = (f32[2,16,256]{2,1,0:T(8,128)S(1)}, f32[2,16,256]{2,1,0:T(8,128)S(1)}, u32[]{:S(2)}, u32[]{:S(2)}) collective-permute-start(f32[2,16,256]{2,1,0:T(8,128)S(1)} %add.12), channel_id=1, source_target_pairs={{0,3},{1,0},{2,1},{3,2},{4,7},{5,4},{6,5},{7,6},{8,11},{9,8},{10,9... | collective-permute-start | bytes 98312 | tf_op jit(solution)/shard_map/ppermute | solution.py:531
  52.7 1.1 %collective-permute-start.8 = (f32[2,16,256]{2,1,0:T(8,128)S(1)}, f32[2,16,256]{2,1,0:T(8,128)S(1)}, u32[]{:S(2)}, u32[]{:S(2)}) collective-permute-start(f32[2,16,256]{2,1,0:T(8,128)S(1)} %add.12), channel_id=1, source_target_pairs={{0,1},{1,2},{2,3},{3,0},{4,5},{5,6},{6,7},{7,4},{8,9},{9,10},{10,1... | collective-permute-start | bytes 98312 | tf_op jit(solution)/shard_map/ppermute | solution.py:531
  53.8 1.1 %collective-permute-start.7 = (f32[2,16,256]{2,1,0:T(8,128)S(1)}, f32[2,16,256]{2,1,0:T(8,128)S(1)}, u32[]{:S(2)}, u32[]{:S(2)}) collective-permute-start(f32[2,16,256]{2,1,0:T(8,128)S(1)} %add.12), channel_id=1, source_target_pairs={{0,2},{1,3},{2,0},{3,1},{4,6},{5,7},{6,4},{7,5},{8,10},{9,11},{10,... | collective-permute-start | bytes 98312 | tf_op jit(solution)/shard_map/ppermute | solution.py:531
  54.9 1.1 %collective-permute-done.9 = f32[2,16,256]{2,1,0:T(8,128)S(1)} collective-permute-done((f32[2,16,256]{2,1,0:T(8,128)S(1)}, f32[2,16,256]{2,1,0:T(8,128)S(1)}, u32[]{:S(2)}, u32[]{:S(2)}) %collective-permute-start.9) | collective-permute-done | bytes 32800 | tf_op jit(solution)/shard_map/ppermute | solution.py:531
  56.0 0.7 %collective-permute-start.4 = (f32[25,8,256]{2,1,0:T(8,128)S(1)}, f32[25,8,256]{2,1,0:T(8,128)S(1)}, u32[]{:S(2)}, u32[]{:S(2)}) collective-permute-start(f32[25,8,256]{2,1,0:T(8,128)S(1)} %get-tuple-element.18), channel_id=1, source_target_pairs={{0,1},{1,2},{2,3},{3,4},{4,5},{5,6},{6,7},{7,0},{8,9},{9,10},{10,1... | collective-permute-start | bytes 614408 | tf_op jit(solution)/shard_map/ppermute | solution.py:531
  56.8 1.0 %collective-permute-done.8 = f32[2,16,256]{2,1,0:T(8,128)S(1)} collective-permute-done((f32[2,16,256]{2,1,0:T(8,128)S(1)}, f32[2,16,256]{2,1,0:T(8,128)S(1)}, u32[]{:S(2)}, u32[]{:S(2)}) %collective-permute-start.8) | collective-permute-done | bytes 32800 | tf_op jit(solution)/shard_map/ppermute | solution.py:531
  57.8 2.4 %collective-permute-start.5 = (f32[25,8,256]{2,1,0:T(8,128)S(1)}, f32[25,8,256]{2,1,0:T(8,128)S(1)}, u32[]{:S(2)}, u32[]{:S(2)}) collective-permute-start(f32[25,8,256]{2,1,0:T(8,128)S(1)} %get-tuple-element.19), channel_id=1, source_target_pairs={{1,0},{2,1},{3,2},{4,3},{5,4},{6,5},{7,6},{0,7},{9,8},{10,9},{11,1... | collective-permute-start | bytes 614408 | tf_op jit(solution)/shard_map/ppermute | solution.py:531
  60.2 0.6 add_add_fusion
  60.8 3.1 %collective-permute-done.4.outp_ref = f32[25,8,256]{2,1,0:T(8,128)S(1)} collective-permute-done((f32[25,8,256]{2,1,0:T(8,128)S(1)}, f32[25,8,256]{2,1,0:T(8,128)S(1)}, u32[]{:S(2)}, u32[]{:S(2)}) %collective-permute-start.4) | collective-permute-done | bytes 204832 | tf_op jit(solution)/shard_map/ppermute | solution.py:531
  63.9 1.3 %join_sectors.1 = f32[50,4,16,256]{3,2,1,0:T(8,128)} custom-call(f32[50,16,256]{2,1,0:T(8,128)S(1)} %get-tuple-element.14.e0_ref, f32[50,16,256]{2,1,0:T(8,128)S(1)} %get-tuple-element.15.e3_ref, f32[25,24,256]{2,1,0:T(8,128)S(1)} %collective-permute-done.2.inp_ref, ...), custom_call_target="tpu_custom_call", output_to_operand_aliasing={{}: (6, {})} | custom-call | tf_op jit(solution)/shard_map/join_sectors/pallas_call | solution.py:602
  (16 shorter events, 0.0 us)
Async XLA Ops:
  0.6 15.4 %copy-start.2 = (f32[8,22]{1,0:T(8,128)S(1)}, f32[8,22]{1,0:T(8,128)}, u32[]{:S(2)}) copy-start(f32[8,22]{1,0:T(8,128)} %constant.6.clone.tab_ref) | copy-start | bytes 2116
  0.6 15.4 %copy-start.3 = (f32[50]{0:T(128)S(1)}, f32[50]{0:T(128)}, u32[]{:S(2)}) copy-start(f32[50]{0:T(128)} %cg_ref.3) | copy-start | bytes 604
  2.1 1.9 %copy-start = (f32[50,4,16,256]{3,2,1,0:T(8,128)S(1)}, f32[50,4,16,256]{3,2,1,0:T(8,128)}, u32[]{:S(2)}) copy-start(f32[50,4,16,256]{3,2,1,0:T(8,128)} %x_ref.3) | copy-start | bytes 9830404
  4.1 11.9 %copy-start.1 = (f32[50,4,16,256]{3,2,1,0:T(8,128)S(1)}, f32[50,4,16,256]{3,2,1,0:T(8,128)}, u32[]{:S(2)}) copy-start(f32[50,4,16,256]{3,2,1,0:T(8,128)} %x_ref.3) | copy-start | bytes 9830404
  4.1 24.6 %copy-start.4 = (f32[50]{0:T(128)S(1)}, f32[50]{0:T(128)}, u32[]{:S(2)}) copy-start(f32[50]{0:T(128)} %ratio_ref.1) | copy-start | bytes 604
  4.1 24.6 %copy-start.5 = (f32[50]{0:T(128)S(1)}, f32[50]{0:T(128)}, u32[]{:S(2)}) copy-start(f32[50]{0:T(128)} %weight_ref.1) | copy-start | bytes 604
  6.0 22.6 %collective-permute-start = (f32[3,208,256]{2,1,0:T(8,128)}, f32[3,208,256]{2,1,0:T(8,128)}, u32[]{:S(2)}, u32[]{:S(2)}) collective-permute-start(f32[3,208,256]{2,1,0:T(8,128)} %get-tuple-element.12.ownup_ref), channel_id=1, source_target_pairs={{0,8},{8,16},{16,24},{24,32},{32,40},{40,48},{48,56},{56,64},{64,7... | collective-permute-start | bytes 1916936 | tf_op jit(solution)/shard_map/ppermute | solution.py:531
  7.9 20.7 %collective-permute-start.1 = (f32[3,208,256]{2,1,0:T(8,128)}, f32[3,208,256]{2,1,0:T(8,128)}, u32[]{:S(2)}, u32[]{:S(2)}) collective-permute-start(f32[3,208,256]{2,1,0:T(8,128)} %get-tuple-element.13.owndn_ref), channel_id=1, source_target_pairs={{8,0},{16,8},{24,16},{32,24},{40,32},{48,40},{56,48},{64,56},{72,6... | collective-permute-start | bytes 1916936 | tf_op jit(solution)/shard_map/ppermute | solution.py:531
  24.4 36.3 %collective-permute-start.2 = (f32[25,24,256]{2,1,0:T(8,128)S(1)}, f32[25,24,256]{2,1,0:T(8,128)S(1)}, u32[]{:S(2)}, u32[]{:S(2)}) collective-permute-start(f32[25,24,256]{2,1,0:T(8,128)S(1)} %get-tuple-element.16), channel_id=1, source_target_pairs={{0,1},{1,2},{2,3},{3,4},{4,5},{5,6},{6,7},{7,0},{8,9},{9,10},{10,1... | collective-permute-start | bytes 1843208 | tf_op jit(solution)/shard_map/ppermute | solution.py:531
  26.1 34.7 %collective-permute-start.3 = (f32[25,24,256]{2,1,0:T(8,128)S(1)}, f32[25,24,256]{2,1,0:T(8,128)S(1)}, u32[]{:S(2)}, u32[]{:S(2)}) collective-permute-start(f32[25,24,256]{2,1,0:T(8,128)S(1)} %get-tuple-element.17), channel_id=1, source_target_pairs={{1,0},{2,1},{3,2},{4,3},{5,4},{6,5},{7,6},{0,7},{9,8},{10,9},{11,1... | collective-permute-start | bytes 1843208 | tf_op jit(solution)/shard_map/ppermute | solution.py:531
  47.7 4.0 %collective-permute-start.6 = (f32[2,16,256]{2,1,0:T(8,128)S(1)}, f32[2,16,256]{2,1,0:T(8,128)S(1)}, u32[]{:S(2)}, u32[]{:S(2)}) collective-permute-start(f32[2,16,256]{2,1,0:T(8,128)S(1)} %get-tuple-element.21), channel_id=1, source_target_pairs={{0,4},{1,5},{2,6},{3,7},{4,0},{5,1},{6,2},{7,3},{8,12},{9,13},{10,... | collective-permute-start | bytes 98312 | tf_op jit(solution)/shard_map/ppermute | solution.py:531
  51.7 4.3 %collective-permute-start.9 = (f32[2,16,256]{2,1,0:T(8,128)S(1)}, f32[2,16,256]{2,1,0:T(8,128)S(1)}, u32[]{:S(2)}, u32[]{:S(2)}) collective-permute-start(f32[2,16,256]{2,1,0:T(8,128)S(1)} %add.12), channel_id=1, source_target_pairs={{0,3},{1,0},{2,1},{3,2},{4,7},{5,4},{6,5},{7,6},{8,11},{9,8},{10,9... | collective-permute-start | bytes 98312 | tf_op jit(solution)/shard_map/ppermute | solution.py:531
  52.7 5.1 %collective-permute-start.8 = (f32[2,16,256]{2,1,0:T(8,128)S(1)}, f32[2,16,256]{2,1,0:T(8,128)S(1)}, u32[]{:S(2)}, u32[]{:S(2)}) collective-permute-start(f32[2,16,256]{2,1,0:T(8,128)S(1)} %add.12), channel_id=1, source_target_pairs={{0,1},{1,2},{2,3},{3,0},{4,5},{5,6},{6,7},{7,4},{8,9},{9,10},{10,1... | collective-permute-start | bytes 98312 | tf_op jit(solution)/shard_map/ppermute | solution.py:531
  53.8 6.4 %collective-permute-start.7 = (f32[2,16,256]{2,1,0:T(8,128)S(1)}, f32[2,16,256]{2,1,0:T(8,128)S(1)}, u32[]{:S(2)}, u32[]{:S(2)}) collective-permute-start(f32[2,16,256]{2,1,0:T(8,128)S(1)} %add.12), channel_id=1, source_target_pairs={{0,2},{1,3},{2,0},{3,1},{4,6},{5,7},{6,4},{7,5},{8,10},{9,11},{10,... | collective-permute-start | bytes 98312 | tf_op jit(solution)/shard_map/ppermute | solution.py:531
  56.0 7.9 %collective-permute-start.4 = (f32[25,8,256]{2,1,0:T(8,128)S(1)}, f32[25,8,256]{2,1,0:T(8,128)S(1)}, u32[]{:S(2)}, u32[]{:S(2)}) collective-permute-start(f32[25,8,256]{2,1,0:T(8,128)S(1)} %get-tuple-element.18), channel_id=1, source_target_pairs={{0,1},{1,2},{2,3},{3,4},{4,5},{5,6},{6,7},{7,0},{8,9},{9,10},{10,1... | collective-permute-start | bytes 614408 | tf_op jit(solution)/shard_map/ppermute | solution.py:531
  57.8 6.1 %collective-permute-start.5 = (f32[25,8,256]{2,1,0:T(8,128)S(1)}, f32[25,8,256]{2,1,0:T(8,128)S(1)}, u32[]{:S(2)}, u32[]{:S(2)}) collective-permute-start(f32[25,8,256]{2,1,0:T(8,128)S(1)} %get-tuple-element.19), channel_id=1, source_target_pairs={{1,0},{2,1},{3,2},{4,3},{5,4},{6,5},{7,6},{0,7},{9,8},{10,9},{11,1... | collective-permute-start | bytes 614408 | tf_op jit(solution)/shard_map/ppermute | solution.py:531

commit v3 on v2

--- a/solution.py
+++ b/solution.py
@@ -83,18 +83,102 @@
     return [flux[c] - left[c] for c in range(len(row))]
 
 
-def advance(g, t, gc, gs, ub, vb, vl, land, start, hi):
+def advance(g, t, right, left, gc, gs, ub, vb, vl, land, start, hi):
     n, m = len(t), len(t[0])
     ahead = g.below(t, hi)
     flux = [[face_flux(gc + ub[r][c], t[r][c], ahead[r][c]) for c in range(m)] for r in range(n)]
     before = g.above(flux, start)
     out = []
     for r in range(n):
-        dy = col_change(g, t[r], gs, vb[r], vl[r])
-        out.append(
-            [land[r][c] * (t[r][c] - ((flux[r][c] - before[r][c]) + dy[c])) for c in range(m)]
+        out.append([])
+        for c in range(m):
+            dy = face_flux(gs + vb[r][c], t[r][c], right[r][c]) - face_flux(
+                gs + vl[r][c], left[r][c], t[r][c]
+            )
+            out[r].append(land[r][c] * (t[r][c] - ((flux[r][c] - before[r][c]) + dy)))
+    return out
+
+
+def shift_matrix(cols):
+    at, to = np.arange(cols)[:, None], np.arange(cols)[None, :]
+    both = np.concatenate([at == to + 1, at == to - 1], axis=1).astype(np.float32)
+    return jnp.asarray(np.concatenate([both, both], axis=0), jnp.bfloat16)
+
+
+def put_halves(ref, t, slot, n):
+    cols = len(t[0]) * LANES
+    at = pl.ds(n * 2 * SUB, 2 * SUB)
+    for c in range(len(t[0])):
+        v = jnp.concatenate([t[0][c], t[1][c]], axis=0)
+        high = v.astype(jnp.bfloat16)
+        low = (v - high.astype(F32)).astype(jnp.bfloat16)
+        ref[slot, at, pl.ds(c * LANES, LANES)] = high
+        ref[slot, at, pl.ds(cols + c * LANES, LANES)] = low
+
+
+def block_of(ref, slot, n, first=0):
+    return [
+        [
+            ref[slot, pl.ds((n * 2 + r) * SUB, SUB), pl.ds((first + c) * LANES, LANES)]
+            for c in range(2)
+        ]
+        for r in range(2)
+    ]
+
+
+def put_block(ref, t, slot, n):
+    for r in range(2):
+        for c in range(2):
+            ref[slot, pl.ds((n * 2 + r) * SUB, SUB), pl.ds(c * LANES, LANES)] = t[r][c]
+
+
+class Substeps:
+    def __init__(self, g, dirs, speeds, x_ref, cur_ref, mat_ref, ub_s, vb_s, vl_s, scratch):
+        self.g, self.dirs, self.speeds = g, dirs, speeds
+        self.x_ref, self.cur_ref, self.mat_ref = x_ref, cur_ref, mat_ref
+        self.ub_s, self.vb_s, self.vl_s = ub_s, vb_s, vl_s
+        self.t0, self.t1, self.h0, self.h1, self.y0, self.y1 = scratch
+        self.members = [(h, d) for h in range(2) for d in dirs]
+
+    def load(self, pair, slot):
+        land = tiles(self.cur_ref, 2)
+        for n, (h, d) in enumerate(self.members):
+            x = tiles(self.x_ref, pair * 2 + h, d)
+            t = [[land[r][c] * x[r][c] for c in range(2)] for r in range(2)]
+            put_block(self.t0, t, slot, n)
+            put_halves(self.h0, t, slot, n)
+        self.y0[slot] = jnp.dot(self.h0[slot], self.mat_ref[...], preferred_element_type=F32)
+
+    def step(self, pair, slot, n, t_ref, y_ref, start, hi):
+        h, d = self.members[n]
+        gc, gs = self.speeds(pair * 2 + h, d)
+        return advance(
+            self.g, block_of(t_ref, slot, n), block_of(y_ref, slot, n), block_of(y_ref, slot, n, 2),
+            gc, gs, tiles(self.ub_s), tiles(self.vb_s), tiles(self.vl_s), tiles(self.cur_ref, 2),
+            start, hi,
         )
-    return out
+
+    def first(self, pair, slot, edges):
+        for n in range(len(self.members)):
+            t = self.step(pair, slot, n, self.t0, self.y0, *edges(pair, n, 0))
+            put_block(self.t1, t, slot, n)
+            put_halves(self.h1, t, slot, n)
+        self.y1[slot] = jnp.dot(self.h1[slot], self.mat_ref[...], preferred_element_type=F32)
+
+    def second(self, pair, slot, edges, n):
+        return self.step(pair, slot, n, self.t1, self.y1, *edges(pair, n, 1))
+
+
+def substep_scratch(members, cols):
+    rows = members * 2 * SUB
+    return [
+        pltpu.VMEM((2, rows, cols), F32),
+        pltpu.VMEM((2, rows, cols), F32),
+        pltpu.VMEM((2, rows, 2 * cols), jnp.bfloat16),
+        pltpu.VMEM((2, rows, 2 * cols), jnp.bfloat16),
+        pltpu.VMEM((2, rows, 2 * cols), F32),
+        pltpu.VMEM((2, rows, 2 * cols), F32),
+    ]
 
 
 def tiles(ref, *lead):
@@ -219,44 +303,54 @@
     return one, two
 
 
-def ends_kernel(total, sec_ref, tab_ref, cg_ref, x_ref, cur_ref,
-                prev_ref, next_ref, ub_s, vb_s, k_s):
+def ends_kernel(total, sec_ref, tab_ref, cg_ref, x_ref, cur_ref, mat_ref,
+                prev_ref, next_ref, ub_s, vb_s, vl_s, k_s, *scratch):
     g = Grid()
     sec = sec_ref[0]
-    freqs = x_ref.shape[0]
+    pairs = x_ref.shape[0] // 2
+    ends = (0, x_ref.shape[1] - 1)
     zero = [jnp.zeros((SUB, LANES), F32)] * 2
-
     u, v = tiles(cur_ref, 0), tiles(cur_ref, 1)
     put_tiles(ub_s, half_sum(u, g.below(u, zero)))
-    put_tiles(vb_s, half_sum(v, [g.right(r) for r in v]))
+    vb = half_sum(v, [g.right(r) for r in v])
+    put_tiles(vb_s, vb)
+    put_tiles(vl_s, [g.left(vb[r], 0.5 * v[r][0]) for r in range(2)])
     sh = shears_of(g, u, v, zero, zero, zero, zero)
     for n, f in ((0, 0), (1, 4)):
         put_tiles(k_s, turning(sh, tab_ref[sec, FSIN + f], tab_ref[sec, FCOS + f], total), n)
 
-    def one(pair, _):
-        for n, (out_ref, d) in enumerate(((prev_ref, 0), (next_ref, 3))):
-            ends = []
+    def speeds(f, d):
+        return cg_ref[f] * tab_ref[sec, COS + 1 + d], cg_ref[f] * tab_ref[sec, SIN + 1 + d]
+
+    sub = Substeps(g, ends, speeds, x_ref, cur_ref, mat_ref, ub_s, vb_s, vl_s, scratch)
+    edges = lambda pair, n, s: (zero, zero)
+
+    def last(pair, slot):
+        for m, (out_ref, limit) in enumerate(((prev_ref, jnp.minimum), (next_ref, jnp.maximum))):
+            k = tiles(k_s, m)
+            both = []
             for h in range(2):
-                f = pair * 2 + h
-                cg = cg_ref[f]
-                gc, gs = cg * tab_ref[sec, COS + 1 + d], cg * tab_ref[sec, SIN + 1 + d]
-                ub, vb = tiles(ub_s), tiles(vb_s)
-                vl = [0.5 * cur_ref[1, pl.ds(r * SUB, SUB), pl.ds(0, LANES)] for r in range(2)]
-                land = tiles(cur_ref, 2)
-                t = tiles(x_ref, f, d)
-                t = [[land[r][c] * t[r][c] for c in range(2)] for r in range(2)]
-                for _ in range(2):
-                    t = advance(g, t, gc, gs, ub, vb, vl, land, zero, zero)
-                k = tiles(k_s, n)
-                limit = jnp.minimum if d == 0 else jnp.maximum
-                ends.append([[limit(k[r][c], 0.0) * t[r][c] for c in range(2)] for r in range(2)])
+                t = sub.second(pair, slot, edges, h * 2 + m)
+                both.append([[limit(k[r][c], 0.0) * t[r][c] for c in range(2)] for r in range(2)])
             for c in range(2):
-                got = pack_inner(g, [ends[0][r][c] for r in range(2)], [ends[1][r][c] for r in range(2)])
+                got = pack_inner(g, [both[0][r][c] for r in range(2)], [both[1][r][c] for r in range(2)])
                 for q in range(3):
                     out_ref[pair, pl.ds(q * SUB, SUB), pl.ds(c * LANES, LANES)] = got[q]
+
+    sub.load(0, 0)
+    sub.first(0, 0, edges)
+    sub.load(1, 1)
+
+    def two(q, _):
+        for slot in (1, 0):
+            pair = q * 2 + 2 - slot
+            sub.load(jnp.minimum(pair + 1, pairs - 1), 1 - slot)
+            sub.first(pair, slot, edges)
+            last(pair - 1, 1 - slot)
         return 0
 
-    lax.fori_loop(0, freqs // 2, one, 0)
+    lax.fori_loop(0, (pairs - 1) // 2, two, 0)
+    last(pairs - 1, 0)
 
 
 FACE, VROW, VLEFT, LAND, SIDE = 0, 4, 7, 10, 13
@@ -294,11 +388,12 @@
 
 
 def main_kernel(total, sec_ref, tab_ref, cg_ref, ratio_ref, weight_ref,
-                x_ref, cur_ref, top_ref, bot_ref, ownup_ref, owndn_ref,
+                x_ref, cur_ref, mat_ref, top_ref, bot_ref, ownup_ref, owndn_ref,
                 part_ref, e0_ref, e3_ref, prev_ref, next_ref, force_ref,
-                new_ref, sem, ub_s, vb_s, k_s, fld_s, ke_s, st_s, r_s, b_s, re_s, be_s):
+                new_ref, sem, ub_s, vb_s, vl_s, k_s, fld_s, ke_s, st_s, r_s, b_s, re_s, be_s,
+                *scratch):
     g = Grid()
-    chunks = sem.shape[0]
+    pairs = x_ref.shape[0] // 2
     sec = sec_ref[0]
     freqs = x_ref.shape[0]
     dirs = x_ref.shape[1]
@@ -314,7 +409,9 @@
 
     us, vs, ls = (beside_fields(n) for n in range(3))
     put_tiles(ub_s, half_sum(u, g.below(u, us[1][2])))
-    put_tiles(vb_s, half_sum(v, [g.right(r) for r in v]))
+    vb = half_sum(v, [g.right(r) for r in v])
+    put_tiles(vb_s, vb)
+    put_tiles(vl_s, [g.left(vb[r], 0.5 * v[r][0]) for r in range(2)])
     for side in range(2):
         for q in range(4):
             put_tiles(fld_s, half_sum([us[side][q]], [us[side][q + 1]]), side, FACE + q)
@@ -346,13 +443,15 @@
 
     cos_rows, sin_rows = by_direction(COS), by_direction(SIN)
 
-    def beside_rows(q, _):
+    def beside_rows(pair_at):
+        q = jnp.minimum(pair_at, pairs - 1)
+        live = jnp.where(pair_at < pairs, 1.0, 0.0)
         at = pl.ds(pl.multiple_of(q * SUB, SUB), SUB)
         pair = lambda a, b: jnp.where(g.s < dirs, a, b)
         f = q * 2
         cg = pair(cg_ref[f], cg_ref[f + 1])
         gc, gs = cg * cos_rows, cg * sin_rows
-        w = pair(weight_ref[f], weight_ref[f + 1])
+        w = pair(weight_ref[f] * live, weight_ref[f + 1] * live)
         wr = w * pair(ratio_ref[f], ratio_ref[f + 1])
         row = lambda ref, n: [ref[n, at, pl.ds(c * LANES, LANES)] for c in range(2)]
         above = [row(top_ref, n) for n in range(HALO)]
@@ -372,37 +471,32 @@
                     st_s[2, at, cc] = once[1][c]
                 re_s[side, :, cc] += wr * twice[c]
                 be_s[side, :, cc] += w * twice[c]
-        return 0
-
-    lax.fori_loop(0, freqs * dirs // SUB, beside_rows, 0)
-
-    def one(pair, _):
-        outs = [[], []]
+
+    def speeds(f, d):
+        return cg_ref[f] * tab_ref[sec, COS + 1 + d], cg_ref[f] * tab_ref[sec, SIN + 1 + d]
+
+    sub = Substeps(
+        g, tuple(range(dirs)), speeds, x_ref, cur_ref, mat_ref, ub_s, vb_s, vl_s, scratch
+    )
+
+    def edges(pair, n, s):
         group = pl.ds(pl.multiple_of(pair * SUB, SUB), SUB)
 
-        def beside(ref, n, *lead):
+        def beside(ref, m):
             return [
-                jnp.broadcast_to(ref[(*lead, group, pl.ds(c * LANES, LANES))][n : n + 1], (SUB, LANES))
+                jnp.broadcast_to(ref[m, group, pl.ds(c * LANES, LANES)][n : n + 1], (SUB, LANES))
                 for c in range(2)
             ]
 
+        return beside(st_s, s), beside(bot_ref, 0) if s == 0 else beside(st_s, 2)
+
+    def finish(pair, slot):
+        outs = [[], []]
         for h in range(2):
             f = pair * 2 + h
-            cg = cg_ref[f]
             w = weight_ref[f]
             wr = w * ratio_ref[f]
-            a2 = []
-            for d in range(dirs):
-                gc, gs = cg * tab_ref[sec, COS + 1 + d], cg * tab_ref[sec, SIN + 1 + d]
-                ub, vb = tiles(ub_s), tiles(vb_s)
-                vl = [0.5 * cur_ref[1, pl.ds(r * SUB, SUB), pl.ds(0, LANES)] for r in range(2)]
-                land = tiles(cur_ref, 2)
-                t = tiles(x_ref, f, d)
-                t = [[land[r][c] * t[r][c] for c in range(2)] for r in range(2)]
-                n = h * dirs + d
-                t = advance(g, t, gc, gs, ub, vb, vl, land, beside(st_s, n, 0), beside(bot_ref, n, 0))
-                t = advance(g, t, gc, gs, ub, vb, vl, land, beside(st_s, n, 1), beside(st_s, n, 2))
-                a2.append(t)
+            a2 = [sub.second(pair, slot, edges, h * dirs + d) for d in range(dirs)]
             for r in range(2):
                 for c in range(2):
                     here = (pl.ds(r * SUB, SUB), pl.ds(c * LANES, LANES))
@@ -424,22 +518,35 @@
                 ref[pair, :, pl.ds(c * LANES, LANES)] = pack_outer(
                     g, [ends[0][r][c] for r in range(2)], [ends[1][r][c] for r in range(2)]
                 )
-        return 0
-
-    per = freqs // chunks
+
+    spans = [(0, 16), (16, 16), (32, 16), (48, 2)]
 
     def put(q):
-        span = pl.ds(q * per, per)
+        span = pl.ds(*spans[q])
         return pltpu.make_async_copy(
             new_ref.at[span], part_ref.at[span, pl.ds(1, dirs - 2)], sem.at[q]
         )
 
-    def chunk(q, _):
-        lax.fori_loop(q * (per // 2), (q + 1) * (per // 2), one, 0)
+    def two(q, _):
+        for slot in (1, 0):
+            pair = q * 2 + 2 - slot
+            sub.load(jnp.minimum(pair + 1, pairs - 1), 1 - slot)
+            sub.first(pair, slot, edges)
+            finish(pair - 1, 1 - slot)
+            beside_rows(pair + 1)
+        return 0
+
+    beside_rows(0)
+    beside_rows(1)
+    sub.load(0, 0)
+    sub.first(0, 0, edges)
+    sub.load(1, 1)
+    for q in range(3):
+        lax.fori_loop(q * 4, q * 4 + 4, two, 0)
         put(q).start()
-        return 0
-
-    lax.fori_loop(0, chunks, chunk, 0)
+    finish(pairs - 1, 0)
+    put(3).start()
+
     cs = [tab_ref[sec, COS + n] for n in range(dirs + 2)]
     sn = [tab_ref[sec, SIN + n] for n in range(dirs + 2)]
     coef = (
@@ -478,11 +585,8 @@
     for n, (p, q) in enumerate(((dx(xx, edges[0]), dy(xy)), (dx(xy, edges[1]), dy(yy)))):
         put_tiles(force_ref, [[-(p[r][c] + q[r][c]) for c in range(2)] for r in range(2)], n)
 
-    def done(q, _):
+    for q in range(4):
         put(q).wait()
-        return 0
-
-    lax.fori_loop(0, chunks, done, 0)
 
 
 def join_kernel(e0_ref, e3_ref, inp_ref, inn_ref, outp_ref, outn_ref, part_ref, o_ref, buf, sem):
@@ -533,6 +637,7 @@
     vmem = lambda *s: pltpu.VMEM(s, F32)
     params = lambda: pltpu.CompilerParams(vmem_limit_bytes=24 * 2**20)
 
+    matrix = shift_matrix(cols)
     fields = jnp.concatenate([currents, land_mask.astype(F32)[None]])
     flat = action.reshape(combos, rows // SUB, SUB, cols // LANES, LANES)
     flat = flat.transpose(0, 1, 3, 2, 4).reshape(combos * rows * cols // LANES, LANES)
@@ -553,13 +658,13 @@
 
     in_prev, in_next = pl.pallas_call(
         functools.partial(ends_kernel, total),
-        in_specs=[smem, smem, smem, vm, vm],
+        in_specs=[smem, smem, smem, vm, vm, vm],
         out_specs=[vm, vm],
         out_shape=[f32(freqs // 2, 24, cols)] * 2,
-        scratch_shapes=[vmem(rows, cols), vmem(rows, cols), vmem(2, rows, cols)],
+        scratch_shapes=[vmem(rows, cols)] * 3 + [vmem(2, rows, cols)] + substep_scratch(4, cols),
         compiler_params=params(),
         name="sector_ends",
-    )(sec, table, group_speed, action, fields)
+    )(sec, table, group_speed, action, fields, matrix)
     fwd = [(i, (i + 1) % sectors) for i in range(sectors)]
     back = [(j, i) for i, j in fwd]
     inner_from_prev = send(in_next, "dir", fwd)
@@ -567,7 +672,7 @@
 
     part, e0, e3, out_prev, out_next, force = pl.pallas_call(
         functools.partial(main_kernel, total),
-        in_specs=[smem] * 5 + [vm] * 6,
+        in_specs=[smem] * 5 + [vm] * 7,
         out_specs=[hbm, vm, vm, vm, vm, vm],
         out_shape=[
             f32(freqs, dirs, rows, cols),
@@ -578,14 +683,15 @@
             f32(2, rows, cols),
         ],
         scratch_shapes=[
-            vmem(freqs, dirs - 2, rows, cols), pltpu.SemaphoreType.DMA((5,)),
-            vmem(rows, cols), vmem(rows, cols), vmem(dirs + 1, rows, cols),
+            vmem(freqs, dirs - 2, rows, cols), pltpu.SemaphoreType.DMA((4,)),
+            vmem(rows, cols), vmem(rows, cols), vmem(rows, cols), vmem(dirs + 1, rows, cols),
             vmem(2, SIDE, SUB, cols), vmem(2, dirs + 1, SUB, cols), vmem(3, combos, cols),
             vmem(dirs, rows, cols), vmem(rows, cols), vmem(2, SUB, cols), vmem(2, SUB, cols),
+            *substep_scratch(2 * dirs, cols),
         ],
         compiler_params=params(),
         name="transport",
-    )(sec, table, group_speed, group_ratio, bin_weight, action, fields,
+    )(sec, table, group_speed, group_ratio, bin_weight, action, fields, matrix,
       top, bot, up_rows, dn_rows)
 
     outer_from_prev = send(out_next, "dir", fwd)

time: 66.3 us -> 61.2 us (0.923)
  Pallas kernels: 30.7 us -> 24.5 us
  local copies, waits for them, and re-layouts: 1.95 us -> 2.99 us
    pallas_call x1, Pallas kernels: 19.1 us -> 13.4 us  [per_device(): pl.pallas_call(functools.partial(main_kernel, total), in_specs=[smem] * 5...]
    unnamed x12 -> x16, local copies, waits for them, and re-layouts: 1.95 us -> 2.99 us
  transfers between devices with their start and end apart: 10 -> 10, of which waited for: 4 -> 4; matrix products, arithmetic and copies ran while one was open for 1% -> 1% of each run, Pallas kernels for 42% -> 35%
where the time goes in v3:
time: 61.2 us; the launch traced here: 60 us
  Pallas kernels  24.5 us (40%)
  starting transfers between devices  20.9 us (34%)
  waiting for transfers between devices  8.72 us (14%)
  local copies, waits for them, and re-layouts  2.99 us (5%)
  other arithmetic  2.13 us (3%)
  between operations  0.74 us (1%)
    ppermute x10, starting transfers between devices, send(): return lax.ppermute(value, axis, pairs)  20.9 us
    pallas_call x1, Pallas kernels, per_device(): pl.pallas_call(functools.partial(main_kernel, total), in_specs=[smem] * 5...  13.4 us
    ppermute x10, waiting for transfers between devices, send(): return lax.ppermute(value, axis, pairs)  8.72 us
    pallas_call x1, Pallas kernels, per_device(): pl.pallas_call(functools.partial(ends_kernel, total), in_specs=[smem, sme...  7.81 us
    unnamed x16, local copies, waits for them, and re-layouts  2.99 us
    pallas_call x1, Pallas kernels, per_device(): pl.pallas_call(rows_kernel, in_specs=[vm, vm], out_specs=[vm, vm], out_sh...  1.96 us
    pallas_call x1, Pallas kernels, per_device(): pl.pallas_call(join_kernel, in_specs=[vm] * 6 + [hbm], out_specs=hbm, out...  1.28 us
  transfers between devices with their start and end apart: 10, of which 4 were waited for; matrix products, arithmetic and copies ran while one was open for 1% of the time, Pallas kernels for 35%

profile of v3, /device:TPU:6, one launch (start us, length us, event | category | flops | bytes accessed | tf_op | source)
XLA Modules:
  0.0 60.0 jit_solution(17093938908277990822)
XLA Ops:
  0.6 0.0 copy-start.4
  0.7 0.7 %convert_bitcast_fusion = f32[1,16,256]{2,1,0:T(8,128)S(1)} fusion(s32[16,256]{1,0:T(8,128)} %param.10), kind=kLoop, calls=%fused_computation.2 | loop fusion | flops 4096 | bytes 32768 | tf_op jit(solution)/shard_map/broadcast_in_dim | solution.py:641
  1.4 0.8 %pad_maximum_fusion.fld_ref.cur_ref = f32[3,16,256]{2,1,0:T(8,128)S(1)} fusion(f32[1,16,256]{2,1,0:T(8,128)S(1)} %convert_bitcast_fusion, f32[2,16,256]{2,1,0:T(8,128)} %param.9), kind=kLoop, calls=%fused_computation | loop fusion | flops 12288 | bytes 98304 | tf_op jit(solution)/shard_map/concatenate | solution.py:641
  2.1 1.9 %copy-done = f32[50,4,16,256]{3,2,1,0:T(8,128)S(1)} copy-done((f32[50,4,16,256]{3,2,1,0:T(8,128)S(1)}, f32[50,4,16,256]{3,2,1,0:T(8,128)}, u32[]{:S(2)}) %copy-start) | copy-done | bytes 3276824
  4.1 2.0 %boundary_rows.1 = (f32[3,208,256]{2,1,0:T(8,128)}, f32[3,208,256]{2,1,0:T(8,128)}) custom-call(f32[6400,128]{1,0:T(8,128)S(1)} %bitcast.8, f32[3,16,256]{2,1,0:T(8,128)S(1)} %pad_maximum_fusion.fld_ref.cur_ref), custom_call_target="tpu_custom_call" | custom-call | tf_op jit(solution)/shard_map/boundary_rows/pallas_call | solution.py:646
  6.0 1.9 %collective-permute-start = (f32[3,208,256]{2,1,0:T(8,128)}, f32[3,208,256]{2,1,0:T(8,128)}, u32[]{:S(2)}, u32[]{:S(2)}) collective-permute-start(f32[3,208,256]{2,1,0:T(8,128)} %get-tuple-element.12.ownup_ref), channel_id=1, source_target_pairs={{0,8},{8,16},{16,24},{24,32},{32,40},{40,48},{48,56},{56,64},{64,7... | collective-permute-start | bytes 1916936 | tf_op jit(solution)/shard_map/ppermute | solution.py:635
  8.0 8.0 %collective-permute-start.1 = (f32[3,208,256]{2,1,0:T(8,128)}, f32[3,208,256]{2,1,0:T(8,128)}, u32[]{:S(2)}, u32[]{:S(2)}) collective-permute-start(f32[3,208,256]{2,1,0:T(8,128)} %get-tuple-element.13.owndn_ref), channel_id=1, source_target_pairs={{8,0},{16,8},{24,16},{32,24},{40,32},{48,40},{56,48},{64,56},{72,6... | collective-permute-start | bytes 1916936 | tf_op jit(solution)/shard_map/ppermute | solution.py:635
  16.1 1.0 %copy-done.2 = bf16[512,512]{1,0:T(8,128)(2,1)S(1)} copy-done((bf16[512,512]{1,0:T(8,128)(2,1)S(1)}, bf16[512,512]{1,0:T(8,128)(2,1)}, u32[]{:S(2)}) %copy-start.2) | copy-done | bytes 524312
  17.1 7.8 %sector_ends.1 = (f32[25,24,256]{2,1,0:T(8,128)S(1)}, f32[25,24,256]{2,1,0:T(8,128)S(1)}) custom-call(s32[1]{0:T(128)} %bitcast.sec_ref, f32[8,22]{1,0:T(8,128)S(1)} %copy-done.4, f32[50]{0:T(128)S(1)} %copy-done.5, f32[50,4,16,256]{3,2,1,0:T(8,128)S(1)} %copy-done.1, f32[3,16,256]{2,1,0:T(8,128)S(1)} %pad_maximum_fusion.fld_ref.cur_ref, ...), custom_call_target="tpu_custom_call" | custom-call | tf_op jit(solution)/shard_map/sector_ends/pallas_call | solution.py:659
  24.9 1.7 %collective-permute-start.2 = (f32[25,24,256]{2,1,0:T(8,128)S(1)}, f32[25,24,256]{2,1,0:T(8,128)S(1)}, u32[]{:S(2)}, u32[]{:S(2)}) collective-permute-start(f32[25,24,256]{2,1,0:T(8,128)S(1)} %get-tuple-element.16), channel_id=1, source_target_pairs={{0,1},{1,2},{2,3},{3,4},{4,5},{5,6},{6,7},{7,0},{8,9},{9,10},{10,1... | collective-permute-start | bytes 1843208 | tf_op jit(solution)/shard_map/ppermute | solution.py:635
  26.6 2.5 %collective-permute-start.3 = (f32[25,24,256]{2,1,0:T(8,128)S(1)}, f32[25,24,256]{2,1,0:T(8,128)S(1)}, u32[]{:S(2)}, u32[]{:S(2)}) collective-permute-start(f32[25,24,256]{2,1,0:T(8,128)S(1)} %get-tuple-element.17), channel_id=1, source_target_pairs={{1,0},{2,1},{3,2},{4,3},{5,4},{6,5},{7,6},{0,7},{9,8},{10,9},{11,1... | collective-permute-start | bytes 1843208 | tf_op jit(solution)/shard_map/ppermute | solution.py:635
  29.2 13.4 %transport.1 = (f32[50,4,16,256]{3,2,1,0:T(8,128)}, f32[50,16,256]{2,1,0:T(8,128)S(1)}, f32[50,16,256]{2,1,0:T(8,128)S(1)}, f32[25,8,256]{2,1,0:T(8,128)S(1)}, f...) custom-call(s32[1]{0:T(128)} %bitcast.sec_ref, f32[8,22]{1,0:T(8,128)S(1)} %copy-done.4, f32[50]{0:T(128)S(1)} %copy-done.5, ...), custom_call_target="tpu_custom_call" | custom-call | tf_op jit(solution)/shard_map/transport/pallas_call | solution.py:673
  42.6 0.5 collective-permute-start.6
  43.1 3.5 %collective-permute-done.6 = f32[2,16,256]{2,1,0:T(8,128)S(1)} collective-permute-done((f32[2,16,256]{2,1,0:T(8,128)S(1)}, f32[2,16,256]{2,1,0:T(8,128)S(1)}, u32[]{:S(2)}, u32[]{:S(2)}) %collective-permute-start.6) | collective-permute-done | bytes 32800 | tf_op jit(solution)/shard_map/ppermute | solution.py:635
  46.6 0.9 %collective-permute-start.9 = (f32[2,16,256]{2,1,0:T(8,128)S(1)}, f32[2,16,256]{2,1,0:T(8,128)S(1)}, u32[]{:S(2)}, u32[]{:S(2)}) collective-permute-start(f32[2,16,256]{2,1,0:T(8,128)S(1)} %add.12), channel_id=1, source_target_pairs={{0,3},{1,0},{2,1},{3,2},{4,7},{5,4},{6,5},{7,6},{8,11},{9,8},{10,9... | collective-permute-start | bytes 98312 | tf_op jit(solution)/shard_map/ppermute | solution.py:635
  47.5 1.1 %collective-permute-start.8 = (f32[2,16,256]{2,1,0:T(8,128)S(1)}, f32[2,16,256]{2,1,0:T(8,128)S(1)}, u32[]{:S(2)}, u32[]{:S(2)}) collective-permute-start(f32[2,16,256]{2,1,0:T(8,128)S(1)} %add.12), channel_id=1, source_target_pairs={{0,1},{1,2},{2,3},{3,0},{4,5},{5,6},{6,7},{7,4},{8,9},{9,10},{10,1... | collective-permute-start | bytes 98312 | tf_op jit(solution)/shard_map/ppermute | solution.py:635
  48.6 1.1 %collective-permute-start.7 = (f32[2,16,256]{2,1,0:T(8,128)S(1)}, f32[2,16,256]{2,1,0:T(8,128)S(1)}, u32[]{:S(2)}, u32[]{:S(2)}) collective-permute-start(f32[2,16,256]{2,1,0:T(8,128)S(1)} %add.12), channel_id=1, source_target_pairs={{0,2},{1,3},{2,0},{3,1},{4,6},{5,7},{6,4},{7,5},{8,10},{9,11},{10,... | collective-permute-start | bytes 98312 | tf_op jit(solution)/shard_map/ppermute | solution.py:635
  49.7 1.1 %collective-permute-done.9 = f32[2,16,256]{2,1,0:T(8,128)S(1)} collective-permute-done((f32[2,16,256]{2,1,0:T(8,128)S(1)}, f32[2,16,256]{2,1,0:T(8,128)S(1)}, u32[]{:S(2)}, u32[]{:S(2)}) %collective-permute-start.9) | collective-permute-done | bytes 32800 | tf_op jit(solution)/shard_map/ppermute | solution.py:635
  50.8 0.8 %collective-permute-start.4 = (f32[25,8,256]{2,1,0:T(8,128)S(1)}, f32[25,8,256]{2,1,0:T(8,128)S(1)}, u32[]{:S(2)}, u32[]{:S(2)}) collective-permute-start(f32[25,8,256]{2,1,0:T(8,128)S(1)} %get-tuple-element.18), channel_id=1, source_target_pairs={{0,1},{1,2},{2,3},{3,4},{4,5},{5,6},{6,7},{7,0},{8,9},{9,10},{10,1... | collective-permute-start | bytes 614408 | tf_op jit(solution)/shard_map/ppermute | solution.py:635
  51.6 1.0 %collective-permute-done.8 = f32[2,16,256]{2,1,0:T(8,128)S(1)} collective-permute-done((f32[2,16,256]{2,1,0:T(8,128)S(1)}, f32[2,16,256]{2,1,0:T(8,128)S(1)}, u32[]{:S(2)}, u32[]{:S(2)}) %collective-permute-start.8) | collective-permute-done | bytes 32800 | tf_op jit(solution)/shard_map/ppermute | solution.py:635
  52.6 2.3 %collective-permute-start.5 = (f32[25,8,256]{2,1,0:T(8,128)S(1)}, f32[25,8,256]{2,1,0:T(8,128)S(1)}, u32[]{:S(2)}, u32[]{:S(2)}) collective-permute-start(f32[25,8,256]{2,1,0:T(8,128)S(1)} %get-tuple-element.19), channel_id=1, source_target_pairs={{1,0},{2,1},{3,2},{4,3},{5,4},{6,5},{7,6},{0,7},{9,8},{10,9},{11,1... | collective-permute-start | bytes 614408 | tf_op jit(solution)/shard_map/ppermute | solution.py:635
  54.9 0.6 %add_add_fusion = f32[2,16,256]{2,1,0:T(8,128)} fusion(f32[2,16,256]{2,1,0:T(8,128)S(1)} %collective-permute-done.8, f32[2,16,256]{2,1,0:T(8,128)S(1)} %collective-permute-done.9, f32[2,16,256]{2,1,0:T(8,128)S(1)} %add.12, f32[2,16,256]{2,1,0:T(8,128)S(1)} %collective-permute-done.7), kind=kLoop, calls=%fused_computation.1 | loop fusion | flops 24576 | bytes 163840 | tf_op jit(solution)/shard_map/add | solution.py:706
  55.6 3.1 %collective-permute-done.4.outp_ref = f32[25,8,256]{2,1,0:T(8,128)S(1)} collective-permute-done((f32[25,8,256]{2,1,0:T(8,128)S(1)}, f32[25,8,256]{2,1,0:T(8,128)S(1)}, u32[]{:S(2)}, u32[]{:S(2)}) %collective-permute-start.4) | collective-permute-done | bytes 204832 | tf_op jit(solution)/shard_map/ppermute | solution.py:635
  58.7 1.3 %join_sectors.1 = f32[50,4,16,256]{3,2,1,0:T(8,128)} custom-call(f32[50,16,256]{2,1,0:T(8,128)S(1)} %get-tuple-element.14.e0_ref, f32[50,16,256]{2,1,0:T(8,128)S(1)} %get-tuple-element.15.e3_ref, f32[25,24,256]{2,1,0:T(8,128)S(1)} %collective-permute-done.2.inp_ref, ...), custom_call_target="tpu_custom_call", output_to_operand_aliasing={{}: (6, {})} | custom-call | tf_op jit(solution)/shard_map/join_sectors/pallas_call | solution.py:708
  (20 shorter events, 0.0 us)
Async XLA Ops:
  0.6 15.4 %copy-start.4 = (f32[8,22]{1,0:T(8,128)S(1)}, f32[8,22]{1,0:T(8,128)}, u32[]{:S(2)}) copy-start(f32[8,22]{1,0:T(8,128)} %constant.8.clone.tab_ref) | copy-start | bytes 2116
  0.6 15.4 %copy-start.5 = (f32[50]{0:T(128)S(1)}, f32[50]{0:T(128)}, u32[]{:S(2)}) copy-start(f32[50]{0:T(128)} %cg_ref.3) | copy-start | bytes 604
  2.1 1.9 %copy-start = (f32[50,4,16,256]{3,2,1,0:T(8,128)S(1)}, f32[50,4,16,256]{3,2,1,0:T(8,128)}, u32[]{:S(2)}) copy-start(f32[50,4,16,256]{3,2,1,0:T(8,128)} %x_ref.3) | copy-start | bytes 9830404
  4.1 12.0 %copy-start.1 = (f32[50,4,16,256]{3,2,1,0:T(8,128)S(1)}, f32[50,4,16,256]{3,2,1,0:T(8,128)}, u32[]{:S(2)}) copy-start(f32[50,4,16,256]{3,2,1,0:T(8,128)} %x_ref.3) | copy-start | bytes 9830404
  4.1 25.1 %copy-start.6 = (f32[50]{0:T(128)S(1)}, f32[50]{0:T(128)}, u32[]{:S(2)}) copy-start(f32[50]{0:T(128)} %ratio_ref.1) | copy-start | bytes 604
  4.1 25.1 %copy-start.7 = (f32[50]{0:T(128)S(1)}, f32[50]{0:T(128)}, u32[]{:S(2)}) copy-start(f32[50]{0:T(128)} %weight_ref.1) | copy-start | bytes 604
  6.0 23.1 %collective-permute-start = (f32[3,208,256]{2,1,0:T(8,128)}, f32[3,208,256]{2,1,0:T(8,128)}, u32[]{:S(2)}, u32[]{:S(2)}) collective-permute-start(f32[3,208,256]{2,1,0:T(8,128)} %get-tuple-element.12.ownup_ref), channel_id=1, source_target_pairs={{0,8},{8,16},{16,24},{24,32},{32,40},{40,48},{48,56},{56,64},{64,7... | collective-permute-start | bytes 1916936 | tf_op jit(solution)/shard_map/ppermute | solution.py:635
  8.0 21.2 %collective-permute-start.1 = (f32[3,208,256]{2,1,0:T(8,128)}, f32[3,208,256]{2,1,0:T(8,128)}, u32[]{:S(2)}, u32[]{:S(2)}) collective-permute-start(f32[3,208,256]{2,1,0:T(8,128)} %get-tuple-element.13.owndn_ref), channel_id=1, source_target_pairs={{8,0},{16,8},{24,16},{32,24},{40,32},{48,40},{56,48},{64,56},{72,6... | collective-permute-start | bytes 1916936 | tf_op jit(solution)/shard_map/ppermute | solution.py:635
  16.0 1.0 %copy-start.2 = (bf16[512,512]{1,0:T(8,128)(2,1)S(1)}, bf16[512,512]{1,0:T(8,128)(2,1)}, u32[]{:S(2)}) copy-start(bf16[512,512]{1,0:T(8,128)(2,1)} %constant.9.clone.mat_ref) | copy-start | bytes 1572868
  17.1 12.1 %copy-start.3 = (bf16[512,512]{1,0:T(8,128)(2,1)S(1)}, bf16[512,512]{1,0:T(8,128)(2,1)}, u32[]{:S(2)}) copy-start(bf16[512,512]{1,0:T(8,128)(2,1)} %constant.9.clone.mat_ref) | copy-start | bytes 1572868
  24.9 30.7 %collective-permute-start.2 = (f32[25,24,256]{2,1,0:T(8,128)S(1)}, f32[25,24,256]{2,1,0:T(8,128)S(1)}, u32[]{:S(2)}, u32[]{:S(2)}) collective-permute-start(f32[25,24,256]{2,1,0:T(8,128)S(1)} %get-tuple-element.16), channel_id=1, source_target_pairs={{0,1},{1,2},{2,3},{3,4},{4,5},{5,6},{6,7},{7,0},{8,9},{9,10},{10,1... | collective-permute-start | bytes 1843208 | tf_op jit(solution)/shard_map/ppermute | solution.py:635
  26.6 29.0 %collective-permute-start.3 = (f32[25,24,256]{2,1,0:T(8,128)S(1)}, f32[25,24,256]{2,1,0:T(8,128)S(1)}, u32[]{:S(2)}, u32[]{:S(2)}) collective-permute-start(f32[25,24,256]{2,1,0:T(8,128)S(1)} %get-tuple-element.17), channel_id=1, source_target_pairs={{1,0},{2,1},{3,2},{4,3},{5,4},{6,5},{7,6},{0,7},{9,8},{10,9},{11,1... | collective-permute-start | bytes 1843208 | tf_op jit(solution)/shard_map/ppermute | solution.py:635
  42.6 4.0 %collective-permute-start.6 = (f32[2,16,256]{2,1,0:T(8,128)S(1)}, f32[2,16,256]{2,1,0:T(8,128)S(1)}, u32[]{:S(2)}, u32[]{:S(2)}) collective-permute-start(f32[2,16,256]{2,1,0:T(8,128)S(1)} %get-tuple-element.21), channel_id=1, source_target_pairs={{0,4},{1,5},{2,6},{3,7},{4,0},{5,1},{6,2},{7,3},{8,12},{9,13},{10,... | collective-permute-start | bytes 98312 | tf_op jit(solution)/shard_map/ppermute | solution.py:635
  46.6 4.2 %collective-permute-start.9 = (f32[2,16,256]{2,1,0:T(8,128)S(1)}, f32[2,16,256]{2,1,0:T(8,128)S(1)}, u32[]{:S(2)}, u32[]{:S(2)}) collective-permute-start(f32[2,16,256]{2,1,0:T(8,128)S(1)} %add.12), channel_id=1, source_target_pairs={{0,3},{1,0},{2,1},{3,2},{4,7},{5,4},{6,5},{7,6},{8,11},{9,8},{10,9... | collective-permute-start | bytes 98312 | tf_op jit(solution)/shard_map/ppermute | solution.py:635
  47.5 5.1 %collective-permute-start.8 = (f32[2,16,256]{2,1,0:T(8,128)S(1)}, f32[2,16,256]{2,1,0:T(8,128)S(1)}, u32[]{:S(2)}, u32[]{:S(2)}) collective-permute-start(f32[2,16,256]{2,1,0:T(8,128)S(1)} %add.12), channel_id=1, source_target_pairs={{0,1},{1,2},{2,3},{3,0},{4,5},{5,6},{6,7},{7,4},{8,9},{9,10},{10,1... | collective-permute-start | bytes 98312 | tf_op jit(solution)/shard_map/ppermute | solution.py:635
  48.6 6.3 %collective-permute-start.7 = (f32[2,16,256]{2,1,0:T(8,128)S(1)}, f32[2,16,256]{2,1,0:T(8,128)S(1)}, u32[]{:S(2)}, u32[]{:S(2)}) collective-permute-start(f32[2,16,256]{2,1,0:T(8,128)S(1)} %add.12), channel_id=1, source_target_pairs={{0,2},{1,3},{2,0},{3,1},{4,6},{5,7},{6,4},{7,5},{8,10},{9,11},{10,... | collective-permute-start | bytes 98312 | tf_op jit(solution)/shard_map/ppermute | solution.py:635
  50.8 7.9 %collective-permute-start.4 = (f32[25,8,256]{2,1,0:T(8,128)S(1)}, f32[25,8,256]{2,1,0:T(8,128)S(1)}, u32[]{:S(2)}, u32[]{:S(2)}) collective-permute-start(f32[25,8,256]{2,1,0:T(8,128)S(1)} %get-tuple-element.18), channel_id=1, source_target_pairs={{0,1},{1,2},{2,3},{3,4},{4,5},{5,6},{6,7},{7,0},{8,9},{9,10},{10,1... | collective-permute-start | bytes 614408 | tf_op jit(solution)/shard_map/ppermute | solution.py:635
  52.6 6.0 %collective-permute-start.5 = (f32[25,8,256]{2,1,0:T(8,128)S(1)}, f32[25,8,256]{2,1,0:T(8,128)S(1)}, u32[]{:S(2)}, u32[]{:S(2)}) collective-permute-start(f32[25,8,256]{2,1,0:T(8,128)S(1)} %get-tuple-element.19), channel_id=1, source_target_pairs={{1,0},{2,1},{3,2},{4,3},{5,4},{6,5},{7,6},{0,7},{9,8},{10,9},{11,1... | collective-permute-start | bytes 614408 | tf_op jit(solution)/shard_map/ppermute | solution.py:635

commit v4 on v3

--- a/solution.py
+++ b/solution.py
@@ -99,10 +99,17 @@
     return out
 
 
-def shift_matrix(cols):
-    at, to = np.arange(cols)[:, None], np.arange(cols)[None, :]
-    both = np.concatenate([at == to + 1, at == to - 1], axis=1).astype(np.float32)
-    return jnp.asarray(np.concatenate([both, both], axis=0), jnp.bfloat16)
+def put_shift_matrix(ref):
+    cols = ref.shape[0] // 2
+    for c in range(2 * cols // LANES):
+        for r in range(cols // LANES):
+            at = lax.broadcasted_iota(jnp.int32, (LANES, LANES), 0) + r * LANES
+            to = lax.broadcasted_iota(jnp.int32, (LANES, LANES), 1) + c * LANES
+            step = 1 if c * LANES < cols else -1
+            base = 0 if c * LANES < cols else cols
+            v = jnp.where(at - (to - base) == step, 1.0, 0.0).astype(jnp.bfloat16)
+            for half in range(2):
+                ref[pl.ds(half * cols + r * LANES, LANES), pl.ds(c * LANES, LANES)] = v
 
 
 def put_halves(ref, t, slot, n):
@@ -169,15 +176,15 @@
         return self.step(pair, slot, n, self.t1, self.y1, *edges(pair, n, 1))
 
 
-def substep_scratch(members, cols):
+def substep_scratch(members, cols, slots):
     rows = members * 2 * SUB
     return [
-        pltpu.VMEM((2, rows, cols), F32),
-        pltpu.VMEM((2, rows, cols), F32),
-        pltpu.VMEM((2, rows, 2 * cols), jnp.bfloat16),
-        pltpu.VMEM((2, rows, 2 * cols), jnp.bfloat16),
-        pltpu.VMEM((2, rows, 2 * cols), F32),
-        pltpu.VMEM((2, rows, 2 * cols), F32),
+        pltpu.VMEM((slots, rows, cols), F32),
+        pltpu.VMEM((slots, rows, cols), F32),
+        pltpu.VMEM((slots, rows, 2 * cols), jnp.bfloat16),
+        pltpu.VMEM((slots, rows, 2 * cols), jnp.bfloat16),
+        pltpu.VMEM((slots, rows, 2 * cols), F32),
+        pltpu.VMEM((slots, rows, 2 * cols), F32),
     ]
 
 
@@ -257,9 +264,25 @@
 HALO = 3
 
 
-def rows_kernel(x_ref, fld_ref, up_ref, dn_ref):
+def rows_kernel(x_ref, cur_ref, land_ref, up_ref, dn_ref, fld_ref, keep_ref, mask_ref, sem):
     last = up_ref.shape[1] - SUB
+    parts = sem.shape[0] - 2
+    count = last // parts
     sides = ((up_ref, range(16 - HALO, 16)), (dn_ref, range(HALO)))
+
+    def fetch(i):
+        span = pl.ds(i * count * 32, count * 32)
+        return pltpu.make_async_copy(x_ref.at[span], keep_ref.at[span], sem.at[i])
+
+    fields = pltpu.make_async_copy(cur_ref, fld_ref.at[pl.ds(0, 2)], sem.at[parts])
+    mask = pltpu.make_async_copy(land_ref, mask_ref, sem.at[parts + 1])
+    fields.start()
+    mask.start()
+    for i in range(parts):
+        fetch(i).start()
+    fields.wait()
+    mask.wait()
+    fld_ref[2] = mask_ref[...].astype(F32)
     for ref, rows in sides:
         for k, row in enumerate(rows):
             ref[k, pl.ds(last, SUB), :] = jnp.zeros((SUB, 2 * LANES), F32)
@@ -272,12 +295,14 @@
             for k, row in enumerate(rows):
                 for c in range(2):
                     start = at * 32 + (row // SUB * 2 + c) * SUB + row % SUB
-                    v = x_ref[pl.ds(start, SUB, stride=32), :]
+                    v = keep_ref[pl.ds(start, SUB, stride=32), :]
                     land = spread_row(fld_ref, 2, 2, row)[c]
                     ref[k, pl.ds(at, SUB), pl.ds(c * LANES, LANES)] = v * land
         return 0
 
-    lax.fori_loop(0, last // SUB, one, 0)
+    for i in range(parts):
+        fetch(i).wait()
+        lax.fori_loop(i * (count // SUB), (i + 1) * (count // SUB), one, 0)
 
 
 def pack_inner(g, a, b):
@@ -303,12 +328,13 @@
     return one, two
 
 
-def ends_kernel(total, sec_ref, tab_ref, cg_ref, x_ref, cur_ref, mat_ref,
-                prev_ref, next_ref, ub_s, vb_s, vl_s, k_s, *scratch):
+def ends_kernel(total, sec_ref, tab_ref, cg_ref, x_ref, cur_ref,
+                prev_ref, next_ref, mat_ref, ub_s, vb_s, vl_s, k_s, *scratch):
     g = Grid()
     sec = sec_ref[0]
     pairs = x_ref.shape[0] // 2
     ends = (0, x_ref.shape[1] - 1)
+    put_shift_matrix(mat_ref)
     zero = [jnp.zeros((SUB, LANES), F32)] * 2
     u, v = tiles(cur_ref, 0), tiles(cur_ref, 1)
     put_tiles(ub_s, half_sum(u, g.below(u, zero)))
@@ -337,20 +363,29 @@
                 for q in range(3):
                     out_ref[pair, pl.ds(q * SUB, SUB), pl.ds(c * LANES, LANES)] = got[q]
 
-    sub.load(0, 0)
-    sub.first(0, 0, edges)
-    sub.load(1, 1)
-
-    def two(q, _):
-        for slot in (1, 0):
-            pair = q * 2 + 2 - slot
-            sub.load(jnp.minimum(pair + 1, pairs - 1), 1 - slot)
-            sub.first(pair, slot, edges)
-            last(pair - 1, 1 - slot)
+    def turn(p, at):
+        sub.load(p + 2, (at + 2) % 3)
+        sub.first(p, at, edges)
+        last(p - 2, (at + 1) % 3)
+
+    for p in range(4):
+        sub.load(p, p % 3)
+        if p >= 2:
+            sub.first(p - 2, p - 2, edges)
+
+    def three(q, _):
+        for n in range(3):
+            turn(q * 3 + 2 + n, (2 + n) % 3)
         return 0
 
-    lax.fori_loop(0, (pairs - 1) // 2, two, 0)
-    last(pairs - 1, 0)
+    turns = (pairs - 4) // 3
+    lax.fori_loop(0, turns, three, 0)
+    for p in range(turns * 3 + 2, pairs + 2):
+        if p + 2 < pairs:
+            sub.load(p + 2, (p + 2) % 3)
+        if p < pairs:
+            sub.first(p, p % 3, edges)
+        last(p - 2, (p - 2) % 3)
 
 
 FACE, VROW, VLEFT, LAND, SIDE = 0, 4, 7, 10, 13
@@ -636,35 +671,38 @@
 
     vmem = lambda *s: pltpu.VMEM(s, F32)
     params = lambda: pltpu.CompilerParams(vmem_limit_bytes=24 * 2**20)
-
-    matrix = shift_matrix(cols)
-    fields = jnp.concatenate([currents, land_mask.astype(F32)[None]])
+    fast = lambda: pltpu.CompilerParams(vmem_limit_bytes=24 * 2**20)
+
     flat = action.reshape(combos, rows // SUB, SUB, cols // LANES, LANES)
     flat = flat.transpose(0, 1, 3, 2, 4).reshape(combos * rows * cols // LANES, LANES)
     vm = pl.BlockSpec(memory_space=pltpu.VMEM)
     hbm = pl.BlockSpec(memory_space=pl.ANY)
-    up_rows, dn_rows = pl.pallas_call(
+    up_rows, dn_rows, fields = pl.pallas_call(
         rows_kernel,
-        in_specs=[vm, vm],
-        out_specs=[vm, vm],
-        out_shape=[f32(HALO, combos + SUB, cols)] * 2,
-        compiler_params=params(),
+        in_specs=[hbm] * 3,
+        out_specs=[vm] * 3,
+        out_shape=[f32(HALO, combos + SUB, cols)] * 2 + [f32(3, rows, cols)],
+        scratch_shapes=[
+            vmem(flat.shape[0] + 32, LANES), pltpu.VMEM((rows, cols), jnp.int32), pltpu.SemaphoreType.DMA((7,))
+        ],
+        compiler_params=pltpu.CompilerParams(vmem_limit_bytes=60 * 2**20),
         name="boundary_rows",
-    )(flat, fields)
+    )(flat, currents, land_mask)
     up = [(i, i + 1) for i in range(points - 1)]
     down = [(j, i) for i, j in up]
     top = send(up_rows, "pts", up)
     bot = send(dn_rows, "pts", down)
 
-    in_prev, in_next = pl.pallas_call(
+    in_prev, in_next, matrix = pl.pallas_call(
         functools.partial(ends_kernel, total),
-        in_specs=[smem, smem, smem, vm, vm, vm],
-        out_specs=[vm, vm],
-        out_shape=[f32(freqs // 2, 24, cols)] * 2,
-        scratch_shapes=[vmem(rows, cols)] * 3 + [vmem(2, rows, cols)] + substep_scratch(4, cols),
-        compiler_params=params(),
+        in_specs=[smem, smem, smem, vm, vm],
+        out_specs=[vm, vm, vm],
+        out_shape=[f32(freqs // 2, 24, cols)] * 2
+        + [jax.ShapeDtypeStruct((2 * cols, 2 * cols), jnp.bfloat16)],
+        scratch_shapes=[vmem(rows, cols)] * 3 + [vmem(2, rows, cols)] + substep_scratch(4, cols, 3),
+        compiler_params=fast(),
         name="sector_ends",
-    )(sec, table, group_speed, action, fields, matrix)
+    )(sec, table, group_speed, action, fields)
     fwd = [(i, (i + 1) % sectors) for i in range(sectors)]
     back = [(j, i) for i, j in fwd]
     inner_from_prev = send(in_next, "dir", fwd)
@@ -687,9 +725,9 @@
             vmem(rows, cols), vmem(rows, cols), vmem(rows, cols), vmem(dirs + 1, rows, cols),
             vmem(2, SIDE, SUB, cols), vmem(2, dirs + 1, SUB, cols), vmem(3, combos, cols),
             vmem(dirs, rows, cols), vmem(rows, cols), vmem(2, SUB, cols), vmem(2, SUB, cols),
-            *substep_scratch(2 * dirs, cols),
+            *substep_scratch(2 * dirs, cols, 2),
         ],
-        compiler_params=params(),
+        compiler_params=fast(),
         name="transport",
     )(sec, table, group_speed, group_ratio, bin_weight, action, fields, matrix,
       top, bot, up_rows, dn_rows)

time: 61.2 us -> 57.5 us (0.940)
  local copies, waits for them, and re-layouts: 2.99 us -> 0.92 us
  other arithmetic: 2.13 us -> 0.63 us
    unnamed x16 -> x18, local copies, waits for them, and re-layouts: 2.99 us -> 0.92 us
    pallas_call x1, Pallas kernels: 1.96 us -> 3.34 us  [per_device(): pl.pallas_call(rows_kernel, in_specs=[hbm] * 3, out_specs=[vm] * 3, out_s...]
    pallas_call x1, Pallas kernels: 7.81 us -> 6.85 us  [per_device(): pl.pallas_call(functools.partial(ends_kernel, total), in_specs=[smem, sme...]
    concatenate x1 -> x0, other arithmetic: 0.76 us -> none  [per_device(): fields = jnp.concatenate([currents, land_mask.astype(F32)[None]])]
    broadcast_in_dim x1 -> x0, other arithmetic: 0.73 us -> none  [per_device(): fields = jnp.concatenate([currents, land_mask.astype(F32)[None]])]
where the time goes in v4:
time: 57.5 us; the launch traced here: 56.5 us
  Pallas kernels  24.5 us (43%)
  starting transfers between devices  20.9 us (36%)
  waiting for transfers between devices  8.76 us (15%)
  local copies, waits for them, and re-layouts  0.92 us (2%)
  between operations  0.81 us (1%)
  other arithmetic  0.63 us (1%)
    ppermute x10, starting transfers between devices, send(): return lax.ppermute(value, axis, pairs)  20.9 us
    pallas_call x1, Pallas kernels, per_device(): pl.pallas_call(functools.partial(main_kernel, total), in_specs=[smem] * 5...  13 us
    ppermute x10, waiting for transfers between devices, send(): return lax.ppermute(value, axis, pairs)  8.76 us
    pallas_call x1, Pallas kernels, per_device(): pl.pallas_call(functools.partial(ends_kernel, total), in_specs=[smem, sme...  6.85 us
    pallas_call x1, Pallas kernels, per_device(): pl.pallas_call(rows_kernel, in_specs=[hbm] * 3, out_specs=[vm] * 3, out_s...  3.34 us
    pallas_call x1, Pallas kernels, per_device(): pl.pallas_call(join_kernel, in_specs=[vm] * 6 + [hbm], out_specs=hbm, out...  1.28 us
  transfers between devices with their start and end apart: 10, of which 4 were waited for; matrix products, arithmetic and copies ran while one was open for 1% of the time, Pallas kernels for 35%

profile of v4, /device:TPU:6, one launch (start us, length us, event | category | flops | bytes accessed | tf_op | source)
XLA Modules:
  0.0 56.5 jit_solution(3822731013548413999)
XLA Ops:
  0.6 0.0 copy-start.5
  0.7 3.3 %boundary_rows.1 = (f32[3,208,256]{2,1,0:T(8,128)}, f32[3,208,256]{2,1,0:T(8,128)}, f32[3,16,256]{2,1,0:T(8,128)}) custom-call(f32[6400,128]{1,0:T(8,128)} %bitcast.6, f32[2,16,256]{2,1,0:T(8,128)} %cur_ref.1, s32[16,256]{1,0:T(8,128)} %land_ref.1), custom_call_target="tpu_custom_call" | custom-call | tf_op jit(solution)/shard_map/boundary_rows/pallas_call | solution.py:680
  4.0 1.9 %collective-permute-start = (f32[3,208,256]{2,1,0:T(8,128)}, f32[3,208,256]{2,1,0:T(8,128)}, u32[]{:S(2)}, u32[]{:S(2)}) collective-permute-start(f32[3,208,256]{2,1,0:T(8,128)} %get-tuple-element.16.ownup_ref), channel_id=1, source_target_pairs={{0,8},{8,16},{16,24},{24,32},{32,40},{40,48},{48,56},{56,64},{64,7... | collective-permute-start | bytes 1916936 | tf_op jit(solution)/shard_map/ppermute | solution.py:670
  6.0 8.0 %collective-permute-start.1 = (f32[3,208,256]{2,1,0:T(8,128)}, f32[3,208,256]{2,1,0:T(8,128)}, u32[]{:S(2)}, u32[]{:S(2)}) collective-permute-start(f32[3,208,256]{2,1,0:T(8,128)} %get-tuple-element.17.owndn_ref), channel_id=1, source_target_pairs={{8,0},{16,8},{24,16},{32,24},{40,32},{48,40},{56,48},{64,56},{72,6... | collective-permute-start | bytes 1916936 | tf_op jit(solution)/shard_map/ppermute | solution.py:670
  14.0 0.0 copy-start.1
  14.1 0.9 %copy-done.3 = f32[3,16,256]{2,1,0:T(8,128)S(1)} copy-done((f32[3,16,256]{2,1,0:T(8,128)S(1)}, f32[3,16,256]{2,1,0:T(8,128)}, u32[]{:S(2)}) %copy-start.3) | copy-done | bytes 49176
  15.0 6.9 %sector_ends.1 = (f32[25,24,256]{2,1,0:T(8,128)S(1)}, f32[25,24,256]{2,1,0:T(8,128)S(1)}, bf16[512,512]{1,0:T(8,128)(2,1)S(1)}) custom-call(s32[1]{0:T(128)} %bitcast.sec_ref, f32[8,22]{1,0:T(8,128)S(1)} %copy-done.5, f32[50]{0:T(128)S(1)} %copy-done.6, f32[50,4,16,256]{3,2,1,0:T(8,128)S(1)} %copy-done, f32[3,16,256]{2,1,0:T(8,128)S(1)} %copy-done.3), custom_call_target="tpu_custom_call" | custom-call | tf_op jit(solution)/shard_map/sector_ends/pallas_call | solution.py:696
  21.8 1.7 %collective-permute-start.2 = (f32[25,24,256]{2,1,0:T(8,128)S(1)}, f32[25,24,256]{2,1,0:T(8,128)S(1)}, u32[]{:S(2)}, u32[]{:S(2)}) collective-permute-start(f32[25,24,256]{2,1,0:T(8,128)S(1)} %get-tuple-element.20), channel_id=1, source_target_pairs={{0,1},{1,2},{2,3},{3,4},{4,5},{5,6},{6,7},{7,0},{8,9},{9,10},{10,1... | collective-permute-start | bytes 1843208 | tf_op jit(solution)/shard_map/ppermute | solution.py:670
  23.5 2.6 %collective-permute-start.3 = (f32[25,24,256]{2,1,0:T(8,128)S(1)}, f32[25,24,256]{2,1,0:T(8,128)S(1)}, u32[]{:S(2)}, u32[]{:S(2)}) collective-permute-start(f32[25,24,256]{2,1,0:T(8,128)S(1)} %get-tuple-element.21), channel_id=1, source_target_pairs={{1,0},{2,1},{3,2},{4,3},{5,4},{6,5},{7,6},{0,7},{9,8},{10,9},{11,1... | collective-permute-start | bytes 1843208 | tf_op jit(solution)/shard_map/ppermute | solution.py:670
  26.1 0.0 collective-permute-done.1.bot_ref
  26.1 13.0 %transport.1 = (f32[50,4,16,256]{3,2,1,0:T(8,128)}, f32[50,16,256]{2,1,0:T(8,128)S(1)}, f32[50,16,256]{2,1,0:T(8,128)S(1)}, f32[25,8,256]{2,1,0:T(8,128)S(1)}, f...) custom-call(s32[1]{0:T(128)} %bitcast.sec_ref, f32[8,22]{1,0:T(8,128)S(1)} %copy-done.5, f32[50]{0:T(128)S(1)} %copy-done.6, ...), custom_call_target="tpu_custom_call" | custom-call | tf_op jit(solution)/shard_map/transport/pallas_call | solution.py:711
  39.1 0.5 collective-permute-start.6
  39.6 3.5 %collective-permute-done.6 = f32[2,16,256]{2,1,0:T(8,128)S(1)} collective-permute-done((f32[2,16,256]{2,1,0:T(8,128)S(1)}, f32[2,16,256]{2,1,0:T(8,128)S(1)}, u32[]{:S(2)}, u32[]{:S(2)}) %collective-permute-start.6) | collective-permute-done | bytes 32800 | tf_op jit(solution)/shard_map/ppermute | solution.py:670
  43.1 0.9 %collective-permute-start.9 = (f32[2,16,256]{2,1,0:T(8,128)S(1)}, f32[2,16,256]{2,1,0:T(8,128)S(1)}, u32[]{:S(2)}, u32[]{:S(2)}) collective-permute-start(f32[2,16,256]{2,1,0:T(8,128)S(1)} %add.12), channel_id=1, source_target_pairs={{0,3},{1,0},{2,1},{3,2},{4,7},{5,4},{6,5},{7,6},{8,11},{9,8},{10,9... | collective-permute-start | bytes 98312 | tf_op jit(solution)/shard_map/ppermute | solution.py:670
  44.0 1.1 %collective-permute-start.8 = (f32[2,16,256]{2,1,0:T(8,128)S(1)}, f32[2,16,256]{2,1,0:T(8,128)S(1)}, u32[]{:S(2)}, u32[]{:S(2)}) collective-permute-start(f32[2,16,256]{2,1,0:T(8,128)S(1)} %add.12), channel_id=1, source_target_pairs={{0,1},{1,2},{2,3},{3,0},{4,5},{5,6},{6,7},{7,4},{8,9},{9,10},{10,1... | collective-permute-start | bytes 98312 | tf_op jit(solution)/shard_map/ppermute | solution.py:670
  45.1 1.1 %collective-permute-start.7 = (f32[2,16,256]{2,1,0:T(8,128)S(1)}, f32[2,16,256]{2,1,0:T(8,128)S(1)}, u32[]{:S(2)}, u32[]{:S(2)}) collective-permute-start(f32[2,16,256]{2,1,0:T(8,128)S(1)} %add.12), channel_id=1, source_target_pairs={{0,2},{1,3},{2,0},{3,1},{4,6},{5,7},{6,4},{7,5},{8,10},{9,11},{10,... | collective-permute-start | bytes 98312 | tf_op jit(solution)/shard_map/ppermute | solution.py:670
  46.2 1.1 %collective-permute-done.9 = f32[2,16,256]{2,1,0:T(8,128)S(1)} collective-permute-done((f32[2,16,256]{2,1,0:T(8,128)S(1)}, f32[2,16,256]{2,1,0:T(8,128)S(1)}, u32[]{:S(2)}, u32[]{:S(2)}) %collective-permute-start.9) | collective-permute-done | bytes 32800 | tf_op jit(solution)/shard_map/ppermute | solution.py:670
  47.4 0.7 %collective-permute-start.4 = (f32[25,8,256]{2,1,0:T(8,128)S(1)}, f32[25,8,256]{2,1,0:T(8,128)S(1)}, u32[]{:S(2)}, u32[]{:S(2)}) collective-permute-start(f32[25,8,256]{2,1,0:T(8,128)S(1)} %get-tuple-element.22), channel_id=1, source_target_pairs={{0,1},{1,2},{2,3},{3,4},{4,5},{5,6},{6,7},{7,0},{8,9},{9,10},{10,1... | collective-permute-start | bytes 614408 | tf_op jit(solution)/shard_map/ppermute | solution.py:670
  48.1 1.0 %collective-permute-done.8 = f32[2,16,256]{2,1,0:T(8,128)S(1)} collective-permute-done((f32[2,16,256]{2,1,0:T(8,128)S(1)}, f32[2,16,256]{2,1,0:T(8,128)S(1)}, u32[]{:S(2)}, u32[]{:S(2)}) %collective-permute-start.8) | collective-permute-done | bytes 32800 | tf_op jit(solution)/shard_map/ppermute | solution.py:670
  49.1 2.4 %collective-permute-start.5 = (f32[25,8,256]{2,1,0:T(8,128)S(1)}, f32[25,8,256]{2,1,0:T(8,128)S(1)}, u32[]{:S(2)}, u32[]{:S(2)}) collective-permute-start(f32[25,8,256]{2,1,0:T(8,128)S(1)} %get-tuple-element.23), channel_id=1, source_target_pairs={{1,0},{2,1},{3,2},{4,3},{5,4},{6,5},{7,6},{0,7},{9,8},{10,9},{11,1... | collective-permute-start | bytes 614408 | tf_op jit(solution)/shard_map/ppermute | solution.py:670
  51.5 0.0 collective-permute-done.7
  51.5 0.6 %add_add_fusion = f32[2,16,256]{2,1,0:T(8,128)} fusion(f32[2,16,256]{2,1,0:T(8,128)S(1)} %collective-permute-done.8, f32[2,16,256]{2,1,0:T(8,128)S(1)} %collective-permute-done.9, f32[2,16,256]{2,1,0:T(8,128)S(1)} %add.12, f32[2,16,256]{2,1,0:T(8,128)S(1)} %collective-permute-done.7), kind=kLoop, calls=%fused_computation | loop fusion | flops 24576 | bytes 163840 | tf_op jit(solution)/shard_map/add | solution.py:744
  52.1 3.1 %collective-permute-done.4.outp_ref = f32[25,8,256]{2,1,0:T(8,128)S(1)} collective-permute-done((f32[25,8,256]{2,1,0:T(8,128)S(1)}, f32[25,8,256]{2,1,0:T(8,128)S(1)}, u32[]{:S(2)}, u32[]{:S(2)}) %collective-permute-start.4) | collective-permute-done | bytes 204832 | tf_op jit(solution)/shard_map/ppermute | solution.py:670
  55.2 1.3 %join_sectors.1 = f32[50,4,16,256]{3,2,1,0:T(8,128)} custom-call(f32[50,16,256]{2,1,0:T(8,128)S(1)} %get-tuple-element.18.e0_ref, f32[50,16,256]{2,1,0:T(8,128)S(1)} %get-tuple-element.19.e3_ref, f32[25,24,256]{2,1,0:T(8,128)S(1)} %collective-permute-done.2.inp_ref, ...), custom_call_target="tpu_custom_call", output_to_operand_aliasing={{}: (6, {})} | custom-call | tf_op jit(solution)/shard_map/join_sectors/pallas_call | solution.py:746
  (20 shorter events, 0.0 us)
Async XLA Ops:
  0.6 13.4 %copy-start.5 = (f32[8,22]{1,0:T(8,128)S(1)}, f32[8,22]{1,0:T(8,128)}, u32[]{:S(2)}) copy-start(f32[8,22]{1,0:T(8,128)} %constant.6.clone.tab_ref) | copy-start | bytes 2116
  0.6 13.4 %copy-start = (f32[50,4,16,256]{3,2,1,0:T(8,128)S(1)}, f32[50,4,16,256]{3,2,1,0:T(8,128)}, u32[]{:S(2)}) copy-start(f32[50,4,16,256]{3,2,1,0:T(8,128)} %x_ref.3) | copy-start | bytes 9830404
  0.7 13.4 %copy-start.6 = (f32[50]{0:T(128)S(1)}, f32[50]{0:T(128)}, u32[]{:S(2)}) copy-start(f32[50]{0:T(128)} %cg_ref.3) | copy-start | bytes 604
  0.7 25.4 %copy-start.7 = (f32[50]{0:T(128)S(1)}, f32[50]{0:T(128)}, u32[]{:S(2)}) copy-start(f32[50]{0:T(128)} %ratio_ref.1) | copy-start | bytes 604
  0.7 25.4 %copy-start.8 = (f32[50]{0:T(128)S(1)}, f32[50]{0:T(128)}, u32[]{:S(2)}) copy-start(f32[50]{0:T(128)} %weight_ref.1) | copy-start | bytes 604
  4.0 22.0 %collective-permute-start = (f32[3,208,256]{2,1,0:T(8,128)}, f32[3,208,256]{2,1,0:T(8,128)}, u32[]{:S(2)}, u32[]{:S(2)}) collective-permute-start(f32[3,208,256]{2,1,0:T(8,128)} %get-tuple-element.16.ownup_ref), channel_id=1, source_target_pairs={{0,8},{8,16},{16,24},{24,32},{32,40},{40,48},{48,56},{56,64},{64,7... | collective-permute-start | bytes 1916936 | tf_op jit(solution)/shard_map/ppermute | solution.py:670
  6.0 20.1 %collective-permute-start.1 = (f32[3,208,256]{2,1,0:T(8,128)}, f32[3,208,256]{2,1,0:T(8,128)}, u32[]{:S(2)}, u32[]{:S(2)}) collective-permute-start(f32[3,208,256]{2,1,0:T(8,128)} %get-tuple-element.17.owndn_ref), channel_id=1, source_target_pairs={{8,0},{16,8},{24,16},{32,24},{40,32},{48,40},{56,48},{64,56},{72,6... | collective-permute-start | bytes 1916936 | tf_op jit(solution)/shard_map/ppermute | solution.py:670
  14.0 12.0 %copy-start.1 = (f32[3,208,256]{2,1,0:T(8,128)S(1)}, f32[3,208,256]{2,1,0:T(8,128)}, u32[]{:S(2)}) copy-start(f32[3,208,256]{2,1,0:T(8,128)} %get-tuple-element.16.ownup_ref) | copy-start | bytes 1916932
  14.0 12.0 %copy-start.2 = (f32[3,208,256]{2,1,0:T(8,128)S(1)}, f32[3,208,256]{2,1,0:T(8,128)}, u32[]{:S(2)}) copy-start(f32[3,208,256]{2,1,0:T(8,128)} %get-tuple-element.17.owndn_ref) | copy-start | bytes 1916932
  14.1 0.9 %copy-start.3 = (f32[3,16,256]{2,1,0:T(8,128)S(1)}, f32[3,16,256]{2,1,0:T(8,128)}, u32[]{:S(2)}) copy-start(f32[3,16,256]{2,1,0:T(8,128)} %get-tuple-element.14.cur_ref) | copy-start | bytes 147460
  15.0 11.1 %copy-start.4 = (f32[3,16,256]{2,1,0:T(8,128)S(1)}, f32[3,16,256]{2,1,0:T(8,128)}, u32[]{:S(2)}) copy-start(f32[3,16,256]{2,1,0:T(8,128)} %get-tuple-element.14.cur_ref) | copy-start | bytes 147460
  21.8 30.3 %collective-permute-start.2 = (f32[25,24,256]{2,1,0:T(8,128)S(1)}, f32[25,24,256]{2,1,0:T(8,128)S(1)}, u32[]{:S(2)}, u32[]{:S(2)}) collective-permute-start(f32[25,24,256]{2,1,0:T(8,128)S(1)} %get-tuple-element.20), channel_id=1, source_target_pairs={{0,1},{1,2},{2,3},{3,4},{4,5},{5,6},{6,7},{7,0},{8,9},{9,10},{10,1... | collective-permute-start | bytes 1843208 | tf_op jit(solution)/shard_map/ppermute | solution.py:670
  23.5 28.6 %collective-permute-start.3 = (f32[25,24,256]{2,1,0:T(8,128)S(1)}, f32[25,24,256]{2,1,0:T(8,128)S(1)}, u32[]{:S(2)}, u32[]{:S(2)}) collective-permute-start(f32[25,24,256]{2,1,0:T(8,128)S(1)} %get-tuple-element.21), channel_id=1, source_target_pairs={{1,0},{2,1},{3,2},{4,3},{5,4},{6,5},{7,6},{0,7},{9,8},{10,9},{11,1... | collective-permute-start | bytes 1843208 | tf_op jit(solution)/shard_map/ppermute | solution.py:670
  39.1 4.0 %collective-permute-start.6 = (f32[2,16,256]{2,1,0:T(8,128)S(1)}, f32[2,16,256]{2,1,0:T(8,128)S(1)}, u32[]{:S(2)}, u32[]{:S(2)}) collective-permute-start(f32[2,16,256]{2,1,0:T(8,128)S(1)} %get-tuple-element.25), channel_id=1, source_target_pairs={{0,4},{1,5},{2,6},{3,7},{4,0},{5,1},{6,2},{7,3},{8,12},{9,13},{10,... | collective-permute-start | bytes 98312 | tf_op jit(solution)/shard_map/ppermute | solution.py:670
  43.1 4.3 %collective-permute-start.9 = (f32[2,16,256]{2,1,0:T(8,128)S(1)}, f32[2,16,256]{2,1,0:T(8,128)S(1)}, u32[]{:S(2)}, u32[]{:S(2)}) collective-permute-start(f32[2,16,256]{2,1,0:T(8,128)S(1)} %add.12), channel_id=1, source_target_pairs={{0,3},{1,0},{2,1},{3,2},{4,7},{5,4},{6,5},{7,6},{8,11},{9,8},{10,9... | collective-permute-start | bytes 98312 | tf_op jit(solution)/shard_map/ppermute | solution.py:670
  44.0 5.1 %collective-permute-start.8 = (f32[2,16,256]{2,1,0:T(8,128)S(1)}, f32[2,16,256]{2,1,0:T(8,128)S(1)}, u32[]{:S(2)}, u32[]{:S(2)}) collective-permute-start(f32[2,16,256]{2,1,0:T(8,128)S(1)} %add.12), channel_id=1, source_target_pairs={{0,1},{1,2},{2,3},{3,0},{4,5},{5,6},{6,7},{7,4},{8,9},{9,10},{10,1... | collective-permute-start | bytes 98312 | tf_op jit(solution)/shard_map/ppermute | solution.py:670
  45.1 6.4 %collective-permute-start.7 = (f32[2,16,256]{2,1,0:T(8,128)S(1)}, f32[2,16,256]{2,1,0:T(8,128)S(1)}, u32[]{:S(2)}, u32[]{:S(2)}) collective-permute-start(f32[2,16,256]{2,1,0:T(8,128)S(1)} %add.12), channel_id=1, source_target_pairs={{0,2},{1,3},{2,0},{3,1},{4,6},{5,7},{6,4},{7,5},{8,10},{9,11},{10,... | collective-permute-start | bytes 98312 | tf_op jit(solution)/shard_map/ppermute | solution.py:670
  47.4 7.9 %collective-permute-start.4 = (f32[25,8,256]{2,1,0:T(8,128)S(1)}, f32[25,8,256]{2,1,0:T(8,128)S(1)}, u32[]{:S(2)}, u32[]{:S(2)}) collective-permute-start(f32[25,8,256]{2,1,0:T(8,128)S(1)} %get-tuple-element.22), channel_id=1, source_target_pairs={{0,1},{1,2},{2,3},{3,4},{4,5},{5,6},{6,7},{7,0},{8,9},{9,10},{10,1... | collective-permute-start | bytes 614408 | tf_op jit(solution)/shard_map/ppermute | solution.py:670
  49.1 6.1 %collective-permute-start.5 = (f32[25,8,256]{2,1,0:T(8,128)S(1)}, f32[25,8,256]{2,1,0:T(8,128)S(1)}, u32[]{:S(2)}, u32[]{:S(2)}) collective-permute-start(f32[25,8,256]{2,1,0:T(8,128)S(1)} %get-tuple-element.23), channel_id=1, source_target_pairs={{1,0},{2,1},{3,2},{4,3},{5,4},{6,5},{7,6},{0,7},{9,8},{10,9},{11,1... | collective-permute-start | bytes 614408 | tf_op jit(solution)/shard_map/ppermute | solution.py:670
